TPU v7x, 256 devices: a whole 4x4x8 slice. The times are simulated.
256 devices in a mesh: row: 2 (over core), sector: 32 (over z, y), slab: 4 (over x).
Axes of the slice: x: 4, y: 4, z: 8, core: 2. Of those that a mesh axis runs over, the one named last changes fastest.
Arguments:
- state: float32 [2, 5, 32, 1024, 128], P('row', None, 'slab', 'sector'), may hold values from -6 to 6
- source: float32 [2, 5, 32, 1024, 128], P('row', None, 'slab', 'sector'), may hold values from -6 to 6
- diag_inverse: float32 [2, 5, 5, 32, 1024, 128], P('row', None, None, 'slab', 'sector'), may hold values from -1 to 1
- jac_axial: float32 [2, 5, 5], P('row'), may hold values from -1 to 2
- jac_cross: float32 [2, 2, 5, 5], P('row'), may hold values from -2.5 to 2.5
- owner: int32 [1024], replicated, may hold values from 0 to 1023, as said below
Outputs:
- residual: float32 [2, 5, 32, 1024, 128], P('row', None, 'slab', 'sector')
- new_state: float32 [2, 5, 32, 1024, 128], P('row', None, 'slab', 'sector')
Inputs may be any that keep to these rules, and one draw needn't show every extreme that they name: owner is a permutation; for some whole s, the columns b * 32 to b * 32 + 31 of the rotor face exactly the stator columns s + b * 32 to s + b * 32 + 31, taken modulo 1024, for every b.
All inputs are finite; a program needn't handle non-finite values.
Results may differ from a plain program's by a relative error of at most 0.0001.
Values sent between devices are 32-bit elements; how exact they have to be, the bound alone decides.
No kernel may reach another device: no remote copies, remote signals or barrier semaphores. Data moves between devices by JAX's collectives and lax.ppermute only.
A program may use at most 64 MiB of HBM per device.

v0:
```python
import jax
import jax.numpy as jnp
from jax import lax
from jax.sharding import PartitionSpec as P

exact_mode = lax.Precision.HIGHEST


def padded(shard, sides, width):
    edges = {}
    for axis, dim in sides:
        peers, length = (lax.axis_size(axis), shard.shape[dim])
        up = [(i, (i + 1) % peers) for i in range(peers - 1)]
        last = lax.slice_in_dim(shard, length - width, length, axis=dim)
        leading = lax.slice_in_dim(shard, 0, width, axis=dim)
        edges[dim] = (
            lax.ppermute(last, axis, up),
            lax.ppermute(leading, axis, [(b, a) for a, b in up]),
        )
    done = []
    for _, dim in sides:
        low, high = edges[dim]
        around = [(width, width) if d in done else (0, 0) for d in range(shard.ndim)]
        shard = jnp.concatenate([jnp.pad(low, around), shard, jnp.pad(high, around)], axis=dim)
        done.append(dim)
    return shard


def passed_along(shard, axis, by):
    peers = lax.axis_size(axis)
    return lax.ppermute(shard, axis, [(i, (i + by) % peers) for i in range(peers)])


def extended(block, sides, width):
    for axis, dim in sides:
        count = lax.axis_size(axis)
        forward = [(i, i + 1) for i in range(count - 1)]
        forward.append((count - 1, 0))
        backward = [(target, source) for source, target in forward]
        low = lax.ppermute(
            lax.slice_in_dim(block, block.shape[dim] - width, None, axis=dim), axis, forward
        )
        high = lax.ppermute(lax.slice_in_dim(block, 0, width, axis=dim), axis, backward)
        block = jnp.concatenate([low, block, high], axis=dim)
    return block


def shifted(block, axis, distance):
    devices = range(lax.axis_size(axis))
    route = [(i - distance, i) for i in devices if i - distance in devices]
    return lax.ppermute(block, axis, route)


def mix_const(matrix, field):
    return jnp.einsum("ij,j...->i...", matrix, field, precision=exact_mode)


def per_cell(blocks, field):
    return jnp.sum(blocks * field[None], axis=1)


def forward_sweep(residual, inverse, axial, entering):
    previous = entering
    plane_list = []
    for plane_at in range(residual.shape[1]):
        present_plane = per_cell(
            inverse[:, :, plane_at], residual[:, plane_at] + 0.5 * mix_const(axial, previous)
        )
        plane_list.append(present_plane)
        previous = present_plane
    return jnp.stack(plane_list, axis=1)


def backward_sweep(provisional, inverse, axial, entering):
    planes = provisional.shape[1]
    following = entering
    plane_list = []
    for step_at in range(planes):
        plane_at = planes - 1 - step_at
        present_plane = provisional[:, plane_at] - per_cell(
            inverse[:, :, plane_at], 0.5 * mix_const(axial, following)
        )
        plane_list.append(present_plane)
        following = present_plane
    return jnp.stack(plane_list[::-1], axis=1)


def per_device(state, source, diag_inverse, jac_axial, jac_cross, owner):
    field = state[0]
    inverse = diag_inverse[0]
    axial = jac_axial[0]
    circular = jac_cross[0, 0]
    radial_jac = jac_cross[0, 1]
    planes = field.shape[1]
    columns = field.shape[2]
    radial_cells = field.shape[3]
    total_columns = owner.shape[0]
    blade_row_index = lax.axis_index("row")
    slab_index = lax.axis_index("slab")
    sector_index = lax.axis_index("sector")
    sectors = lax.axis_size("sector")
    slabs = lax.axis_size("slab")
    axial_padded = padded(field, ((("row", "slab"), 1),), 1)
    below = axial_padded[:, 0]
    above = axial_padded[:, planes + 1]
    partner = jnp.where(blade_row_index == 0, above, below)
    doubled = jnp.concatenate([owner, owner])
    local_ids = sector_index * columns + jnp.arange(columns, dtype=jnp.int32)
    owner_local = lax.dynamic_slice_in_dim(doubled, sector_index * columns, columns)
    leading = owner[:columns]
    present = jnp.any(leading[None, :] == (leading[:, None] - 1) % total_columns, axis=1)
    start_column = jnp.sum(jnp.where(present, 0, leading))
    offset_sectors = start_column // columns
    turn = jnp.where(blade_row_index == 0, (sectors - offset_sectors) % sectors, offset_sectors)
    turned = partner
    for bit_at in range((sectors - 1).bit_length()):
        moved = passed_along(turned, "sector", 1 << bit_at)
        turned = jnp.where(turn // (1 << bit_at) % 2 == 1, moved, turned)
    sides = extended(turned[:, None], (("sector", 1),), 1)
    candidates = sides.reshape(5, 3 * columns, radial_cells)
    centre = (sector_index - turn) % sectors
    block_starts = (centre + jnp.arange(-1, 2, dtype=jnp.int32)) % sectors * columns
    candidate_ids = (block_starts[:, None] + jnp.arange(columns, dtype=jnp.int32)[None, :]).reshape(
        3 * columns
    )
    candidate_owner = jnp.concatenate(
        [lax.dynamic_slice_in_dim(doubled, block_starts[which], columns) for which in range(3)]
    )
    rotor_hits = owner_local[:, None] == candidate_ids[None, :]
    stator_hits = candidate_owner[None, :] == local_ids[:, None]
    section_chooser = jnp.where(blade_row_index == 0, rotor_hits, stator_hits).astype(jnp.float32)
    ghost = jnp.einsum("jk,vkr->vjr", section_chooser, candidates, precision=exact_mode)
    rotor_top = (blade_row_index == 0) & (slab_index == slabs - 1)
    stator_foot = (blade_row_index == 1) & (slab_index == 0)
    upper = jnp.where(rotor_top, ghost, above)
    lower = jnp.where(stator_foot, ghost, below)
    axial_diff = jnp.concatenate([field[:, 1:], upper[:, None]], axis=1) - jnp.concatenate(
        [lower[:, None], field[:, :-1]], axis=1
    )
    cycle = extended(field, (("sector", 2),), 1)
    cycle_diff = cycle[:, :, 2:] - cycle[:, :, :-2]
    radial = jnp.pad(field, ((0, 0), (0, 0), (0, 0), (1, 1)))
    radial_diff = radial[..., 2:] - radial[..., :-2]
    residual = source[0] - 0.5 * (
        mix_const(axial, axial_diff)
        + mix_const(circular, cycle_diff)
        + mix_const(radial_jac, radial_diff)
    )
    zeros_plane = jnp.zeros((5, columns, radial_cells), jnp.float32)
    entering = zeros_plane
    for section_lookup in range(slabs - 1):
        provisional = forward_sweep(residual, inverse, axial, entering)
        entering = shifted(provisional[:, -1], "slab", 1)
    provisional = forward_sweep(residual, inverse, axial, entering)
    entering = zeros_plane
    for section_lookup in range(slabs - 1):
        update = backward_sweep(provisional, inverse, axial, entering)
        entering = shifted(update[:, 0], "slab", -1)
    update = backward_sweep(provisional, inverse, axial, entering)
    return (residual[None], (field + update)[None])


def solution(mesh):
    return jax.shard_map(
        per_device,
        mesh=mesh,
        in_specs=(
            P("row", None, "slab", "sector", None),
            P("row", None, "slab", "sector", None),
            P("row", None, None, "slab", "sector", None),
            P("row", None, None),
            P("row", None, None, None),
            P(),
        ),
        out_specs=(P("row", None, "slab", "sector", None), P("row", None, "slab", "sector", None)),
        check_vma=False,
    )
```

profile of v0, /device:TPU:0, one launch (start us, length us, event | category | flops | bytes accessed | tf_op | source)
XLA Modules:
  0.0 142.8 jit_solution(17880110814073175584)
XLA Ops:
  0.7 1.1 copy.775
  1.8 1.3 collective-permute-start
  3.1 4.6 %collective-permute-start.1 = (f32[5,1,32,128]{3,2,0,1:T(8,128)S(1)}, f32[5,1,32,128]{3,2,0,1:T(8,128)S(1)}, u32[]{:S(2)}, u32[]{:S(2)}) collective-permute-start(f32[5,1,32,128]{3,2,0,1:T(8,128)S(1)} %get-tuple-element.21), channel_id=1, source_target_pairs={{0,1},{1,2},{2,3},{3,128},{128,129},{129,130},{130,131},{4,5},{5,6... | collective-permute-start | bytes 245768 | tf_op jit(solution)/shard_map/ppermute | solution.py:17
  7.8 6.6 %collective-permute-start.9 = (f32[5,8,1,128]{3,2,0,1:T(1,128)S(1)}, f32[5,8,1,128]{3,2,0,1:T(1,128)S(1)}, u32[]{:S(2)}, u32[]{:S(2)}) collective-permute-start(f32[5,8,1,128]{3,2,0,1:T(1,128)S(1)} %get-tuple-element.16), channel_id=1, source_target_pairs={{4,0},{8,4},{12,8},{16,12},{20,16},{24,20},{28,24},{32,28},{36,32}... | collective-permute-start | bytes 61448 | tf_op jit(solution)/shard_map/ppermute | solution.py:43
  14.5 0.7 and_select_fusion.1
  15.3 1.3 select_reduce_fusion
  19.6 0.7 fusion.184
  26.6 8.2 %collective-permute-done.2 = f32[5,32,128]{2,1,0:T(8,128)S(1)} collective-permute-done((f32[5,32,128]{2,1,0:T(8,128)S(1)}, f32[5,32,128]{2,1,0:T(8,128)S(1)}, u32[]{:S(2)}, u32[]{:S(2)}) %collective-permute-start.2) | collective-permute-done | bytes 81952 | tf_op jit(solution)/shard_map/ppermute | solution.py:31
  34.9 8.0 %collective-permute-done.3 = f32[5,32,128]{2,1,0:T(8,128)S(1)} collective-permute-done((f32[5,32,128]{2,1,0:T(8,128)S(1)}, f32[5,32,128]{2,1,0:T(8,128)S(1)}, u32[]{:S(2)}, u32[]{:S(2)}) %collective-permute-start.3) | collective-permute-done | bytes 81952 | tf_op jit(solution)/shard_map/ppermute | solution.py:31
  43.2 5.7 %collective-permute-done.4 = f32[5,32,128]{2,1,0:T(8,128)S(1)} collective-permute-done((f32[5,32,128]{2,1,0:T(8,128)S(1)}, f32[5,32,128]{2,1,0:T(8,128)S(1)}, u32[]{:S(2)}, u32[]{:S(2)}) %collective-permute-start.4) | collective-permute-done | bytes 81952 | tf_op jit(solution)/shard_map/ppermute | solution.py:31
  48.9 6.5 %collective-permute-done.5 = f32[5,32,128]{2,1,0:T(8,128)S(1)} collective-permute-done((f32[5,32,128]{2,1,0:T(8,128)S(1)}, f32[5,32,128]{2,1,0:T(8,128)S(1)}, u32[]{:S(2)}, u32[]{:S(2)}) %collective-permute-start.5) | collective-permute-done | bytes 81952 | tf_op jit(solution)/shard_map/ppermute | solution.py:31
  55.5 5.0 %collective-permute-start.6 = (f32[5,32,128]{2,1,0:T(8,128)S(1)}, f32[5,32,128]{2,1,0:T(8,128)S(1)}, u32[]{:S(2)}, u32[]{:S(2)}) collective-permute-start(f32[5,32,128]{2,1,0:T(8,128)S(1)} %broadcast_select_fusion.3), channel_id=1, source_target_pairs={{0,64},{4,68},{8,72},{12,76},{16,80},{20,84},{24,88},{28,92},{32,9... | collective-permute-start | bytes 245768 | tf_op jit(solution)/shard_map/ppermute | solution.py:31
  60.5 3.4 %collective-permute-done.6 = f32[5,32,128]{2,1,0:T(8,128)S(1)} collective-permute-done((f32[5,32,128]{2,1,0:T(8,128)S(1)}, f32[5,32,128]{2,1,0:T(8,128)S(1)}, u32[]{:S(2)}, u32[]{:S(2)}) %collective-permute-start.6) | collective-permute-done | bytes 81952 | tf_op jit(solution)/shard_map/ppermute | solution.py:31
  64.0 5.3 %collective-permute-start.8 = (f32[5,1,32,128]{3,2,0,1:T(8,128)S(1)}, f32[5,1,32,128]{3,2,0,1:T(8,128)S(1)}, u32[]{:S(2)}, u32[]{:S(2)}) collective-permute-start(f32[5,1,32,128]{3,2,0,1:T(8,128)S(1)} %select_bitcast_fusion), channel_id=1, source_target_pairs={{4,0},{8,4},{12,8},{16,12},{20,16},{24,20},{28,24},{32,28},{36,32}... | collective-permute-start | bytes 245768 | tf_op jit(solution)/shard_map/ppermute | solution.py:43
  69.3 0.5 fusion.101
  69.8 1.9 %collective-permute-done.7 = f32[5,1,32,128]{3,2,0,1:T(8,128)S(1)} collective-permute-done((f32[5,1,32,128]{3,2,0,1:T(8,128)S(1)}, f32[5,1,32,128]{3,2,0,1:T(8,128)S(1)}, u32[]{:S(2)}, u32[]{:S(2)}) %collective-permute-start.7) | collective-permute-done | bytes 81952 | tf_op jit(solution)/shard_map/ppermute | solution.py:40
  72.2 1.4 fusion.99
  73.6 1.4 convolution_add_fusion.1
  74.9 1.7 %fusion.2 = f32[5,8,32,128]{3,0,2,1:T(8,128)S(1)} fusion(f32[8,32,128,5]{2,3,1,0:T(8,128)S(1)} %convolution_add_fusion.1, f32[5,8,32,128]{3,2,0,1:T(8,128)S(1)} %get-tuple-element.14, f32[1,5,8,32,128]{4,3,2,1,0:T(8,128)S(1)} %copy-done.3, f32[1,1,5,5]{3,1,2,0:T(1,128)S(1)} %get-tuple-element.28), kind=kOutput, calls=%fused_computation.5 | convolution fusion | flops 10321920 | bytes 2621540 | tf_op jit(solution)/shard_map/ij,j...->i.../dot_general | solution.py:55
  77.0 0.3 fusion.66
  77.4 0.3 fusion.67
  78.1 0.3 fusion.69
  78.5 0.3 fusion.70
  79.2 0.3 fusion.72
  79.6 3.7 %collective-permute-start.11 = (f32[5,32,128]{2,0,1:T(8,128)S(1)}, f32[5,32,128]{2,0,1:T(8,128)S(1)}, u32[]{:S(2)}, u32[]{:S(2)}) collective-permute-start(f32[5,32,128]{2,0,1:T(8,128)S(1)} %copy.455), channel_id=1, source_target_pairs={{0,1},{1,2},{2,3},{4,5},{5,6},{6,7},{8,9},{9,10},{10,11},{12,13},{... | collective-permute-start | bytes 245768 | tf_op jit(solution)/shard_map/ppermute | solution.py:51
  83.4 3.6 %collective-permute-done.11 = f32[5,32,128]{2,0,1:T(8,128)S(1)} collective-permute-done((f32[5,32,128]{2,0,1:T(8,128)S(1)}, f32[5,32,128]{2,0,1:T(8,128)S(1)}, u32[]{:S(2)}, u32[]{:S(2)}) %collective-permute-start.11) | collective-permute-done | bytes 81952 | tf_op jit(solution)/shard_map/ppermute | solution.py:51
  87.3 0.3 fusion.74
  87.7 0.3 fusion.75
  88.1 0.3 fusion.76
  88.8 0.3 fusion.78
  90.0 4.6 %collective-permute-start.12 = (f32[5,32,128]{2,0,1:T(8,128)S(1)}, f32[5,32,128]{2,0,1:T(8,128)S(1)}, u32[]{:S(2)}, u32[]{:S(2)}) collective-permute-start(f32[5,32,128]{2,0,1:T(8,128)S(1)} %copy.471), channel_id=1, source_target_pairs={{0,1},{1,2},{2,3},{4,5},{5,6},{6,7},{8,9},{9,10},{10,11},{12,13},{... | collective-permute-start | bytes 245768 | tf_op jit(solution)/shard_map/ppermute | solution.py:51
  94.6 2.7 %collective-permute-done.12 = f32[5,32,128]{2,0,1:T(8,128)S(1)} collective-permute-done((f32[5,32,128]{2,0,1:T(8,128)S(1)}, f32[5,32,128]{2,0,1:T(8,128)S(1)}, u32[]{:S(2)}, u32[]{:S(2)}) %collective-permute-start.12) | collective-permute-done | bytes 81952 | tf_op jit(solution)/shard_map/ppermute | solution.py:51
  100.3 4.4 %collective-permute-start.13 = (f32[5,32,128]{2,0,1:T(8,128)S(1)}, f32[5,32,128]{2,0,1:T(8,128)S(1)}, u32[]{:S(2)}, u32[]{:S(2)}) collective-permute-start(f32[5,32,128]{2,0,1:T(8,128)S(1)} %copy.487), channel_id=1, source_target_pairs={{0,1},{1,2},{2,3},{4,5},{5,6},{6,7},{8,9},{9,10},{10,11},{12,13},{... | collective-permute-start | bytes 245768 | tf_op jit(solution)/shard_map/ppermute | solution.py:51
  104.7 2.5 %collective-permute-done.13 = f32[5,32,128]{2,0,1:T(8,128)S(1)} collective-permute-done((f32[5,32,128]{2,0,1:T(8,128)S(1)}, f32[5,32,128]{2,0,1:T(8,128)S(1)}, u32[]{:S(2)}, u32[]{:S(2)}) %collective-permute-start.13) | collective-permute-done | bytes 81952 | tf_op jit(solution)/shard_map/ppermute | solution.py:51
  109.8 0.3 fusion.96
  112.1 0.3 fusion.28
  112.9 1.3 collective-permute-start.14
  114.2 5.5 %collective-permute-done.14 = f32[5,32,128]{2,1,0:T(8,128)S(1)} collective-permute-done((f32[5,32,128]{2,1,0:T(8,128)S(1)}, f32[5,32,128]{2,1,0:T(8,128)S(1)}, u32[]{:S(2)}, u32[]{:S(2)}) %collective-permute-start.14) | collective-permute-done | bytes 81952 | tf_op jit(solution)/shard_map/ppermute | solution.py:51
  121.2 0.3 fusion.22
  122.8 1.3 collective-permute-start.15
  124.1 5.0 %collective-permute-done.15 = f32[5,32,128]{2,1,0:T(8,128)S(1)} collective-permute-done((f32[5,32,128]{2,1,0:T(8,128)S(1)}, f32[5,32,128]{2,1,0:T(8,128)S(1)}, u32[]{:S(2)}, u32[]{:S(2)}) %collective-permute-start.15) | collective-permute-done | bytes 81952 | tf_op jit(solution)/shard_map/ppermute | solution.py:51
  131.1 0.3 fusion.13
  132.2 1.6 %collective-permute-start.16 = (f32[5,32,128]{2,1,0:T(8,128)S(1)}, f32[5,32,128]{2,1,0:T(8,128)S(1)}, u32[]{:S(2)}, u32[]{:S(2)}) collective-permute-start(f32[5,32,128]{2,1,0:T(8,128)S(1)} %sub.258), channel_id=1, source_target_pairs={{1,0},{2,1},{3,2},{5,4},{6,5},{7,6},{9,8},{10,9},{11,10},{13,12},{... | collective-permute-start | bytes 245768 | tf_op jit(solution)/shard_map/ppermute | solution.py:51
  133.8 1.0 copy.567
  134.7 3.8 %collective-permute-done.16 = f32[5,32,128]{2,1,0:T(8,128)S(1)} collective-permute-done((f32[5,32,128]{2,1,0:T(8,128)S(1)}, f32[5,32,128]{2,1,0:T(8,128)S(1)}, u32[]{:S(2)}, u32[]{:S(2)}) %collective-permute-start.16) | collective-permute-done | bytes 81952 | tf_op jit(solution)/shard_map/ppermute | solution.py:51
  139.3 0.3 fusion.8
  140.9 0.3 fusion.4
  141.9 0.9 copy.568
  (264 shorter events, 20.0 us)
Async XLA Ops:
  0.6 25.9 %copy-start.4 = (s32[1024]{0:T(1024)S(1)}, s32[1024]{0:T(1024)}, u32[]{:S(2)}) copy-start(s32[1024]{0:T(1024)} %param.11) | copy-start | bytes 12292
  0.6 18.9 %copy-start.5 = (f32[1,2,5,5]{3,1,2,0:T(2,128)S(1)}, f32[1,2,5,5]{3,1,2,0:T(2,128)}, u32[]{:S(2)}) copy-start(f32[1,2,5,5]{3,1,2,0:T(2,128)} %param.10) | copy-start | bytes 604
  1.8 24.6 %collective-permute-start = (f32[5,1,32,128]{3,2,0,1:T(8,128)S(1)}, f32[5,1,32,128]{3,2,0,1:T(8,128)S(1)}, u32[]{:S(2)}, u32[]{:S(2)}) collective-permute-start(f32[5,1,32,128]{3,2,0,1:T(8,128)S(1)} %get-tuple-element.20), channel_id=1, source_target_pairs={{1,0},{2,1},{3,2},{128,3},{129,128},{130,129},{131,130},{5,4},{6,5... | collective-permute-start | bytes 245768 | tf_op jit(solution)/shard_map/ppermute | solution.py:18
  3.1 23.3 %collective-permute-start.1 = (f32[5,1,32,128]{3,2,0,1:T(8,128)S(1)}, f32[5,1,32,128]{3,2,0,1:T(8,128)S(1)}, u32[]{:S(2)}, u32[]{:S(2)}) collective-permute-start(f32[5,1,32,128]{3,2,0,1:T(8,128)S(1)} %get-tuple-element.21), channel_id=1, source_target_pairs={{0,1},{1,2},{2,3},{3,128},{128,129},{129,130},{130,131},{4,5},{5,6... | collective-permute-start | bytes 245768 | tf_op jit(solution)/shard_map/ppermute | solution.py:17
  7.7 61.6 %collective-permute-start.10 = (f32[5,8,1,128]{3,2,0,1:T(1,128)S(1)}, f32[5,8,1,128]{3,2,0,1:T(1,128)S(1)}, u32[]{:S(2)}, u32[]{:S(2)}) collective-permute-start(f32[5,8,1,128]{3,2,0,1:T(1,128)S(1)} %get-tuple-element.17), channel_id=1, source_target_pairs={{0,4},{4,8},{8,12},{12,16},{16,20},{20,24},{24,28},{28,32},{32,36}... | collective-permute-start | bytes 61448 | tf_op jit(solution)/shard_map/ppermute | solution.py:40
  7.8 61.5 %collective-permute-start.9 = (f32[5,8,1,128]{3,2,0,1:T(1,128)S(1)}, f32[5,8,1,128]{3,2,0,1:T(1,128)S(1)}, u32[]{:S(2)}, u32[]{:S(2)}) collective-permute-start(f32[5,8,1,128]{3,2,0,1:T(1,128)S(1)} %get-tuple-element.16), channel_id=1, source_target_pairs={{4,0},{8,4},{12,8},{16,12},{20,16},{24,20},{28,24},{32,28},{36,32}... | collective-permute-start | bytes 61448 | tf_op jit(solution)/shard_map/ppermute | solution.py:43
  26.5 8.3 %collective-permute-start.2 = (f32[5,32,128]{2,1,0:T(8,128)S(1)}, f32[5,32,128]{2,1,0:T(8,128)S(1)}, u32[]{:S(2)}, u32[]{:S(2)}) collective-permute-start(f32[5,32,128]{2,1,0:T(8,128)S(1)} %bitcast_select_fusion.1), channel_id=1, source_target_pairs={{0,4},{4,8},{8,12},{12,16},{16,20},{20,24},{24,28},{28,32},{32,36}... | collective-permute-start | bytes 245768 | tf_op jit(solution)/shard_map/ppermute | solution.py:31
  34.8 37.4 %copy-start.1 = (f32[1,5,5]{2,0,1:T(1,128)S(1)}, f32[1,5,5]{2,0,1:T(1,128)}, u32[]{:S(2)}) copy-start(f32[1,5,5]{2,0,1:T(1,128)} %param.9) | copy-start | bytes 304
  34.8 8.1 %collective-permute-start.3 = (f32[5,32,128]{2,1,0:T(8,128)S(1)}, f32[5,32,128]{2,1,0:T(8,128)S(1)}, u32[]{:S(2)}, u32[]{:S(2)}) collective-permute-start(f32[5,32,128]{2,1,0:T(8,128)S(1)} %broadcast_select_fusion), channel_id=1, source_target_pairs={{0,8},{4,12},{8,16},{12,20},{16,24},{20,28},{24,32},{28,36},{32,40... | collective-permute-start | bytes 245768 | tf_op jit(solution)/shard_map/ppermute | solution.py:31
  43.0 5.8 %collective-permute-start.4 = (f32[5,32,128]{2,1,0:T(8,128)S(1)}, f32[5,32,128]{2,1,0:T(8,128)S(1)}, u32[]{:S(2)}, u32[]{:S(2)}) collective-permute-start(f32[5,32,128]{2,1,0:T(8,128)S(1)} %broadcast_select_fusion.1), channel_id=1, source_target_pairs={{0,16},{4,20},{8,24},{12,28},{16,32},{20,36},{24,40},{28,44},{32,4... | collective-permute-start | bytes 245768 | tf_op jit(solution)/shard_map/ppermute | solution.py:31
  48.8 6.6 %collective-permute-start.5 = (f32[5,32,128]{2,1,0:T(8,128)S(1)}, f32[5,32,128]{2,1,0:T(8,128)S(1)}, u32[]{:S(2)}, u32[]{:S(2)}) collective-permute-start(f32[5,32,128]{2,1,0:T(8,128)S(1)} %broadcast_select_fusion.2), channel_id=1, source_target_pairs={{0,32},{4,36},{8,40},{12,44},{16,48},{20,52},{24,56},{28,60},{32,6... | collective-permute-start | bytes 245768 | tf_op jit(solution)/shard_map/ppermute | solution.py:31
  55.5 8.4 %collective-permute-start.6 = (f32[5,32,128]{2,1,0:T(8,128)S(1)}, f32[5,32,128]{2,1,0:T(8,128)S(1)}, u32[]{:S(2)}, u32[]{:S(2)}) collective-permute-start(f32[5,32,128]{2,1,0:T(8,128)S(1)} %broadcast_select_fusion.3), channel_id=1, source_target_pairs={{0,64},{4,68},{8,72},{12,76},{16,80},{20,84},{24,88},{28,92},{32,9... | collective-permute-start | bytes 245768 | tf_op jit(solution)/shard_map/ppermute | solution.py:31
  63.9 7.8 %collective-permute-start.7 = (f32[5,1,32,128]{3,2,0,1:T(8,128)S(1)}, f32[5,1,32,128]{3,2,0,1:T(8,128)S(1)}, u32[]{:S(2)}, u32[]{:S(2)}) collective-permute-start(f32[5,1,32,128]{3,2,0,1:T(8,128)S(1)} %select_bitcast_fusion), channel_id=1, source_target_pairs={{0,4},{4,8},{8,12},{12,16},{16,20},{20,24},{24,28},{28,32},{32,36}... | collective-permute-start | bytes 245768 | tf_op jit(solution)/shard_map/ppermute | solution.py:40
  64.0 7.8 %collective-permute-start.8 = (f32[5,1,32,128]{3,2,0,1:T(8,128)S(1)}, f32[5,1,32,128]{3,2,0,1:T(8,128)S(1)}, u32[]{:S(2)}, u32[]{:S(2)}) collective-permute-start(f32[5,1,32,128]{3,2,0,1:T(8,128)S(1)} %select_bitcast_fusion), channel_id=1, source_target_pairs={{4,0},{8,4},{12,8},{16,12},{20,16},{24,20},{28,24},{32,28},{36,32}... | collective-permute-start | bytes 245768 | tf_op jit(solution)/shard_map/ppermute | solution.py:43
  72.1 2.9 %copy-start.3 = (f32[1,5,8,32,128]{4,3,2,1,0:T(8,128)S(1)}, f32[1,5,8,32,128]{4,3,2,1,0:T(8,128)}, u32[]{:S(2)}) copy-start(f32[1,5,8,32,128]{4,3,2,1,0:T(8,128)} %param.7) | copy-start | bytes 1966084
  73.6 3.4 %copy-start = (f32[1,5,5,8,32,128]{5,4,3,2,1,0:T(8,128)S(1)}, f32[1,5,5,8,32,128]{5,4,3,2,1,0:T(8,128)}, u32[]{:S(2)}) copy-start(f32[1,5,5,8,32,128]{5,4,3,2,1,0:T(8,128)} %param.8) | copy-start | bytes 9830404
  79.6 7.3 %collective-permute-start.11 = (f32[5,32,128]{2,0,1:T(8,128)S(1)}, f32[5,32,128]{2,0,1:T(8,128)S(1)}, u32[]{:S(2)}, u32[]{:S(2)}) collective-permute-start(f32[5,32,128]{2,0,1:T(8,128)S(1)} %copy.455), channel_id=1, source_target_pairs={{0,1},{1,2},{2,3},{4,5},{5,6},{6,7},{8,9},{9,10},{10,11},{12,13},{... | collective-permute-start | bytes 245768 | tf_op jit(solution)/shard_map/ppermute | solution.py:51
  90.0 7.4 %collective-permute-start.12 = (f32[5,32,128]{2,0,1:T(8,128)S(1)}, f32[5,32,128]{2,0,1:T(8,128)S(1)}, u32[]{:S(2)}, u32[]{:S(2)}) collective-permute-start(f32[5,32,128]{2,0,1:T(8,128)S(1)} %copy.471), channel_id=1, source_target_pairs={{0,1},{1,2},{2,3},{4,5},{5,6},{6,7},{8,9},{9,10},{10,11},{12,13},{... | collective-permute-start | bytes 245768 | tf_op jit(solution)/shard_map/ppermute | solution.py:51
  100.3 6.9 %collective-permute-start.13 = (f32[5,32,128]{2,0,1:T(8,128)S(1)}, f32[5,32,128]{2,0,1:T(8,128)S(1)}, u32[]{:S(2)}, u32[]{:S(2)}) collective-permute-start(f32[5,32,128]{2,0,1:T(8,128)S(1)} %copy.487), channel_id=1, source_target_pairs={{0,1},{1,2},{2,3},{4,5},{5,6},{6,7},{8,9},{9,10},{10,11},{12,13},{... | collective-permute-start | bytes 245768 | tf_op jit(solution)/shard_map/ppermute | solution.py:51
  112.9 6.8 %collective-permute-start.14 = (f32[5,32,128]{2,1,0:T(8,128)S(1)}, f32[5,32,128]{2,1,0:T(8,128)S(1)}, u32[]{:S(2)}, u32[]{:S(2)}) collective-permute-start(f32[5,32,128]{2,1,0:T(8,128)S(1)} %sub.242), channel_id=1, source_target_pairs={{1,0},{2,1},{3,2},{5,4},{6,5},{7,6},{9,8},{10,9},{11,10},{13,12},{... | collective-permute-start | bytes 245768 | tf_op jit(solution)/shard_map/ppermute | solution.py:51
  122.8 6.3 %collective-permute-start.15 = (f32[5,32,128]{2,1,0:T(8,128)S(1)}, f32[5,32,128]{2,1,0:T(8,128)S(1)}, u32[]{:S(2)}, u32[]{:S(2)}) collective-permute-start(f32[5,32,128]{2,1,0:T(8,128)S(1)} %sub.250), channel_id=1, source_target_pairs={{1,0},{2,1},{3,2},{5,4},{6,5},{7,6},{9,8},{10,9},{11,10},{13,12},{... | collective-permute-start | bytes 245768 | tf_op jit(solution)/shard_map/ppermute | solution.py:51
  132.2 6.3 %collective-permute-start.16 = (f32[5,32,128]{2,1,0:T(8,128)S(1)}, f32[5,32,128]{2,1,0:T(8,128)S(1)}, u32[]{:S(2)}, u32[]{:S(2)}) collective-permute-start(f32[5,32,128]{2,1,0:T(8,128)S(1)} %sub.258), channel_id=1, source_target_pairs={{1,0},{2,1},{3,2},{5,4},{6,5},{7,6},{9,8},{10,9},{11,10},{13,12},{... | collective-permute-start | bytes 245768 | tf_op jit(solution)/shard_map/ppermute | solution.py:51
  140.1 1.7 %copy-start.2 = (f32[1,5,8,32,128]{4,3,2,1,0:T(8,128)S(1)}, f32[1,5,8,32,128]{4,3,2,1,0:T(8,128)}, u32[]{:S(2)}) copy-start(f32[1,5,8,32,128]{4,3,2,1,0:T(8,128)} %param.6) | copy-start | bytes 1966084
where the time goes:
time: 146 us; the launch traced here: 143 us
  waiting for transfers between devices  56.9 us (39%)
  starting transfers between devices  40.2 us (28%)
  matrix products  22.6 us (15%)
  between operations  11.4 us (8%)
  other arithmetic  6.3 us (4%)
  local copies, waits for them, and re-layouts  5.45 us (4%)
    ppermute x5, waiting for transfers between devices, passed_along(): lax.ppermute(shard, axis, [(i, (i + by) % peers) for i in range(peers)])  31.8 us
    ppermute x6, waiting for transfers between devices, shifted(): return lax.ppermute(block, axis, route)  23.1 us
    dot_general x66, matrix products, mix_const(): return jnp.einsum('ij,j...->i...', matrix, field, precision=exact_mode)  22.3 us
    ppermute x6, starting transfers between devices, shifted(): return lax.ppermute(block, axis, route)  16.9 us
    ppermute x2, starting transfers between devices, extended(): lax.ppermute(lax.slice_in_dim(block, 0, width, axis=dim), axis, backward)  12 us
    ppermute x5, starting transfers between devices, passed_along(): lax.ppermute(shard, axis, [(i, (i + by) % peers) for i in range(peers)])  5.29 us
    ppermute x1, starting transfers between devices, padded(): lax.ppermute(last, axis, up)  4.55 us
    unnamed x22, local copies, waits for them, and re-layouts  3.08 us
  transfers between devices with their start and end apart: 17, of which 12 were waited for; matrix products, arithmetic and copies ran while one was open for 3% of the time, Pallas kernels for 0%

commit v1 on v0

v1 whole, which is shorter than its diff:
```python
import jax
import jax.numpy as jnp
from jax import lax
from jax.experimental import pallas as pl
from jax.experimental.pallas import tpu as pltpu
from jax.sharding import PartitionSpec as P

F32 = jnp.float32
V = 5
AXES = ("row", "sector", "slab")
VMEM_BYTES = 14 * 1024 * 1024


def matvec(mat, vec):
    out = []
    for i in range(V):
        acc = mat(i, 0) * vec[0]
        for j in range(1, V):
            acc = acc + mat(i, j) * vec[j]
        out.append(acc)
    return out


def stacked(ref, base):
    return lambda i, j: ref[base + V * i + j]


def planes_of(ref, base):
    return [ref[base + v] for v in range(V)]


def put(ref, base, values):
    for v in range(V):
        ref[base + v] = values[v]


def pack_kernel(planes, columns, state, towards_low, interface, towards_high, lowest):
    row = lax.axis_index("row")
    face = jnp.where(row == 0, planes - 1, 0)
    for v in range(V):
        plane = state[0, v, face]
        interface[v] = plane
        towards_low[v, planes:] = plane
        lowest[v] = state[0, v, 0]
        for x in range(planes):
            towards_low[v, x : x + 1] = state[0, v, x, 0:1]
            towards_high[v, x : x + 1] = state[0, v, x, columns - 1 : columns]


def window_kernel(planes, columns, sectors, owner, own, next_one, next_two, message, table, landing):
    row = lax.axis_index("row")
    sector = lax.axis_index("sector")
    total = sectors * columns
    for v in range(V):
        table[v, 0:columns] = own[v]
        table[v, columns : 2 * columns] = next_one[v, planes:]
        table[v, 2 * columns :] = next_two[v]
    lead = owner[0]

    def lower(i, best):
        gap = lax.rem(owner[i] - lead + total + total // 2, total) - total // 2
        return jnp.minimum(best, gap)

    start = lax.rem(lead + lax.fori_loop(0, columns, lower, 0) + total, total)
    turn = start // columns
    even = turn // 2 * 2

    @pl.when(row == 1)
    def _():
        facing = lax.rem(sector - even + sectors, sectors)

        def step(i, carry):
            at = lax.rem(owner[facing * columns + i] - sector * columns + total, total)
            at = jnp.minimum(at, 3 * columns - 1)
            for v in range(V):
                landing[v, pl.ds(i, 1)] = table[v, pl.ds(at, 1)]
            return carry

        lax.fori_loop(0, columns, step, 0, unroll=4)

    @pl.when(row == 0)
    def _():
        facing = lax.rem(sector + even + 2, sectors)
        first = (1 - (turn - even)) * columns

        def step(i, carry):
            at = first + i
            column = owner[lax.rem(sector * columns + at, total)]
            to = lax.rem(column - facing * columns + total, total)
            to = jnp.minimum(to, columns)
            for v in range(V):
                landing[v, pl.ds(to, 1)] = table[v, pl.ds(at, 1)]
            return carry

        lax.fori_loop(0, 2 * columns, step, 0, unroll=4)

    for v in range(V):
        message[v] = landing[v, 0:columns]


def matrix_kernel(planes, axial, inverse, up, down, product, prefix, left, right):
    scaled = [[0.5 * axial[0, i, j] for j in range(V)] for i in range(V)]

    def forward(x, carry):
        for i in range(V):
            entries = [inverse[0, i, k, x] for k in range(V)]
            for j in range(V):
                acc = entries[0] * scaled[0][j]
                for k in range(1, V):
                    acc = acc + entries[k] * scaled[k][j]
                product[x, V * i + j] = acc
        before = jnp.maximum(x - 1, 0)
        for j in range(V):
            column = [
                jnp.where(x == 0, jnp.full((8, 128), float(i == j), F32), prefix[before, V * i + j])
                for i in range(V)
            ]
            put_column(prefix.at[x], j, matvec(stacked(product.at[x], 0), column))
        return carry

    for k in range(V * V):
        prefix[0, k] = jnp.zeros((8, 128), F32)
        left[k] = jnp.zeros((8, 128), F32)
        right[k] = jnp.full((8, 128), float(k // V == k % V), F32)
    lax.fori_loop(0, planes, forward, 0)

    def backward(step, carry):
        x = planes - 1 - step
        before = jnp.maximum(x - 1, 0)
        for j in range(V):
            column = [
                jnp.where(x == 0, jnp.full((8, 128), float(i == j), F32), prefix[before, V * i + j])
                - left[V * i + j]
                for i in range(V)
            ]
            put_column(left, j, matvec(stacked(product.at[x], 0), column))
            column = [-right[V * i + j] for i in range(V)]
            put_column(right, j, matvec(stacked(product.at[x], 0), column))
        return carry

    lax.fori_loop(0, planes, backward, 0)
    for k in range(V * V):
        up[2 * V + k] = prefix[planes - 1, k]
        down[V + k] = right[k]
        down[V + V * V + k] = left[k]


def put_column(ref, j, values):
    for i in range(V):
        ref[V * i + j] = values[i]


def residual_kernel(
    planes, columns, axial, cross, state, source, inverse, from_high, from_low, above, up_in, down_in,
    residual, up, down, wide, forward,
):
    step = pl.program_id(0)

    @pl.when(step == 0)
    def _():
        for v in range(V):
            for x in range(planes):
                wide[v, x, 8 : 8 + columns] = state[0, v, x]
                wide[v, x, 7:8] = from_low[v, x : x + 1]
                wide[v, x, 8 + columns : 9 + columns] = from_high[v, x : x + 1]

    middle = pl.multiple_of(step * 8 + 8, 8)
    low = pl.multiple_of(step * 8, 8)
    high = pl.multiple_of(step * 8 + 16, 8)
    rows = lax.broadcasted_iota(jnp.int32, (8, 128), 0)
    lanes = lax.broadcasted_iota(jnp.int32, (8, 128), 1)
    ja = lambda i, j: 0.5 * axial[0, i, j]
    jb = lambda i, j: 0.5 * cross[0, 0, i, j]
    jr = lambda i, j: 0.5 * cross[0, 1, i, j]
    previous = None
    for x in range(planes):
        along, around, outward = [], [], []
        for v in range(V):
            here = wide[v, x, pl.ds(middle, 8)]
            nearer = wide[v, x + 1, pl.ds(middle, 8)] if x + 1 < planes else above[v]
            along.append(nearer - wide[v, x - 1, pl.ds(middle, 8)] if x else nearer)
            plus = jnp.where(rows == 0, wide[v, x, pl.ds(high, 8)], here)
            minus = jnp.where(rows == 7, wide[v, x, pl.ds(low, 8)], here)
            around.append(pltpu.roll(plus, 7, 0) - pltpu.roll(minus, 1, 0))
            outward.append(
                jnp.where(lanes == 127, 0.0, pltpu.roll(here, 127, 1))
                - jnp.where(lanes == 0, 0.0, pltpu.roll(here, 1, 1))
            )
        one, two, three = matvec(ja, along), matvec(jb, around), matvec(jr, outward)
        values = [source[0, v, x] - (one[v] + two[v] + three[v]) for v in range(V)]
        for v in range(V):
            residual[v, x] = values[v]
        if previous is not None:
            carried = matvec(ja, previous)
            values = [values[v] + carried[v] for v in range(V)]
        previous = matvec(lambda i, j, x=x: inverse[0, i, j, x], values)
        for v in range(V):
            forward[v, x] = previous[v]
    for v in range(V):
        last = wide[v, planes - 1, pl.ds(middle, 8)]
        up[v] = previous[v] + last
        up[V + v] = last
    for x in range(planes - 2, -1, -1):
        carried = matvec(lambda i, j, x=x: inverse[0, i, j, x], matvec(ja, previous))
        previous = [forward[v, x] - carried[v] for v in range(V)]
    for v in range(V):
        down[v] = previous[v]


def first_kernel(slabs, ghost, up, down, entry, message):
    slab = lax.axis_index("slab")
    values = planes_of(ghost, 0)
    for v in range(V):
        message[V + v] = up[V + v]

    @pl.when(slab == 0)
    def _():
        moved = matvec(stacked(up, 2 * V), values)
        for v in range(V):
            total = up[v] + moved[v]
            entry[v] = total
            message[v] = total

    @pl.when(slab != 0)
    def _():
        moved = matvec(stacked(down, V), values)
        for v in range(V):
            entry[v] = up[v]
            message[v] = moved[v]


def middle_kernel(came, came_side, up_other, down_other, up, down, lower, message, entry, leaving):
    slab = lax.axis_index("slab")

    @pl.when(slab == 2)
    def _():
        moved = matvec(stacked(up_other, 2 * V), planes_of(came, 0))
        second = [up_other[v] + moved[v] for v in range(V)]
        moved = matvec(stacked(up, 2 * V), second)
        third = [up[v] + moved[v] for v in range(V)]
        moved = matvec(stacked(down_other, V + V * V), third)
        top = [down_other[v] + came_side[v] + moved[v] for v in range(V)]
        moved = matvec(stacked(down, V + V * V), second)
        again = matvec(stacked(down, V), top)
        put(lower, 0, [down[v] + moved[v] + again[v] for v in range(V)])
        put(message, 0, third)
        put(message, V, planes_of(up, V))
        put(entry, 0, second)
        put(leaving, 0, top)


def last_kernel(
    planes, axial, ghost, came_side, to_third, to_zero, to_one, entry, leaving, zeroth,
    up_other, down_other, partial, inverse, state, residual, new_state, forward, inflow, beyond, under,
):
    row = lax.axis_index("row")
    slab = lax.axis_index("slab")
    ja = lambda i, j: 0.5 * axial[0, i, j]

    @pl.when(slab == 0)
    def _():
        put(inflow, 0, planes_of(ghost, 0))
        put(under, 0, planes_of(ghost, 0))
        one = matvec(stacked(down_other, V + V * V), planes_of(zeroth, 0))
        two = matvec(stacked(down_other, V), planes_of(to_zero, 0))
        put(beyond, 0, [down_other[v] + one[v] + two[v] for v in range(V)])

    @pl.when(slab == 1)
    def _():
        put(inflow, 0, planes_of(came_side, 0))
        put(under, 0, planes_of(came_side, V))
        put(beyond, 0, planes_of(to_one, 0))

    @pl.when(slab == 2)
    def _():
        put(inflow, 0, planes_of(entry, 0))
        put(under, 0, planes_of(up_other, V))
        put(beyond, 0, planes_of(leaving, 0))

    @pl.when(slab == 3)
    def _():
        put(inflow, 0, planes_of(to_third, 0))
        put(under, 0, planes_of(to_third, V))
        put(beyond, 0, [jnp.zeros((8, 128), F32)] * V)

    has_top = jnp.where((row == 0) & (slab == 3), 1.0, 0.0)
    previous = planes_of(inflow, 0)
    for x in range(planes):
        values = [partial[v, x] for v in range(V)]
        if x == planes - 1:
            top = matvec(ja, [ghost[v] * has_top for v in range(V)])
            values = [values[v] - top[v] for v in range(V)]
        if x == 0:
            bottom = matvec(ja, planes_of(under, 0))
            for v in range(V):
                residual[0, v, x] = values[v] + bottom[v]
        else:
            for v in range(V):
                residual[0, v, x] = values[v]
        carried = matvec(ja, previous)
        values = [values[v] + carried[v] for v in range(V)]
        previous = matvec(lambda i, j, x=x: inverse[0, i, j, x], values)
        for v in range(V):
            forward[v, x] = previous[v]
    following = planes_of(beyond, 0)
    for x in range(planes - 1, -1, -1):
        carried = matvec(lambda i, j, x=x: inverse[0, i, j, x], matvec(ja, following))
        following = [forward[v, x] - carried[v] for v in range(V)]
        for v in range(V):
            new_state[0, v, x] = state[0, v, x] + following[v]


def sds(*shape):
    return jax.ShapeDtypeStruct(shape, F32)


def full(shape):
    return pl.BlockSpec(shape, lambda *_: (0,) * len(shape))


def strip(lead):
    return pl.BlockSpec((lead, 8, 128), lambda i: (0, i, 0))


SCALARS = pl.BlockSpec(memory_space=pltpu.SMEM)


def params(**more):
    return pltpu.CompilerParams(vmem_limit_bytes=VMEM_BYTES, **more)


def cost(amount):
    return pl.CostEstimate(flops=amount, bytes_accessed=amount // 8, transcendentals=0)


def per_device(state, source, diag_inverse, jac_axial, jac_cross, owner):
    planes, columns, radial = state.shape[2:]
    sectors = lax.axis_size("sector")
    slabs = lax.axis_size("slab")
    strips = columns // 8
    plane = (V, columns, radial)
    cells = pl.BlockSpec((1, V, planes, 8, radial), lambda i: (0, 0, 0, i, 0))
    blocks = pl.BlockSpec((1, V, V, planes, 8, radial), lambda i: (0, 0, 0, 0, i, 0))
    inner = pl.BlockSpec((V, planes, 8, radial), lambda i: (0, 0, i, 0))
    size = slabs * sectors

    def device(row, sector, slab):
        return row * size + sector % sectors * slabs + slab

    def import_pairs(even):
        pairs = []
        for j in range(sectors):
            pairs.append((device(1, j, 0), device(0, j - even, slabs - 1)))
            pairs.append((device(0, j, slabs - 1), device(1, j + even + 2, 0)))
        return pairs

    two_down = []
    for j in range(sectors):
        two_down.append((device(0, j, slabs - 1), device(0, j - 2, slabs - 1)))
        two_down.append((device(1, j, 0), device(1, j - 2, 0)))

    towards_low, interface, towards_high, lowest = pl.pallas_call(
        lambda *refs: pack_kernel(planes, columns, *refs),
        out_shape=(sds(V, planes + columns, radial), sds(*plane), sds(V, planes, radial), sds(*plane)),
        compiler_params=params(),
        name="pack",
    )(state)
    from_high = lax.ppermute(towards_low, "sector", [(j, (j - 1) % sectors) for j in range(sectors)])
    from_second = lax.ppermute(interface, AXES, two_down)
    from_low = lax.ppermute(towards_high, "sector", [(j, (j + 1) % sectors) for j in range(sectors)])
    above = lax.ppermute(lowest, "slab", [(k, k - 1) for k in range(1, slabs)])

    up, down = pl.pallas_call(
        lambda *refs: matrix_kernel(planes, *refs),
        grid=(strips,),
        in_specs=[SCALARS, blocks],
        out_specs=(strip(2 * V + V * V), strip(V + 2 * V * V)),
        out_shape=(sds(2 * V + V * V, columns, radial), sds(V + 2 * V * V, columns, radial)),
        scratch_shapes=[
            pltpu.VMEM((planes, V * V, 8, radial), F32),
            pltpu.VMEM((planes, V * V, 8, radial), F32),
            pltpu.VMEM((V * V, 8, radial), F32),
            pltpu.VMEM((V * V, 8, radial), F32),
        ],
        compiler_params=params(),
        cost_estimate=cost(80_000_000),
        name="matrices",
    )(jac_axial, diag_inverse)

    message = pl.pallas_call(
        lambda *refs: window_kernel(planes, columns, sectors, *refs),
        in_specs=[SCALARS] + [pl.BlockSpec(memory_space=pltpu.VMEM)] * 3,
        out_shape=sds(*plane),
        scratch_shapes=[
            pltpu.VMEM((V, 3 * columns, radial), F32),
            pltpu.VMEM((V, columns + 8, radial), F32),
        ],
        compiler_params=params(),
        name="window",
    )(owner, interface, from_high, from_second)

    def exchange(even, message, from_low, above, from_high, up, down):
        ghost = lax.ppermute(message, AXES, import_pairs(even))
        partial, up, down = pl.pallas_call(
            lambda *refs: residual_kernel(planes, columns, *refs),
            grid=(strips,),
            in_specs=[
                SCALARS, SCALARS, full(state.shape), cells, blocks,
                full(towards_low.shape), full(towards_high.shape), strip(V),
                pl.BlockSpec(memory_space=pl.ANY), pl.BlockSpec(memory_space=pl.ANY),
            ],
            out_specs=(inner, strip(2 * V), strip(V)),
            out_shape=(sds(V, planes, columns, radial), up, down),
            input_output_aliases={8: 1, 9: 2},
            scratch_shapes=[
                pltpu.VMEM((V, planes, columns + 16, radial), F32),
                pltpu.VMEM((V, planes, 8, radial), F32),
            ],
            compiler_params=params(),
            cost_estimate=cost(40_000_000),
            name="residual",
        )(jac_axial, jac_cross, state, source, diag_inverse, from_high, from_low, above, up, down)
        up_other = lax.ppermute(up, "slab", [(1, 2)])
        down_other = lax.ppermute(down, "slab", [(1, 0), (3, 2)])
        return ghost, partial, up, down, up_other, down_other

    total = sectors * columns
    assert total & (total - 1) == 0
    lead = owner[:columns]
    gaps = ((lead - owner[0] + total // 2) & (total - 1)) - total // 2
    pair = lax.shift_right_logical(
        (owner[0] + jnp.min(gaps)) & (total - 1), jnp.int32((2 * columns).bit_length() - 1)
    )
    ghost, partial, up, down, up_other, down_other = lax.switch(
        pair,
        [lambda *args, e=e: exchange(2 * e, *args) for e in range(sectors // 2)],
        message, from_low, above, from_high, up, down,
    )

    entry, side = pl.pallas_call(
        lambda *refs: first_kernel(slabs, *refs),
        out_shape=(sds(*plane), sds(2 * V, columns, radial)),
        compiler_params=params(),
        name="first",
    )(ghost, up, down)
    came = lax.ppermute(entry, "slab", [(0, 2)])
    came_side = lax.ppermute(side, "slab", [(0, 1), (3, 2)])
    lower, onward, second, top = pl.pallas_call(
        middle_kernel,
        out_shape=(sds(*plane), sds(2 * V, columns, radial), sds(*plane), sds(*plane)),
        compiler_params=params(),
        name="middle",
    )(came, came_side, up_other, down_other, up, down)
    to_zero = lax.ppermute(lower, "slab", [(2, 0)])
    to_one = lax.ppermute(lower, "slab", [(2, 1)])
    to_third = lax.ppermute(onward, "slab", [(2, 3)])

    residual, new_state = pl.pallas_call(
        lambda *refs: last_kernel(planes, *refs),
        grid=(strips,),
        in_specs=[
            SCALARS, strip(V), strip(2 * V), strip(2 * V), strip(V), strip(V), strip(V), strip(V),
            strip(V), strip(2 * V + V * V), strip(V + 2 * V * V), inner, blocks, cells,
        ],
        out_specs=(cells, cells),
        out_shape=(sds(*state.shape), sds(*state.shape)),
        scratch_shapes=[pltpu.VMEM((V, planes, 8, radial), F32)]
        + [pltpu.VMEM((V, 8, radial), F32)] * 3,
        compiler_params=params(),
        name="last",
    )(
        jac_axial, ghost, came_side, to_third, to_zero, to_one, second, top, entry,
        up_other, down_other, partial, diag_inverse, state,
    )
    return residual, new_state


def solution(mesh):
    return jax.shard_map(
        per_device,
        mesh=mesh,
        in_specs=(
            P("row", None, "slab", "sector", None),
            P("row", None, "slab", "sector", None),
            P("row", None, None, "slab", "sector", None),
            P("row", None, None),
            P("row", None, None, None),
            P(),
        ),
        out_specs=(P("row", None, "slab", "sector", None), P("row", None, "slab", "sector", None)),
        check_vma=False,
    )
```

time: 146 us -> 77.9 us (0.53); the launches traced: 143 us -> 77.3 us
  waiting for transfers between devices: 56.9 us -> 28.8 us
  matrix products: 22.6 us -> 0 us
  Pallas kernels: 0 us -> 19.9 us
  starting transfers between devices: 40.2 us -> 22.6 us
  between operations: 11.4 us -> 2.14 us
  other arithmetic: 6.3 us -> 1.97 us
  local copies, waits for them, and re-layouts: 5.45 us -> 1.92 us
    ppermute x17 -> x12, waiting for transfers between devices: 56.9 us -> 28.8 us  [the longest x1 19 us: exchange(): down_other = lax.ppermute(down, 'slab', [(1, 0), (3, 2)])]
    dot_general x67 -> x0, matrix products: 22.6 us -> none  [the longest x66 22.3 us: mix_const(): return jnp.einsum('ij,j...->i...', matrix, field, precision=exact_mode)]
    pallas_call x0 -> x7, Pallas kernels: none -> 19.9 us  [the longest x1 6.93 us: per_device(): pl.pallas_call(lambda *refs: matrix_kernel(planes, *refs), grid=(strips,)...]
    ppermute x17 -> x12, starting transfers between devices: 40.2 us -> 22.6 us  [the longest x1 6.65 us: per_device(): lax.ppermute(towards_low, 'sector', [(j, (j - 1) % sectors) for j in rang...]
    reduce_sum x64 -> x0, other arithmetic: 3.95 us -> none  [the longest x63 2.62 us: per_cell(): return jnp.sum(blocks * field[None], axis=1)]
    unnamed x22 -> x13, local copies, waits for them, and re-layouts: 3.08 us -> 0.72 us
    reduce_min x0 -> x1, other arithmetic: none -> 1.97 us  [per_device(): jnp.min(gaps)]
  transfers between devices with their start and end apart: 17 -> 12, of which waited for: 12 -> 3; matrix products, arithmetic and copies ran while one was open for 3% -> 5% of each run, Pallas kernels for 0% -> 11%
where the time goes in v1:
time: 77.9 us; the launch traced here: 77.3 us
  waiting for transfers between devices  28.8 us (37%)
  starting transfers between devices  22.6 us (29%)
  Pallas kernels  19.9 us (26%)
  between operations  2.14 us (3%)
  other arithmetic  1.97 us (3%)
  local copies, waits for them, and re-layouts  1.92 us (2%)
    ppermute x1, waiting for transfers between devices, exchange(): down_other = lax.ppermute(down, 'slab', [(1, 0), (3, 2)])  19 us
    ppermute x1, waiting for transfers between devices, per_device(): to_zero = lax.ppermute(lower, 'slab', [(2, 0)])  7.74 us
    pallas_call x1, Pallas kernels, per_device(): pl.pallas_call(lambda *refs: matrix_kernel(planes, *refs), grid=(strips,)...  6.93 us
    ppermute x1, starting transfers between devices, per_device(): lax.ppermute(towards_low, 'sector', [(j, (j - 1) % sectors) for j in rang...  6.65 us
    ppermute x1, starting transfers between devices, per_device(): came = lax.ppermute(entry, 'slab', [(0, 2)])  5.85 us
    pallas_call x1, Pallas kernels, per_device(): pl.pallas_call(lambda *refs: last_kernel(planes, *refs), grid=(strips,),...  4.21 us
    pallas_call x1, Pallas kernels, exchange(): pl.pallas_call(lambda *refs: residual_kernel(planes, columns, *refs), gri...  3.7 us
    ppermute x1, waiting for transfers between devices, per_device(): came = lax.ppermute(entry, 'slab', [(0, 2)])  2.04 us
  transfers between devices with their start and end apart: 12, of which 3 were waited for; matrix products, arithmetic and copies ran while one was open for 5% of the time, Pallas kernels for 11%

profile of v1, /device:TPU:0, one launch (start us, length us, event | category | flops | bytes accessed | tf_op | source)
XLA Modules:
  0.0 77.3 jit_solution(4541771750692692171)
XLA Ops:
  0.6 0.0 copy-start.3
  0.6 0.0 copy-start
  0.7 0.0 copy-start.5
  0.7 0.0 copy-start.4
  0.7 1.2 %pack.1 = (f32[5,40,128]{2,1,0:T(8,128)S(1)}, f32[5,32,128]{2,1,0:T(8,128)S(1)}, f32[5,8,128]{2,1,0:T(8,128)S(1)}, f32[5,32,128]{2,1,0:T(8,128)S(1)}) custom-call(f32[1,5,8,32,128]{4,3,2,1,0:T(8,128)} %refs_13_.1), custom_call_target="tpu_custom_call" | custom-call | tf_op jit(solution)/shard_map/pack/pallas_call | solution.py:362
  1.9 0.1 collective-permute-start.50
  2.0 1.3 %collective-permute-start.51 = (f32[5,32,128]{2,1,0:T(8,128)S(1)}, f32[5,32,128]{2,1,0:T(8,128)S(1)}, u32[]{:S(2)}, u32[]{:S(2)}) collective-permute-start(f32[5,32,128]{2,1,0:T(8,128)S(1)} %get-tuple-element.599), channel_id=1, source_target_pairs={{1,0},{2,1},{3,2},{5,4},{6,5},{7,6},{9,8},{10,9},{11,10},{13,12},{... | collective-permute-start | bytes 245768 | tf_op jit(solution)/shard_map/ppermute | solution.py:371
  3.3 0.7 collective-permute-start.49
  3.9 6.6 %collective-permute-start.48 = (f32[5,40,128]{2,1,0:T(8,128)S(1)}, f32[5,40,128]{2,1,0:T(8,128)S(1)}, u32[]{:S(2)}, u32[]{:S(2)}) collective-permute-start(f32[5,40,128]{2,1,0:T(8,128)S(1)} %get-tuple-element.597), channel_id=1, source_target_pairs={{0,124},{4,0},{8,4},{12,8},{16,12},{20,16},{24,20},{28,24},{32,28}... | collective-permute-start | bytes 307208 | tf_op jit(solution)/shard_map/ppermute | solution.py:368
  10.6 1.2 %slice.7 = s32[1]{0:T(128)} slice(s32[1024]{0:T(1024)} %refs_0_.5), slice={[0:1]} | slice | bytes 8 | tf_op jit(solution)/shard_map/slice | solution.py:432
  11.8 2.0 %add_reduce_fusion = s32[]{:T(128)} fusion(s32[1024]{0:T(1024)} %refs_0_.5, s32[]{:T(128)} %bitcast), kind=kLoop, calls=%fused_computation | loop fusion | flops 159 | bytes 136 | tf_op jit(solution)/shard_map/reduce_min | solution.py:432
  15.0 0.7 copy.73.refs_0_
  15.7 0.0 copy-start.1
  15.7 6.9 %matrices.1 = (f32[35,32,128]{2,1,0:T(8,128)S(1)}, f32[55,32,128]{2,1,0:T(8,128)S(1)}) custom-call(f32[1,5,5]{2,1,0:T(8,128)S(1)} %copy.73.refs_0_, f32[1,5,5,8,32,128]{5,4,3,2,1,0:T(8,128)} %refs_12_.1), custom_call_target="tpu_custom_call" | custom-call | flops 80000000 | bytes 10000000 | tf_op jit(solution)/shard_map/matrices/pallas_call | solution.py:373
  22.7 0.0 collective-permute-done.49.refs_3_
  22.7 0.0 collective-permute-done.48.refs_2_
  22.7 0.0 copy-done
  22.7 1.4 %window.1 = f32[5,32,128]{2,1,0:T(8,128)S(1)} custom-call(s32[1024]{0:T(1024)S(1)} %copy-done, f32[5,32,128]{2,1,0:T(8,128)S(1)} %get-tuple-element.596.refs_1_, f32[5,40,128]{2,1,0:T(8,128)S(1)} %collective-permute-done.48.refs_2_, f32[5,32,128]{2,1,0:T(8,128)S(1)} %collective-permute-done.49.refs_3_), custom_call_target="tpu_custom_call" | custom-call | tf_op jit(solution)/shard_map/window/pallas_call | solution.py:390
  24.1 0.0 collective-permute-done.50
  24.2 0.0 collective-permute-done.51
  24.2 0.0 copy-done.3
  24.2 0.0 copy-done.5
  24.2 0.0 copy-done.4
  24.2 0.0 copy-done.1
  24.2 26.8 %conditional.1 = (f32[5,32,128]{2,1,0:T(8,128)}, f32[5,8,32,128]{3,2,1,0:T(8,128)S(1)}, f32[35,32,128]{2,1,0:T(8,128)S(1)}, f32[55,32,128]{2,1,0:T(8,128)S(1)}, ...) conditional(s32[]{:T(128)} %clamp.3, (f32[5,32,128]{2,1,0:T(8,128)S(1)}, ...), branch_computations={%region_1.0_spmd, %region_2.0_spmd, %region_3.0_spmd, %region_4.0_... | conditional | flops 40000000 | bytes 11226688 | solution.py:434
  24.3 3.7 %residual.23 = (f32[5,8,32,128]{3,2,1,0:T(8,128)S(1)}, f32[35,32,128]{2,1,0:T(8,128)S(1)}, f32[55,32,128]{2,1,0:T(8,128)S(1)}) custom-call(f32[1,5,5]{2,1,0:T(8,128)S(1)} %copy.55.refs_0_, f32[1,2,5,5]{3,2,1,0:T(8,128)S(1)} %copy.56.refs_1_, f32[1,5,8,32,128]{4,3,2,1,0:T(8,128)S(1)} %get-tuple-element.453.refs_2_, ...), custom_call_target="tpu_custom_call", output_to_operand_aliasing={{1}: (8, {}), {2}: (9, {})} | custom-call | flops 40000000 | bytes 5000000 | tf_op jit(solution)/shard_map/cond/branch_7_fun/residual/pallas_call | solution.py:404
  28.0 1.3 %collective-permute-start.23 = (f32[55,32,128]{2,1,0:T(8,128)S(1)}, f32[55,32,128]{2,1,0:T(8,128)}, u32[]{:S(2)}, u32[]{:S(2)}) collective-permute-start(f32[55,32,128]{2,1,0:T(8,128)S(1)} %get-tuple-element.835), channel_id=1, source_target_pairs={{1,0},{3,2},{5,4},{7,6},{9,8},{11,10},{13,12},{15,14},{17,16},{19,... | collective-permute-start | bytes 2703368 | tf_op jit(solution)/shard_map/cond/branch_7_fun/ppermute | solution.py:424
  29.3 1.5 %collective-permute-start.22 = (f32[35,32,128]{2,1,0:T(8,128)S(1)}, f32[35,32,128]{2,1,0:T(8,128)}, u32[]{:S(2)}, u32[]{:S(2)}) collective-permute-start(f32[35,32,128]{2,1,0:T(8,128)S(1)} %get-tuple-element.834), channel_id=1, source_target_pairs={{1,2},{5,6},{9,10},{13,14},{17,18},{21,22},{25,26},{29,30},{33,34}... | collective-permute-start | bytes 1720328 | tf_op jit(solution)/shard_map/cond/branch_7_fun/ppermute | solution.py:423
  30.8 1.3 %collective-permute-start.21 = (f32[5,32,128]{2,1,0:T(8,128)S(1)}, f32[5,32,128]{2,1,0:T(8,128)}, u32[]{:S(2)}, u32[]{:S(2)}) collective-permute-start(f32[5,32,128]{2,1,0:T(8,128)S(1)} %get-tuple-element.450), channel_id=1, source_target_pairs={{128,75},{3,192},{132,79},{7,196},{136,83},{11,200},{140,87},{15,2... | collective-permute-start | bytes 245768 | tf_op jit(solution)/shard_map/cond/branch_7_fun/ppermute | solution.py:403
  32.1 0.0 collective-permute-done.21
  32.1 0.0 collective-permute-done.22
  32.1 19.0 %collective-permute-done.23 = f32[55,32,128]{2,1,0:T(8,128)} collective-permute-done((f32[55,32,128]{2,1,0:T(8,128)S(1)}, f32[55,32,128]{2,1,0:T(8,128)}, u32[]{:S(2)}, u32[]{:S(2)}) %collective-permute-start.23) | collective-permute-done | bytes 901152 | tf_op jit(solution)/shard_map/cond/branch_7_fun/ppermute | solution.py:424
  51.0 0.0 copy-start.2
  51.0 1.1 %first.1 = (f32[5,32,128]{2,1,0:T(8,128)S(1)}, f32[10,32,128]{2,1,0:T(8,128)S(1)}) custom-call(f32[5,32,128]{2,1,0:T(8,128)} %get-tuple-element.602.refs_0_.refs_1_, f32[35,32,128]{2,1,0:T(8,128)S(1)} %get-tuple-element.603.refs_1_.up, f32[55,32,128]{2,1,0:T(8,128)S(1)} %get-tuple-element.604.refs_2_.down), custom_call_target="tpu_custom_call" | custom-call | tf_op jit(solution)/shard_map/first/pallas_call | solution.py:440
  52.1 1.3 %collective-permute-start.52 = (f32[10,32,128]{2,1,0:T(8,128)S(1)}, f32[10,32,128]{2,1,0:T(8,128)S(1)}, u32[]{:S(2)}, u32[]{:S(2)}) collective-permute-start(f32[10,32,128]{2,1,0:T(8,128)S(1)} %get-tuple-element.605), channel_id=1, source_target_pairs={{0,1},{3,2},{4,5},{7,6},{8,9},{11,10},{12,13},{15,14},{16,17},{19,... | collective-permute-start | bytes 491528 | tf_op jit(solution)/shard_map/ppermute | solution.py:447
  53.5 5.9 %collective-permute-start.53 = (f32[5,32,128]{2,1,0:T(8,128)S(1)}, f32[5,32,128]{2,1,0:T(8,128)S(1)}, u32[]{:S(2)}, u32[]{:S(2)}) collective-permute-start(f32[5,32,128]{2,1,0:T(8,128)S(1)} %get-tuple-element.606.refs_8_), channel_id=1, source_target_pairs={{0,2},{4,6},{8,10},{12,14},{16,18},{20,22},{24,26},{28,30},{32,34}... | collective-permute-start | bytes 245768 | tf_op jit(solution)/shard_map/ppermute | solution.py:446
  59.3 2.0 %collective-permute-done.53.came = f32[5,32,128]{2,1,0:T(8,128)S(1)} collective-permute-done((f32[5,32,128]{2,1,0:T(8,128)S(1)}, f32[5,32,128]{2,1,0:T(8,128)S(1)}, u32[]{:S(2)}, u32[]{:S(2)}) %collective-permute-start.53) | collective-permute-done | bytes 81952 | tf_op jit(solution)/shard_map/ppermute | solution.py:446
  61.4 0.0 collective-permute-done.52.came_side.refs_2_
  61.4 1.4 %middle.1 = (f32[5,32,128]{2,1,0:T(8,128)S(1)}, f32[10,32,128]{2,1,0:T(8,128)S(1)}, f32[5,32,128]{2,1,0:T(8,128)S(1)}, f32[5,32,128]{2,1,0:T(8,128)S(1)}) custom-call(f32[5,32,128]{2,1,0:T(8,128)S(1)} %collective-permute-done.53.came, f32[10,32,128]{2,1,0:T(8,128)S(1)} %collective-permute-done.52.came_side.refs_2_, ...), custom_call_target="tpu_custom_call" | custom-call | tf_op jit(solution)/shard_map/middle/pallas_call | solution.py:448
  62.7 0.7 collective-permute-start.54
  63.4 0.7 collective-permute-start.56
  64.1 1.3 %collective-permute-start.55 = (f32[5,32,128]{2,1,0:T(8,128)S(1)}, f32[5,32,128]{2,1,0:T(8,128)S(1)}, u32[]{:S(2)}, u32[]{:S(2)}) collective-permute-start(f32[5,32,128]{2,1,0:T(8,128)S(1)} %get-tuple-element.610), channel_id=1, source_target_pairs={{2,0},{6,4},{10,8},{14,12},{18,16},{22,20},{26,24},{30,28},{34,32}... | collective-permute-start | bytes 245768 | tf_op jit(solution)/shard_map/ppermute | solution.py:454
  65.4 0.0 collective-permute-done.56.refs_5_
  65.4 7.7 %collective-permute-done.55.refs_4_ = f32[5,32,128]{2,1,0:T(8,128)S(1)} collective-permute-done((f32[5,32,128]{2,1,0:T(8,128)S(1)}, f32[5,32,128]{2,1,0:T(8,128)S(1)}, u32[]{:S(2)}, u32[]{:S(2)}) %collective-permute-start.55) | collective-permute-done | bytes 81952 | tf_op jit(solution)/shard_map/ppermute | solution.py:454
  73.1 0.0 collective-permute-done.54.refs_3_
  73.1 0.0 copy-done.2
  73.1 4.2 %last.1 = (f32[1,5,8,32,128]{4,3,2,1,0:T(8,128)}, f32[1,5,8,32,128]{4,3,2,1,0:T(8,128)}) custom-call(f32[1,5,5]{2,1,0:T(8,128)S(1)} %copy.73.refs_0_, f32[5,32,128]{2,1,0:T(8,128)} %get-tuple-element.602.refs_0_.refs_1_, f32[10,32,128]{2,1,0:T(8,128)S(1)} %collective-permute-done.52.came_side.refs_2_, f32[10,32,128]{2,1,0:T(8,128)S(1)} %collective-permute-done.54.refs_3_, ...), custom_call_target="tpu_custom_call" | custom-call | tf_op jit(solution)/shard_map/last/pallas_call | solution.py:458
  (2 shorter events, 0.0 us)
Async XLA Ops:
  0.6 23.5 %copy-start.3 = (f32[1,5,8,32,128]{4,3,2,1,0:T(8,128)S(1)}, f32[1,5,8,32,128]{4,3,2,1,0:T(8,128)}, u32[]{:S(2)}) copy-start(f32[1,5,8,32,128]{4,3,2,1,0:T(8,128)} %refs_13_.1) | copy-start | bytes 1966084
  0.6 22.1 %copy-start = (s32[1024]{0:T(1024)S(1)}, s32[1024]{0:T(1024)}, u32[]{:S(2)}) copy-start(s32[1024]{0:T(1024)} %refs_0_.5) | copy-start | bytes 12292
  0.7 23.5 %copy-start.5 = (f32[1,5,5]{2,0,1:T(1,128)S(1)}, f32[1,5,5]{2,0,1:T(1,128)}, u32[]{:S(2)}) copy-start(f32[1,5,5]{2,0,1:T(1,128)} %param.25) | copy-start | bytes 304
  0.7 23.5 %copy-start.4 = (f32[1,2,5,5]{3,1,2,0:T(2,128)S(1)}, f32[1,2,5,5]{3,1,2,0:T(2,128)}, u32[]{:S(2)}) copy-start(f32[1,2,5,5]{3,1,2,0:T(2,128)} %param.26) | copy-start | bytes 604
  1.9 22.3 %collective-permute-start.50 = (f32[5,8,128]{2,1,0:T(8,128)S(1)}, f32[5,8,128]{2,1,0:T(8,128)S(1)}, u32[]{:S(2)}, u32[]{:S(2)}) collective-permute-start(f32[5,8,128]{2,1,0:T(8,128)S(1)} %get-tuple-element.598), channel_id=1, source_target_pairs={{0,4},{4,8},{8,12},{12,16},{16,20},{20,24},{24,28},{28,32},{32,36}... | collective-permute-start | bytes 61448 | tf_op jit(solution)/shard_map/ppermute | solution.py:370
  2.0 22.2 %collective-permute-start.51 = (f32[5,32,128]{2,1,0:T(8,128)S(1)}, f32[5,32,128]{2,1,0:T(8,128)S(1)}, u32[]{:S(2)}, u32[]{:S(2)}) collective-permute-start(f32[5,32,128]{2,1,0:T(8,128)S(1)} %get-tuple-element.599), channel_id=1, source_target_pairs={{1,0},{2,1},{3,2},{5,4},{6,5},{7,6},{9,8},{10,9},{11,10},{13,12},{... | collective-permute-start | bytes 245768 | tf_op jit(solution)/shard_map/ppermute | solution.py:371
  3.3 19.4 %collective-permute-start.49 = (f32[5,32,128]{2,1,0:T(8,128)S(1)}, f32[5,32,128]{2,1,0:T(8,128)S(1)}, u32[]{:S(2)}, u32[]{:S(2)}) collective-permute-start(f32[5,32,128]{2,1,0:T(8,128)S(1)} %get-tuple-element.596.refs_1_), channel_id=1, source_target_pairs={{3,123},{128,248},{7,127},{132,252},{11,3},{136,128},{15,7},{140,1... | collective-permute-start | bytes 245768 | tf_op jit(solution)/shard_map/ppermute | solution.py:369
  3.9 18.8 %collective-permute-start.48 = (f32[5,40,128]{2,1,0:T(8,128)S(1)}, f32[5,40,128]{2,1,0:T(8,128)S(1)}, u32[]{:S(2)}, u32[]{:S(2)}) collective-permute-start(f32[5,40,128]{2,1,0:T(8,128)S(1)} %get-tuple-element.597), channel_id=1, source_target_pairs={{0,124},{4,0},{8,4},{12,8},{16,12},{20,16},{24,20},{28,24},{32,28}... | collective-permute-start | bytes 307208 | tf_op jit(solution)/shard_map/ppermute | solution.py:368
  15.7 8.5 %copy-start.1 = (f32[1,5,5,8,32,128]{5,4,3,2,1,0:T(8,128)S(1)}, f32[1,5,5,8,32,128]{5,4,3,2,1,0:T(8,128)}, u32[]{:S(2)}) copy-start(f32[1,5,5,8,32,128]{5,4,3,2,1,0:T(8,128)} %refs_12_.1) | copy-start | bytes 9830404
  28.0 23.1 %collective-permute-start.23 = (f32[55,32,128]{2,1,0:T(8,128)S(1)}, f32[55,32,128]{2,1,0:T(8,128)}, u32[]{:S(2)}, u32[]{:S(2)}) collective-permute-start(f32[55,32,128]{2,1,0:T(8,128)S(1)} %get-tuple-element.835), channel_id=1, source_target_pairs={{1,0},{3,2},{5,4},{7,6},{9,8},{11,10},{13,12},{15,14},{17,16},{19,... | collective-permute-start | bytes 2703368 | tf_op jit(solution)/shard_map/cond/branch_7_fun/ppermute | solution.py:424
  29.3 2.8 %collective-permute-start.22 = (f32[35,32,128]{2,1,0:T(8,128)S(1)}, f32[35,32,128]{2,1,0:T(8,128)}, u32[]{:S(2)}, u32[]{:S(2)}) collective-permute-start(f32[35,32,128]{2,1,0:T(8,128)S(1)} %get-tuple-element.834), channel_id=1, source_target_pairs={{1,2},{5,6},{9,10},{13,14},{17,18},{21,22},{25,26},{29,30},{33,34}... | collective-permute-start | bytes 1720328 | tf_op jit(solution)/shard_map/cond/branch_7_fun/ppermute | solution.py:423
  30.8 1.3 %collective-permute-start.21 = (f32[5,32,128]{2,1,0:T(8,128)S(1)}, f32[5,32,128]{2,1,0:T(8,128)}, u32[]{:S(2)}, u32[]{:S(2)}) collective-permute-start(f32[5,32,128]{2,1,0:T(8,128)S(1)} %get-tuple-element.450), channel_id=1, source_target_pairs={{128,75},{3,192},{132,79},{7,196},{136,83},{11,200},{140,87},{15,2... | collective-permute-start | bytes 245768 | tf_op jit(solution)/shard_map/cond/branch_7_fun/ppermute | solution.py:403
  51.0 22.1 %copy-start.2 = (f32[1,5,5,8,32,128]{5,4,3,2,1,0:T(8,128)S(1)}, f32[1,5,5,8,32,128]{5,4,3,2,1,0:T(8,128)}, u32[]{:S(2)}) copy-start(f32[1,5,5,8,32,128]{5,4,3,2,1,0:T(8,128)} %refs_12_.1) | copy-start | bytes 9830404
  52.1 9.3 %collective-permute-start.52 = (f32[10,32,128]{2,1,0:T(8,128)S(1)}, f32[10,32,128]{2,1,0:T(8,128)S(1)}, u32[]{:S(2)}, u32[]{:S(2)}) collective-permute-start(f32[10,32,128]{2,1,0:T(8,128)S(1)} %get-tuple-element.605), channel_id=1, source_target_pairs={{0,1},{3,2},{4,5},{7,6},{8,9},{11,10},{12,13},{15,14},{16,17},{19,... | collective-permute-start | bytes 491528 | tf_op jit(solution)/shard_map/ppermute | solution.py:447
  53.5 7.9 %collective-permute-start.53 = (f32[5,32,128]{2,1,0:T(8,128)S(1)}, f32[5,32,128]{2,1,0:T(8,128)S(1)}, u32[]{:S(2)}, u32[]{:S(2)}) collective-permute-start(f32[5,32,128]{2,1,0:T(8,128)S(1)} %get-tuple-element.606.refs_8_), channel_id=1, source_target_pairs={{0,2},{4,6},{8,10},{12,14},{16,18},{20,22},{24,26},{28,30},{32,34}... | collective-permute-start | bytes 245768 | tf_op jit(solution)/shard_map/ppermute | solution.py:446
  62.7 10.4 %collective-permute-start.54 = (f32[10,32,128]{2,1,0:T(8,128)S(1)}, f32[10,32,128]{2,1,0:T(8,128)S(1)}, u32[]{:S(2)}, u32[]{:S(2)}) collective-permute-start(f32[10,32,128]{2,1,0:T(8,128)S(1)} %get-tuple-element.609), channel_id=1, source_target_pairs={{2,3},{6,7},{10,11},{14,15},{18,19},{22,23},{26,27},{30,31},{34,35... | collective-permute-start | bytes 491528 | tf_op jit(solution)/shard_map/ppermute | solution.py:456
  63.4 2.0 %collective-permute-start.56 = (f32[5,32,128]{2,1,0:T(8,128)S(1)}, f32[5,32,128]{2,1,0:T(8,128)S(1)}, u32[]{:S(2)}, u32[]{:S(2)}) collective-permute-start(f32[5,32,128]{2,1,0:T(8,128)S(1)} %get-tuple-element.610), channel_id=1, source_target_pairs={{2,1},{6,5},{10,9},{14,13},{18,17},{22,21},{26,25},{30,29},{34,33}... | collective-permute-start | bytes 245768 | tf_op jit(solution)/shard_map/ppermute | solution.py:455
  64.1 9.0 %collective-permute-start.55 = (f32[5,32,128]{2,1,0:T(8,128)S(1)}, f32[5,32,128]{2,1,0:T(8,128)S(1)}, u32[]{:S(2)}, u32[]{:S(2)}) collective-permute-start(f32[5,32,128]{2,1,0:T(8,128)S(1)} %get-tuple-element.610), channel_id=1, source_target_pairs={{2,0},{6,4},{10,8},{14,12},{18,16},{22,20},{26,24},{30,28},{34,32}... | collective-permute-start | bytes 245768 | tf_op jit(solution)/shard_map/ppermute | solution.py:454

commit v2 on v1

v2 whole, which is shorter than its diff:
```python
import jax
import jax.numpy as jnp
from jax import lax
from jax.experimental import pallas as pl
from jax.experimental.pallas import tpu as pltpu
from jax.sharding import PartitionSpec as P

F32 = jnp.float32
V = 5
AXES = ("row", "sector", "slab")
VMEM_BYTES = 14 * 1024 * 1024


def matvec(mat, vec):
    out = []
    for i in range(V):
        acc = mat(i, 0) * vec[0]
        for j in range(1, V):
            acc = acc + mat(i, j) * vec[j]
        out.append(acc)
    return out


def stacked(ref, base):
    return lambda i, j: ref[base + V * i + j]


def planes_of(ref, base):
    return [ref[base + v] for v in range(V)]


def put(ref, base, values):
    for v in range(V):
        ref[base + v] = values[v]


def sliding(owner, columns, total):
    lead = owner[0]

    def lower(i, best):
        return jnp.minimum(best, ((owner[i] - lead + total // 2) & (total - 1)) - total // 2)

    return (lead + lax.fori_loop(1, columns, lower, jnp.int32(0), unroll=True)) & (total - 1)


def pack_kernel(planes, columns, owner, state, towards_low, interface, towards_high, lowest, pair):
    row = lax.axis_index("row")
    face = jnp.where(row == 0, planes - 1, 0)
    pair[0] = sliding(owner, columns, owner.shape[0]) >> ((2 * columns).bit_length() - 1)
    for v in range(V):
        plane = state[0, v, face]
        interface[v] = plane
        towards_low[v, planes:] = plane
        lowest[v] = state[0, v, 0]
        for x in range(planes):
            towards_low[v, x : x + 1] = state[0, v, x, 0:1]
            towards_high[v, x : x + 1] = state[0, v, x, columns - 1 : columns]


def window_kernel(planes, columns, sectors, owner, own, next_one, next_two, message, table, landing):
    row = lax.axis_index("row")
    sector = lax.axis_index("sector")
    total = sectors * columns
    for v in range(V):
        table[v, 0:columns] = own[v]
        table[v, columns : 2 * columns] = next_one[v, planes:]
        table[v, 2 * columns :] = next_two[v]
    turn = sliding(owner, columns, total) >> (columns.bit_length() - 1)
    even = turn & -2

    @pl.when(row == 1)
    def _():
        facing = (sector - even) & (sectors - 1)

        def step(i, carry):
            at = (owner[facing * columns + i] - sector * columns) & (total - 1)
            at = jnp.minimum(at, 3 * columns - 1)
            for v in range(V):
                landing[v, pl.ds(i, 1)] = table[v, pl.ds(at, 1)]
            return carry

        lax.fori_loop(0, columns, step, 0, unroll=8)

    @pl.when(row == 0)
    def _():
        facing = (sector + even + 2) & (sectors - 1)
        first = (1 - (turn - even)) * columns

        def step(i, carry):
            at = first + i
            column = owner[(sector * columns + at) & (total - 1)]
            to = jnp.minimum((column - facing * columns) & (total - 1), columns)
            for v in range(V):
                landing[v, pl.ds(to, 1)] = table[v, pl.ds(at, 1)]
            return carry

        lax.fori_loop(0, 2 * columns, step, 0, unroll=8)

    for v in range(V):
        message[v] = landing[v, 0:columns]


def matrix_kernel(planes, axial, inverse, up, right, left, side, splat, product, prefix):
    row = lax.axis_index("row")
    slab = lax.axis_index("slab")
    strip = (8, 128)

    @pl.when(pl.program_id(0) == 0)
    def _():
        for i in range(V):
            for j in range(V):
                splat[V * i + j] = jnp.full(strip, 0.5 * axial[0, i, j], F32)

    def flux_times(x):
        for i in range(V):
            entries = [inverse[0, i, k, x] for k in range(V)]
            for j in range(V):
                acc = entries[0] * splat[j]
                for k in range(1, V):
                    acc = acc + entries[k] * splat[V * k + j]
                product[x, V * i + j] = acc

    def forward(x, carry):
        flux_times(x)
        for j in range(V):
            column = [prefix[x - 1, V * i + j] for i in range(V)]
            put_column(prefix.at[x], j, matvec(stacked(product.at[x], 0), column))
        return carry

    flux_times(0)
    for k in range(V * V):
        prefix[0, k] = product[0, k]
    lax.fori_loop(1, planes, forward, 0)
    for k in range(V * V):
        up[2 * V + k] = prefix[planes - 1, k]

    @pl.when(slab > 0)
    def _():
        for j in range(V):
            column = [prefix[planes - 2, V * i + j] for i in range(V)]
            put_column(left, j, matvec(stacked(product.at[planes - 1], 0), column))

        def backward(step, carry):
            x = planes - 1 - step
            for j in range(V):
                column = [prefix[x - 1, V * i + j] - left[V * i + j] for i in range(V)]
                put_column(left, j, matvec(stacked(product.at[x], 0), column))
            return carry

        lax.fori_loop(1, planes - 1, backward, 0)
        for j in range(V):
            column = [float(i == j) - left[V * i + j] for i in range(V)]
            put_column(left, j, matvec(stacked(product.at[0], 0), column))
        for k in range(V * V):
            side[k] = left[k]

    @pl.when((slab == 1) | (slab == 2) | ((slab == 3) & (row == 0)))
    def _():
        for k in range(V * V):
            right[k] = product[planes - 1, k]

        def backward(step, carry):
            x = planes - 1 - step
            for j in range(V):
                column = [right[V * i + j] for i in range(V)]
                put_column(right, j, matvec(stacked(product.at[x], 0), column))
            return carry

        lax.fori_loop(1, planes, backward, 0)

    @pl.when(slab == 1)
    def _():
        for k in range(V * V):
            side[k] = right[k]


def put_column(ref, j, values):
    for i in range(V):
        ref[V * i + j] = values[i]


def residual_kernel(
    planes, columns, axial, cross, state, source, inverse, from_high, from_low, above, up_in,
    residual, up, down, wide, forward,
):
    step = pl.program_id(0)

    @pl.when(step == 0)
    def _():
        for v in range(V):
            for x in range(planes):
                wide[v, x, 8 : 8 + columns] = state[0, v, x]
                wide[v, x, 7:8] = from_low[v, x : x + 1]
                wide[v, x, 8 + columns : 9 + columns] = from_high[v, x : x + 1]

    middle = pl.multiple_of(step * 8 + 8, 8)
    low = pl.multiple_of(step * 8, 8)
    high = pl.multiple_of(step * 8 + 16, 8)
    rows = lax.broadcasted_iota(jnp.int32, (8, 128), 0)
    lanes = lax.broadcasted_iota(jnp.int32, (8, 128), 1)
    ja = lambda i, j: 0.5 * axial[0, i, j]
    jb = lambda i, j: 0.5 * cross[0, 0, i, j]
    jr = lambda i, j: 0.5 * cross[0, 1, i, j]
    previous = None
    for x in range(planes):
        along, around, outward = [], [], []
        for v in range(V):
            here = wide[v, x, pl.ds(middle, 8)]
            nearer = wide[v, x + 1, pl.ds(middle, 8)] if x + 1 < planes else above[v]
            along.append(nearer - wide[v, x - 1, pl.ds(middle, 8)] if x else nearer)
            plus = jnp.where(rows == 0, wide[v, x, pl.ds(high, 8)], here)
            minus = jnp.where(rows == 7, wide[v, x, pl.ds(low, 8)], here)
            around.append(pltpu.roll(plus, 7, 0) - pltpu.roll(minus, 1, 0))
            outward.append(
                jnp.where(lanes == 127, 0.0, pltpu.roll(here, 127, 1))
                - jnp.where(lanes == 0, 0.0, pltpu.roll(here, 1, 1))
            )
        one, two, three = matvec(ja, along), matvec(jb, around), matvec(jr, outward)
        values = [source[0, v, x] - (one[v] + two[v] + three[v]) for v in range(V)]
        for v in range(V):
            residual[v, x] = values[v]
        if previous is not None:
            carried = matvec(ja, previous)
            values = [values[v] + carried[v] for v in range(V)]
        previous = matvec(lambda i, j, x=x: inverse[0, i, j, x], values)
        for v in range(V):
            forward[v, x] = previous[v]
    for v in range(V):
        last = wide[v, planes - 1, pl.ds(middle, 8)]
        up[v] = previous[v] + last
        up[V + v] = last
    for x in range(planes - 2, -1, -1):
        carried = matvec(lambda i, j, x=x: inverse[0, i, j, x], matvec(ja, previous))
        previous = [forward[v, x] - carried[v] for v in range(V)]
    for v in range(V):
        down[v] = previous[v]


def first_kernel(ghost, up, down, right, entry, message):
    slab = lax.axis_index("slab")
    for v in range(V):
        message[V + v] = up[V + v]

    @pl.when(slab == 0)
    def _():
        moved = matvec(stacked(up, 2 * V), planes_of(ghost, 0))
        for v in range(V):
            total = up[v] + moved[v]
            entry[v] = total
            message[v] = total

    @pl.when(slab == 3)
    def _():
        moved = matvec(stacked(right, 0), planes_of(ghost, 0))
        for v in range(V):
            message[v] = jnp.where(lax.axis_index("row") == 0, down[v] + moved[v], down[v])


def middle_kernel(
    came, came_side, up_other, left_other, up, down, right, left, lower, message, inflow, under, beyond,
):
    slab = lax.axis_index("slab")

    @pl.when(slab == 1)
    def _():
        moved = matvec(stacked(left, 0), planes_of(came_side, 0))
        put(lower, 0, [down[v] + moved[v] for v in range(V)])

    @pl.when(slab == 2)
    def _():
        moved = matvec(stacked(up_other, 2 * V), planes_of(came, 0))
        second = [up_other[v] + moved[v] for v in range(V)]
        moved = matvec(stacked(up, 2 * V), second)
        third = [up[v] + moved[v] for v in range(V)]
        moved = matvec(stacked(left_other, 0), third)
        top = [came_side[v] + moved[v] for v in range(V)]
        moved = matvec(stacked(left, 0), second)
        again = matvec(stacked(right, 0), top)
        put(lower, 0, [down[v] + moved[v] + again[v] for v in range(V)])
        put(message, 0, third)
        put(message, V, planes_of(up, V))
        put(inflow, 0, second)
        put(under, 0, planes_of(up_other, V))
        put(beyond, 0, top)


def last_kernel(
    planes, axial, ghost, came_side, to_third, to_zero, to_lower, second, under_second, top,
    right_other, partial, inverse, state, residual, new_state, forward, inflow, beyond, under,
):
    row = lax.axis_index("row")
    slab = lax.axis_index("slab")
    splats = [jnp.full((8, 128), 0.5 * axial[0, k // V, k % V], F32) for k in range(V * V)]
    ja = lambda i, j: splats[V * i + j]
    has_top = jnp.where((row == 0) & (slab == 3), 1.0, 0.0)

    @pl.when(slab == 0)
    def _():
        inflow[...] = ghost[...]
        under[...] = ghost[...]

    @pl.when(slab == 1)
    def _():
        inflow[...] = came_side[0:V]
        under[...] = came_side[V:]
        beyond[...] = to_lower[...]

    @pl.when(slab == 2)
    def _():
        inflow[...] = second[...]
        under[...] = under_second[...]
        beyond[...] = top[...]

    @pl.when(slab == 3)
    def _():
        inflow[...] = to_third[0:V]
        under[...] = to_third[V:]
        beyond[...] = jnp.zeros_like(beyond)

    def one_strip(step, carry):
        at = pl.ds(pl.multiple_of(step * 8, 8), 8)

        @pl.when(slab == 0)
        def _():
            came = [to_zero[v, at] for v in range(V)]
            moved = matvec(lambda i, j: right_other[V * i + j, at], came)
            for v in range(V):
                beyond[v, at] = to_lower[v, at] + moved[v]

        previous = [inflow[v, at] for v in range(V)]
        for x in range(planes):
            values = [partial[v, x, at] for v in range(V)]
            if x == planes - 1:
                top_part = matvec(ja, [ghost[v, at] * has_top for v in range(V)])
                values = [values[v] - top_part[v] for v in range(V)]
            if x == 0:
                bottom = matvec(ja, [under[v, at] for v in range(V)])
                for v in range(V):
                    residual[0, v, x, at] = values[v] + bottom[v]
            else:
                for v in range(V):
                    residual[0, v, x, at] = values[v]
            carried = matvec(ja, previous)
            values = [values[v] + carried[v] for v in range(V)]
            previous = matvec(lambda i, j: inverse[0, i, j, x, at], values)
            for v in range(V):
                forward[v, x] = previous[v]
        following = [beyond[v, at] for v in range(V)]
        for x in range(planes - 1, -1, -1):
            carried = matvec(lambda i, j: inverse[0, i, j, x, at], matvec(ja, following))
            following = [forward[v, x] - carried[v] for v in range(V)]
            for v in range(V):
                new_state[0, v, x, at] = state[0, v, x, at] + following[v]
        return carry

    lax.fori_loop(0, state.shape[3] // 8, one_strip, 0)


def sds(*shape):
    return jax.ShapeDtypeStruct(shape, F32)


def full(shape):
    return pl.BlockSpec(shape, lambda *_: (0,) * len(shape))


def strip(lead):
    return pl.BlockSpec((lead, 8, 128), lambda i: (0, i, 0))


SCALARS = pl.BlockSpec(memory_space=pltpu.SMEM)
WHOLE = pl.BlockSpec(memory_space=pltpu.VMEM)


def params(**more):
    return pltpu.CompilerParams(vmem_limit_bytes=VMEM_BYTES, **more)


def cost(amount):
    return pl.CostEstimate(flops=amount, bytes_accessed=amount // 8, transcendentals=0)


def per_device(state, source, diag_inverse, jac_axial, jac_cross, owner):
    planes, columns, radial = state.shape[2:]
    sectors = lax.axis_size("sector")
    slabs = lax.axis_size("slab")
    strips = columns // 8
    plane = (V, columns, radial)
    cells = pl.BlockSpec((1, V, planes, 8, radial), lambda i: (0, 0, 0, i, 0))
    blocks = pl.BlockSpec((1, V, V, planes, 8, radial), lambda i: (0, 0, 0, 0, i, 0))
    inner = pl.BlockSpec((V, planes, 8, radial), lambda i: (0, 0, i, 0))
    size = slabs * sectors

    def device(row, sector, slab):
        return row * size + sector % sectors * slabs + slab

    def import_pairs(even):
        pairs = []
        for j in range(sectors):
            pairs.append((device(1, j, 0), device(0, j - even, slabs - 1)))
            pairs.append((device(0, j, slabs - 1), device(1, j + even + 2, 0)))
        return pairs

    two_down = []
    for j in range(sectors):
        two_down.append((device(0, j, slabs - 1), device(0, j - 2, slabs - 1)))
        two_down.append((device(1, j, 0), device(1, j - 2, 0)))

    total = sectors * columns
    assert total & (total - 1) == 0 and columns & (columns - 1) == 0
    towards_low, interface, towards_high, lowest, pair = pl.pallas_call(
        lambda *refs: pack_kernel(planes, columns, *refs),
        in_specs=[SCALARS, WHOLE],
        out_specs=[WHOLE] * 4 + [SCALARS],
        out_shape=(
            sds(V, planes + columns, radial), sds(*plane), sds(V, planes, radial), sds(*plane),
            jax.ShapeDtypeStruct((1,), jnp.int32),
        ),
        compiler_params=params(),
        name="pack",
    )(owner, state)
    above = lax.ppermute(lowest, "slab", [(k, k - 1) for k in range(1, slabs)])
    from_low = lax.ppermute(towards_high, "sector", [(j, (j + 1) % sectors) for j in range(sectors)])
    from_second = lax.ppermute(interface, AXES, two_down)
    from_high = lax.ppermute(towards_low, "sector", [(j, (j - 1) % sectors) for j in range(sectors)])

    message = pl.pallas_call(
        lambda *refs: window_kernel(planes, columns, sectors, *refs),
        in_specs=[SCALARS] + [WHOLE] * 3,
        out_shape=sds(*plane),
        scratch_shapes=[
            pltpu.VMEM((V, 3 * columns, radial), F32),
            pltpu.VMEM((V, columns + 8, radial), F32),
        ],
        compiler_params=params(),
        name="window",
    )(owner, interface, from_high, from_second)

    square = sds(V * V, columns, radial)

    def exchange(even, message, from_low, above, from_high):
        ghost = lax.ppermute(message, AXES, import_pairs(even))
        up, right, left, side = pl.pallas_call(
            lambda *refs: matrix_kernel(planes, *refs),
            grid=(strips,),
            in_specs=[SCALARS, blocks],
            out_specs=(strip(2 * V + V * V), strip(V * V), strip(V * V), strip(V * V)),
            out_shape=(sds(2 * V + V * V, columns, radial), square, square, square),
            scratch_shapes=[
                pltpu.VMEM((V * V, 8, radial), F32),
                pltpu.VMEM((planes, V * V, 8, radial), F32),
                pltpu.VMEM((planes, V * V, 8, radial), F32),
            ],
            compiler_params=params(),
            cost_estimate=cost(80_000_000),
            name="matrices",
        )(jac_axial, diag_inverse)
        partial, up, down = pl.pallas_call(
            lambda *refs: residual_kernel(planes, columns, *refs),
            grid=(strips,),
            in_specs=[
                SCALARS, SCALARS, full(state.shape), cells, blocks,
                full(towards_low.shape), full(towards_high.shape), strip(V),
                pl.BlockSpec(memory_space=pl.ANY),
            ],
            out_specs=(inner, strip(2 * V), strip(V)),
            out_shape=(sds(V, planes, columns, radial), up, sds(*plane)),
            input_output_aliases={8: 1},
            scratch_shapes=[
                pltpu.VMEM((V, planes, columns + 16, radial), F32),
                pltpu.VMEM((V, planes, 8, radial), F32),
            ],
            compiler_params=params(),
            cost_estimate=cost(40_000_000),
            name="residual",
        )(jac_axial, jac_cross, state, source, diag_inverse, from_high, from_low, above, up)
        return ghost, partial, up, down, right, left, side

    ghost, partial, up, down, right, left, side = lax.switch(
        pair[0],
        [lambda *args, e=e: exchange(2 * e, *args) for e in range(sectors // 2)],
        message, from_low, above, from_high,
    )
    up_other = lax.ppermute(up, "slab", [(1, 2)])
    side_other = lax.ppermute(side, "slab", [(1, 0), (3, 2)])
    entry, side_message = pl.pallas_call(
        first_kernel,
        out_shape=(sds(*plane), sds(2 * V, columns, radial)),
        compiler_params=params(),
        name="first",
    )(ghost, up, down, right)
    came_side = lax.ppermute(side_message, "slab", [(0, 1), (3, 2)])
    came = lax.ppermute(entry, "slab", [(0, 2)])
    lower, onward, second, under, top = pl.pallas_call(
        middle_kernel,
        out_shape=(sds(*plane), sds(2 * V, columns, radial), sds(*plane), sds(*plane), sds(*plane)),
        compiler_params=params(),
        name="middle",
    )(came, came_side, up_other, side_other, up, down, right, left)
    to_lower = lax.ppermute(lower, "slab", [(2, 1), (1, 0)])
    to_third = lax.ppermute(onward, "slab", [(2, 3)])
    to_zero = lax.ppermute(lower, "slab", [(2, 0)])

    residual, new_state = pl.pallas_call(
        lambda *refs: last_kernel(planes, *refs),
        in_specs=[SCALARS] + [WHOLE] * 12,
        out_shape=(sds(*state.shape), sds(*state.shape)),
        scratch_shapes=[pltpu.VMEM((V, planes, 8, radial), F32)] + [pltpu.VMEM(plane, F32)] * 3,
        compiler_params=params(),
        name="last",
    )(
        jac_axial, ghost, came_side, to_third, to_zero, to_lower, second, under, top,
        side_other, partial, diag_inverse, state,
    )
    return residual, new_state


def solution(mesh):
    return jax.shard_map(
        per_device,
        mesh=mesh,
        in_specs=(
            P("row", None, "slab", "sector", None),
            P("row", None, "slab", "sector", None),
            P("row", None, None, "slab", "sector", None),
            P("row", None, None),
            P("row", None, None, None),
            P(),
        ),
        out_specs=(P("row", None, "slab", "sector", None), P("row", None, "slab", "sector", None)),
        check_vma=False,
    )
```

time: 77.9 us -> 66.4 us (0.85)
  the two profiles are of different devices: /device:TPU:0 before, /device:TPU:2 now
where the time goes in v2:
time: 66.4 us; the launch traced here: 65.8 us
  starting transfers between devices  23.8 us (36%)
  Pallas kernels  19.7 us (30%)
  waiting for transfers between devices  18.8 us (28%)
  local copies, waits for them, and re-layouts  2.07 us (3%)
  between operations  1.46 us (2%)
    ppermute x1, starting transfers between devices, per_device(): lax.ppermute(towards_low, 'sector', [(j, (j - 1) % sectors) for j in rang...  8.38 us
    ppermute x1, waiting for transfers between devices, per_device(): came_side = lax.ppermute(side_message, 'slab', [(0, 1), (3, 2)])  6.87 us
    pallas_call x1, Pallas kernels, exchange(): pl.pallas_call(lambda *refs: matrix_kernel(planes, *refs), grid=(strips,)...  6.85 us
    ppermute x1, waiting for transfers between devices, per_device(): lax.ppermute(towards_high, 'sector', [(j, (j + 1) % sectors) for j in ran...  5.59 us
    ppermute x1, waiting for transfers between devices, per_device(): to_lower = lax.ppermute(lower, 'slab', [(2, 1), (1, 0)])  4.84 us
    pallas_call x1, Pallas kernels, exchange(): pl.pallas_call(lambda *refs: residual_kernel(planes, columns, *refs), gri...  4.63 us
    ppermute x1, starting transfers between devices, per_device(): up_other = lax.ppermute(up, 'slab', [(1, 2)])  3.56 us
    pallas_call x1, Pallas kernels, per_device(): pl.pallas_call(lambda *refs: last_kernel(planes, *refs), in_specs=[SCALAR...  3.34 us
  transfers between devices with their start and end apart: 12, of which 4 were waited for; matrix products, arithmetic and copies ran while one was open for 2% of the time, Pallas kernels for 21%

profile of v2, /device:TPU:2, one launch (start us, length us, event | category | flops | bytes accessed | tf_op | source)
XLA Modules:
  0.0 65.8 jit_solution(15364357931441288274)
XLA Ops:
  0.6 0.0 copy-start
  0.6 0.7 %copy-done = s32[1024]{0:T(1024)S(1)} copy-done((s32[1024]{0:T(1024)S(1)}, s32[1024]{0:T(1024)}, u32[]{:S(2)}) %copy-start) | copy-done | bytes 4120
  1.3 1.7 %pack.1 = (f32[5,40,128]{2,1,0:T(8,128)S(1)}, f32[5,32,128]{2,1,0:T(8,128)S(1)}, f32[5,8,128]{2,1,0:T(8,128)S(1)}, f32[5,32,128]{2,1,0:T(8,128)S(1)}, s32[1]{0:T(128)}) custom-call(s32[1024]{0:T(1024)S(1)} %copy-done, f32[1,5,8,32,128]{4,3,2,1,0:T(8,128)} %refs_12_.1), custom_call_target="tpu_custom_call" | custom-call | tf_op jit(solution)/shard_map/pack/pallas_call | solution.py:411
  3.0 8.4 %collective-permute-start.16 = (f32[5,40,128]{2,1,0:T(8,128)S(1)}, f32[5,40,128]{2,1,0:T(8,128)S(1)}, u32[]{:S(2)}, u32[]{:S(2)}) collective-permute-start(f32[5,40,128]{2,1,0:T(8,128)S(1)} %get-tuple-element.567), channel_id=1, source_target_pairs={{0,124},{4,0},{8,4},{12,8},{16,12},{20,16},{24,20},{28,24},{32,28}... | collective-permute-start | bytes 307208 | tf_op jit(solution)/shard_map/ppermute | solution.py:425
  11.4 0.7 collective-permute-start.17
  12.1 2.4 %collective-permute-start.19 = (f32[5,32,128]{2,1,0:T(8,128)S(1)}, f32[5,32,128]{2,1,0:T(8,128)S(1)}, u32[]{:S(2)}, u32[]{:S(2)}) collective-permute-start(f32[5,32,128]{2,1,0:T(8,128)S(1)} %get-tuple-element.569), channel_id=1, source_target_pairs={{1,0},{2,1},{3,2},{5,4},{6,5},{7,6},{9,8},{10,9},{11,10},{13,12},{... | collective-permute-start | bytes 245768 | tf_op jit(solution)/shard_map/ppermute | solution.py:422
  14.5 0.1 collective-permute-start.18
  15.3 0.0 collective-permute-done.17.refs_3_
  15.3 0.0 collective-permute-done.16.refs_2_
  15.3 0.9 %window.1 = f32[5,32,128]{2,1,0:T(8,128)S(1)} custom-call(s32[1024]{0:T(1024)S(1)} %copy-done, f32[5,32,128]{2,1,0:T(8,128)S(1)} %get-tuple-element.566.refs_1_, f32[5,40,128]{2,1,0:T(8,128)S(1)} %collective-permute-done.16.refs_2_, f32[5,32,128]{2,1,0:T(8,128)S(1)} %collective-permute-done.17.refs_3_), custom_call_target="tpu_custom_call" | custom-call | tf_op jit(solution)/shard_map/window/pallas_call | solution.py:427
  16.2 5.6 %collective-permute-done.18 = f32[5,8,128]{2,1,0:T(8,128)S(1)} collective-permute-done((f32[5,8,128]{2,1,0:T(8,128)S(1)}, f32[5,8,128]{2,1,0:T(8,128)S(1)}, u32[]{:S(2)}, u32[]{:S(2)}) %collective-permute-start.18) | collective-permute-done | bytes 20512 | tf_op jit(solution)/shard_map/ppermute | solution.py:423
  21.8 0.0 collective-permute-done.19
  21.8 14.3 %conditional.1 = (f32[5,32,128]{2,1,0:T(8,128)}, f32[5,8,32,128]{3,2,1,0:T(8,128)S(1)}, f32[35,32,128]{2,1,0:T(8,128)}, f32[5,32,128]{2,1,0:T(8,128)S(1)}, f32[2...) conditional(s32[]{:T(128)} %bitcast, ...), branch_computations={%region_0.0_spmd, %region_1.0_spmd, %region_2.0_spmd, %region_3.0_... | conditional | flops 120000000 | bytes 28435604 | solution.py:479
  21.8 0.0 copy-start.4
  21.8 1.4 %collective-permute-start.2 = (f32[5,32,128]{2,1,0:T(8,128)S(1)}, f32[5,32,128]{2,1,0:T(8,128)}, u32[]{:S(2)}, u32[]{:S(2)}) collective-permute-start(f32[5,32,128]{2,1,0:T(8,128)S(1)} %get-tuple-element.320), channel_id=1, source_target_pairs={{128,115},{3,152},{132,119},{7,156},{136,123},{11,160},{140,127},{... | collective-permute-start | bytes 245768 | tf_op jit(solution)/shard_map/cond/branch_2_fun/ppermute | solution.py:442
  23.2 0.7 %copy.28.refs_0_ = f32[1,5,5]{2,1,0:T(8,128)S(1)} copy(f32[1,5,5]{2,0,1:T(1,128)} %get-tuple-element.603) | data formatting | bytes 200 | tf_op jit(solution)/shard_map
  23.9 0.7 %copy.29.refs_1_ = f32[1,2,5,5]{3,2,1,0:T(8,128)S(1)} copy(f32[1,2,5,5]{3,1,2,0:T(2,128)} %get-tuple-element.605) | data formatting | bytes 400 | tf_op jit(solution)/shard_map
  24.6 6.9 %matrices.18 = (f32[35,32,128]{2,1,0:T(8,128)}, f32[25,32,128]{2,1,0:T(8,128)S(1)}, f32[25,32,128]{2,1,0:T(8,128)S(1)}, f32[25,32,128]{2,1,0:T(8,128)S(1)}) custom-call(f32[1,5,5]{2,1,0:T(8,128)S(1)} %copy.28.refs_0_, f32[1,5,5,8,32,128]{5,4,3,2,1,0:T(8,128)} %get-tuple-element.325.refs_1_.refs_4_), custom_call_target="tpu_custom_call" | custom-call | flops 80000000 | bytes 10000000 | tf_op jit(solution)/shard_map/cond/branch_2_fun/matrices/pallas_call | solution.py:443
  31.5 0.0 copy-done.4
  31.5 4.6 %residual.18 = (f32[5,8,32,128]{3,2,1,0:T(8,128)S(1)}, f32[35,32,128]{2,1,0:T(8,128)}, f32[5,32,128]{2,1,0:T(8,128)S(1)}) custom-call(f32[1,5,5]{2,1,0:T(8,128)S(1)} %copy.28.refs_0_, f32[1,2,5,5]{3,2,1,0:T(8,128)S(1)} %copy.29.refs_1_, f32[1,5,8,32,128]{4,3,2,1,0:T(8,128)} %get-tuple-element.323.refs_2_, ...), custom_call_target="tpu_custom_call", output_to_operand_aliasing={{1}: (8, {})} | custom-call | flops 40000000 | bytes 5000000 | tf_op jit(solution)/shard_map/cond/branch_2_fun/residual/pallas_call | solution.py:458
  36.1 0.0 collective-permute-done.2
  36.1 0.0 copy-start.18
  36.1 0.0 copy-start.1
  36.1 3.6 %collective-permute-start.22 = (f32[35,32,128]{2,1,0:T(8,128)}, f32[35,32,128]{2,1,0:T(8,128)S(1)}, u32[]{:S(2)}, u32[]{:S(2)}) collective-permute-start(f32[35,32,128]{2,1,0:T(8,128)} %get-tuple-element.571.up), channel_id=1, source_target_pairs={{1,2},{5,6},{9,10},{13,14},{17,18},{21,22},{25,26},{29,30},{33,34}... | collective-permute-start | bytes 1720328 | tf_op jit(solution)/shard_map/ppermute | solution.py:484
  39.7 1.3 %collective-permute-start.23 = (f32[25,32,128]{2,1,0:T(8,128)S(1)}, f32[25,32,128]{2,1,0:T(8,128)S(1)}, u32[]{:S(2)}, u32[]{:S(2)}) collective-permute-start(f32[25,32,128]{2,1,0:T(8,128)S(1)} %get-tuple-element.576), channel_id=1, source_target_pairs={{1,0},{3,2},{5,4},{7,6},{9,8},{11,10},{13,12},{15,14},{17,16},{19,... | collective-permute-start | bytes 1228808 | tf_op jit(solution)/shard_map/ppermute | solution.py:485
  41.0 1.1 %first.1 = (f32[5,32,128]{2,1,0:T(8,128)S(1)}, f32[10,32,128]{2,1,0:T(8,128)S(1)}) custom-call(f32[5,32,128]{2,1,0:T(8,128)} %get-tuple-element.570.ghost.refs_1_, f32[35,32,128]{2,1,0:T(8,128)} %get-tuple-element.571.up, f32[5,32,128]{2,1,0:T(8,128)S(1)} %get-tuple-element.572.down, f32[25,32,128]{2,1,0:T(8,128)S(1)} %get-tuple-element.573.right), custom_call_target="tpu_custom_call" | custom-call | tf_op jit(solution)/shard_map/first/pallas_call | solution.py:486
  42.1 1.3 %collective-permute-start.20 = (f32[10,32,128]{2,1,0:T(8,128)S(1)}, f32[10,32,128]{2,1,0:T(8,128)S(1)}, u32[]{:S(2)}, u32[]{:S(2)}) collective-permute-start(f32[10,32,128]{2,1,0:T(8,128)S(1)} %get-tuple-element.574), channel_id=1, source_target_pairs={{0,1},{3,2},{4,5},{7,6},{8,9},{11,10},{12,13},{15,14},{16,17},{19,... | collective-permute-start | bytes 491528 | tf_op jit(solution)/shard_map/ppermute | solution.py:492
  43.4 0.7 %collective-permute-start.21 = (f32[5,32,128]{2,1,0:T(8,128)S(1)}, f32[5,32,128]{2,1,0:T(8,128)S(1)}, u32[]{:S(2)}, u32[]{:S(2)}) collective-permute-start(f32[5,32,128]{2,1,0:T(8,128)S(1)} %get-tuple-element.575), channel_id=1, source_target_pairs={{0,2},{4,6},{8,10},{12,14},{16,18},{20,22},{24,26},{28,30},{32,34}... | collective-permute-start | bytes 245768 | tf_op jit(solution)/shard_map/ppermute | solution.py:493
  44.1 0.0 collective-permute-done.21.came
  44.1 6.9 %collective-permute-done.20.came_side.refs_2_ = f32[10,32,128]{2,1,0:T(8,128)S(1)} collective-permute-done((f32[10,32,128]{2,1,0:T(8,128)S(1)}, f32[10,32,128]{2,1,0:T(8,128)S(1)}, u32[]{:S(2)}, u32[]{:S(2)}) %collective-permute-start.20) | collective-permute-done | bytes 163872 | tf_op jit(solution)/shard_map/ppermute | solution.py:492
  51.0 0.0 collective-permute-done.23.left_other.refs_9_
  51.0 1.4 %collective-permute-done.22.up_other = f32[35,32,128]{2,1,0:T(8,128)S(1)} collective-permute-done((f32[35,32,128]{2,1,0:T(8,128)}, f32[35,32,128]{2,1,0:T(8,128)S(1)}, u32[]{:S(2)}, u32[]{:S(2)}) %collective-permute-start.22) | collective-permute-done | bytes 573472 | tf_op jit(solution)/shard_map/ppermute | solution.py:484
  52.4 1.1 %middle.1 = (f32[5,32,128]{2,1,0:T(8,128)S(1)}, f32[10,32,128]{2,1,0:T(8,128)S(1)}, f32[5,32,128]{2,1,0:T(8,128)S(1)}, f32[5,32,128]{2,1,0:T(8,128)S(1)}, f32[5,32,128]{2,1,0:T(8,128)S(1)}) custom-call(f32[5,32,128]{2,1,0:T(8,128)S(1)} %collective-permute-done.21.came, f32[10,32,128]{2,1,0:T(8,128)S(1)} %collective-permute-done.20.came_side.refs_2_, ...), custom_call_target="tpu_custom_call" | custom-call | tf_op jit(solution)/shard_map/middle/pallas_call | solution.py:494
  53.5 0.7 %collective-permute-start.24 = (f32[10,32,128]{2,1,0:T(8,128)S(1)}, f32[10,32,128]{2,1,0:T(8,128)S(1)}, u32[]{:S(2)}, u32[]{:S(2)}) collective-permute-start(f32[10,32,128]{2,1,0:T(8,128)S(1)} %get-tuple-element.578), channel_id=1, source_target_pairs={{2,3},{6,7},{10,11},{14,15},{18,19},{22,23},{26,27},{30,31},{34,35... | collective-permute-start | bytes 491528 | tf_op jit(solution)/shard_map/ppermute | solution.py:501
  54.2 0.7 %collective-permute-start.25 = (f32[5,32,128]{2,1,0:T(8,128)S(1)}, f32[5,32,128]{2,1,0:T(8,128)S(1)}, u32[]{:S(2)}, u32[]{:S(2)}) collective-permute-start(f32[5,32,128]{2,1,0:T(8,128)S(1)} %get-tuple-element.579), channel_id=1, source_target_pairs={{2,0},{6,4},{10,8},{14,12},{18,16},{22,20},{26,24},{30,28},{34,32}... | collective-permute-start | bytes 245768 | tf_op jit(solution)/shard_map/ppermute | solution.py:502
  54.9 2.7 %collective-permute-start.26 = (f32[5,32,128]{2,1,0:T(8,128)S(1)}, f32[5,32,128]{2,1,0:T(8,128)S(1)}, u32[]{:S(2)}, u32[]{:S(2)}) collective-permute-start(f32[5,32,128]{2,1,0:T(8,128)S(1)} %get-tuple-element.579), channel_id=1, source_target_pairs={{2,1},{1,0},{6,5},{5,4},{10,9},{9,8},{14,13},{13,12},{18,17},{17,1... | collective-permute-start | bytes 245768 | tf_op jit(solution)/shard_map/ppermute | solution.py:500
  57.6 0.0 copy-done.18
  57.6 0.0 collective-permute-done.25.refs_4_
  57.6 4.8 %collective-permute-done.26.refs_5_ = f32[5,32,128]{2,1,0:T(8,128)S(1)} collective-permute-done((f32[5,32,128]{2,1,0:T(8,128)S(1)}, f32[5,32,128]{2,1,0:T(8,128)S(1)}, u32[]{:S(2)}, u32[]{:S(2)}) %collective-permute-start.26) | collective-permute-done | bytes 81952 | tf_op jit(solution)/shard_map/ppermute | solution.py:500
  62.4 0.0 collective-permute-done.24.refs_3_
  62.4 0.0 copy-done.1
  62.4 3.3 %last.1 = (f32[1,5,8,32,128]{4,3,2,1,0:T(8,128)}, f32[1,5,8,32,128]{4,3,2,1,0:T(8,128)}) custom-call(f32[1,5,5]{2,1,0:T(8,128)S(1)} %copy.56.refs_0_, f32[5,32,128]{2,1,0:T(8,128)} %get-tuple-element.570.ghost.refs_1_, f32[10,32,128]{2,1,0:T(8,128)S(1)} %collective-permute-done.20.came_side.refs_2_, f32[10,32,128]{2,1,0:T(8,128)S(1)} %collective-permute-done.24.refs_3_, ...), custom_call_target="tpu_custom_call" | custom-call | tf_op jit(solution)/shard_map/last/pallas_call | solution.py:504
  (1 shorter events, 0.0 us)
Async XLA Ops:
  0.6 0.7 %copy-start = (s32[1024]{0:T(1024)S(1)}, s32[1024]{0:T(1024)}, u32[]{:S(2)}) copy-start(s32[1024]{0:T(1024)} %refs_0_.4) | copy-start | bytes 12292
  3.0 12.2 %collective-permute-start.16 = (f32[5,40,128]{2,1,0:T(8,128)S(1)}, f32[5,40,128]{2,1,0:T(8,128)S(1)}, u32[]{:S(2)}, u32[]{:S(2)}) collective-permute-start(f32[5,40,128]{2,1,0:T(8,128)S(1)} %get-tuple-element.567), channel_id=1, source_target_pairs={{0,124},{4,0},{8,4},{12,8},{16,12},{20,16},{24,20},{28,24},{32,28}... | collective-permute-start | bytes 307208 | tf_op jit(solution)/shard_map/ppermute | solution.py:425
  11.4 3.9 %collective-permute-start.17 = (f32[5,32,128]{2,1,0:T(8,128)S(1)}, f32[5,32,128]{2,1,0:T(8,128)S(1)}, u32[]{:S(2)}, u32[]{:S(2)}) collective-permute-start(f32[5,32,128]{2,1,0:T(8,128)S(1)} %get-tuple-element.566.refs_1_), channel_id=1, source_target_pairs={{3,123},{128,248},{7,127},{132,252},{11,3},{136,128},{15,7},{140,1... | collective-permute-start | bytes 245768 | tf_op jit(solution)/shard_map/ppermute | solution.py:424
  12.1 9.8 %collective-permute-start.19 = (f32[5,32,128]{2,1,0:T(8,128)S(1)}, f32[5,32,128]{2,1,0:T(8,128)S(1)}, u32[]{:S(2)}, u32[]{:S(2)}) collective-permute-start(f32[5,32,128]{2,1,0:T(8,128)S(1)} %get-tuple-element.569), channel_id=1, source_target_pairs={{1,0},{2,1},{3,2},{5,4},{6,5},{7,6},{9,8},{10,9},{11,10},{13,12},{... | collective-permute-start | bytes 245768 | tf_op jit(solution)/shard_map/ppermute | solution.py:422
  14.5 7.3 %collective-permute-start.18 = (f32[5,8,128]{2,1,0:T(8,128)S(1)}, f32[5,8,128]{2,1,0:T(8,128)S(1)}, u32[]{:S(2)}, u32[]{:S(2)}) collective-permute-start(f32[5,8,128]{2,1,0:T(8,128)S(1)} %get-tuple-element.568), channel_id=1, source_target_pairs={{0,4},{4,8},{8,12},{12,16},{16,20},{20,24},{24,28},{28,32},{32,36}... | collective-permute-start | bytes 61448 | tf_op jit(solution)/shard_map/ppermute | solution.py:423
  21.8 9.6 %copy-start.4 = (f32[1,5,5,8,32,128]{5,4,3,2,1,0:T(8,128)S(1)}, f32[1,5,5,8,32,128]{5,4,3,2,1,0:T(8,128)}, u32[]{:S(2)}) copy-start(f32[1,5,5,8,32,128]{5,4,3,2,1,0:T(8,128)} %get-tuple-element.325.refs_1_.refs_4_) | copy-start | bytes 9830404 | tf_op jit(solution)/shard_map/cond
  21.8 14.3 %collective-permute-start.2 = (f32[5,32,128]{2,1,0:T(8,128)S(1)}, f32[5,32,128]{2,1,0:T(8,128)}, u32[]{:S(2)}, u32[]{:S(2)}) collective-permute-start(f32[5,32,128]{2,1,0:T(8,128)S(1)} %get-tuple-element.320), channel_id=1, source_target_pairs={{128,115},{3,152},{132,119},{7,156},{136,123},{11,160},{140,127},{... | collective-permute-start | bytes 245768 | tf_op jit(solution)/shard_map/cond/branch_2_fun/ppermute | solution.py:442
  36.1 21.5 %copy-start.18 = (f32[1,5,5]{2,0,1:T(1,128)S(1)}, f32[1,5,5]{2,0,1:T(1,128)}, u32[]{:S(2)}) copy-start(f32[1,5,5]{2,0,1:T(1,128)} %param.25) | copy-start | bytes 304
  36.1 26.3 %copy-start.1 = (f32[1,5,5,8,32,128]{5,4,3,2,1,0:T(8,128)S(1)}, f32[1,5,5,8,32,128]{5,4,3,2,1,0:T(8,128)}, u32[]{:S(2)}) copy-start(f32[1,5,5,8,32,128]{5,4,3,2,1,0:T(8,128)} %refs_11_.1) | copy-start | bytes 9830404
  36.1 16.3 %collective-permute-start.22 = (f32[35,32,128]{2,1,0:T(8,128)}, f32[35,32,128]{2,1,0:T(8,128)S(1)}, u32[]{:S(2)}, u32[]{:S(2)}) collective-permute-start(f32[35,32,128]{2,1,0:T(8,128)} %get-tuple-element.571.up), channel_id=1, source_target_pairs={{1,2},{5,6},{9,10},{13,14},{17,18},{21,22},{25,26},{29,30},{33,34}... | collective-permute-start | bytes 1720328 | tf_op jit(solution)/shard_map/ppermute | solution.py:484
  39.7 11.3 %collective-permute-start.23 = (f32[25,32,128]{2,1,0:T(8,128)S(1)}, f32[25,32,128]{2,1,0:T(8,128)S(1)}, u32[]{:S(2)}, u32[]{:S(2)}) collective-permute-start(f32[25,32,128]{2,1,0:T(8,128)S(1)} %get-tuple-element.576), channel_id=1, source_target_pairs={{1,0},{3,2},{5,4},{7,6},{9,8},{11,10},{13,12},{15,14},{17,16},{19,... | collective-permute-start | bytes 1228808 | tf_op jit(solution)/shard_map/ppermute | solution.py:485
  42.1 8.8 %collective-permute-start.20 = (f32[10,32,128]{2,1,0:T(8,128)S(1)}, f32[10,32,128]{2,1,0:T(8,128)S(1)}, u32[]{:S(2)}, u32[]{:S(2)}) collective-permute-start(f32[10,32,128]{2,1,0:T(8,128)S(1)} %get-tuple-element.574), channel_id=1, source_target_pairs={{0,1},{3,2},{4,5},{7,6},{8,9},{11,10},{12,13},{15,14},{16,17},{19,... | collective-permute-start | bytes 491528 | tf_op jit(solution)/shard_map/ppermute | solution.py:492
  43.4 0.7 %collective-permute-start.21 = (f32[5,32,128]{2,1,0:T(8,128)S(1)}, f32[5,32,128]{2,1,0:T(8,128)S(1)}, u32[]{:S(2)}, u32[]{:S(2)}) collective-permute-start(f32[5,32,128]{2,1,0:T(8,128)S(1)} %get-tuple-element.575), channel_id=1, source_target_pairs={{0,2},{4,6},{8,10},{12,14},{16,18},{20,22},{24,26},{28,30},{32,34}... | collective-permute-start | bytes 245768 | tf_op jit(solution)/shard_map/ppermute | solution.py:493
  53.5 8.9 %collective-permute-start.24 = (f32[10,32,128]{2,1,0:T(8,128)S(1)}, f32[10,32,128]{2,1,0:T(8,128)S(1)}, u32[]{:S(2)}, u32[]{:S(2)}) collective-permute-start(f32[10,32,128]{2,1,0:T(8,128)S(1)} %get-tuple-element.578), channel_id=1, source_target_pairs={{2,3},{6,7},{10,11},{14,15},{18,19},{22,23},{26,27},{30,31},{34,35... | collective-permute-start | bytes 491528 | tf_op jit(solution)/shard_map/ppermute | solution.py:501
  54.2 3.4 %collective-permute-start.25 = (f32[5,32,128]{2,1,0:T(8,128)S(1)}, f32[5,32,128]{2,1,0:T(8,128)S(1)}, u32[]{:S(2)}, u32[]{:S(2)}) collective-permute-start(f32[5,32,128]{2,1,0:T(8,128)S(1)} %get-tuple-element.579), channel_id=1, source_target_pairs={{2,0},{6,4},{10,8},{14,12},{18,16},{22,20},{26,24},{30,28},{34,32}... | collective-permute-start | bytes 245768 | tf_op jit(solution)/shard_map/ppermute | solution.py:502
  54.9 7.5 %collective-permute-start.26 = (f32[5,32,128]{2,1,0:T(8,128)S(1)}, f32[5,32,128]{2,1,0:T(8,128)S(1)}, u32[]{:S(2)}, u32[]{:S(2)}) collective-permute-start(f32[5,32,128]{2,1,0:T(8,128)S(1)} %get-tuple-element.579), channel_id=1, source_target_pairs={{2,1},{1,0},{6,5},{5,4},{10,9},{9,8},{14,13},{13,12},{18,17},{17,1... | collective-permute-start | bytes 245768 | tf_op jit(solution)/shard_map/ppermute | solution.py:500

commit v3 on v2

v3 whole, which is shorter than its diff:
```python
import jax
import jax.numpy as jnp
from jax import lax
from jax.experimental import pallas as pl
from jax.experimental.pallas import tpu as pltpu
from jax.sharding import PartitionSpec as P

F32 = jnp.float32
V = 5
AXES = ("row", "sector", "slab")
VMEM_BYTES = 14 * 1024 * 1024


def matvec(mat, vec):
    out = []
    for i in range(V):
        acc = mat(i, 0) * vec[0]
        for j in range(1, V):
            acc = acc + mat(i, j) * vec[j]
        out.append(acc)
    return out


def stacked(ref, base):
    return lambda i, j: ref[base + V * i + j]


def planes_of(ref, base):
    return [ref[base + v] for v in range(V)]


def put(ref, base, values):
    for v in range(V):
        ref[base + v] = values[v]


def sliding(owner, columns, total):
    lead = owner[0]

    def lower(i, best):
        return jnp.minimum(best, ((owner[i] - lead + total // 2) & (total - 1)) - total // 2)

    return (lead + lax.fori_loop(1, columns, lower, jnp.int32(0), unroll=True)) & (total - 1)


def pack_kernel(planes, columns, state, towards_low, interface, towards_high, lowest):
    row = lax.axis_index("row")
    face = jnp.where(row == 0, planes - 1, 0)
    for v in range(V):
        plane = state[0, v, face]
        interface[v] = plane
        towards_low[v, planes:] = plane
        lowest[v] = state[0, v, 0]
        for x in range(planes):
            towards_low[v, x : x + 1] = state[0, v, x, 0:1]
            towards_high[v, x : x + 1] = state[0, v, x, columns - 1 : columns]


def window_kernel(planes, columns, sectors, owner, own, next_one, next_two, message, pair, table, landing):
    row = lax.axis_index("row")
    sector = lax.axis_index("sector")
    total = sectors * columns
    for v in range(V):
        table[v, 0:columns] = own[v]
        table[v, columns : 2 * columns] = next_one[v, planes:]
        table[v, 2 * columns :] = next_two[v]
    turn = sliding(owner, columns, total) >> (columns.bit_length() - 1)
    even = turn & -2
    pair[0] = turn >> 1

    @pl.when(row == 1)
    def _():
        facing = (sector - even) & (sectors - 1)

        def step(i, carry):
            at = (owner[facing * columns + i] - sector * columns) & (total - 1)
            at = jnp.minimum(at, 3 * columns - 1)
            for v in range(V):
                landing[v, pl.ds(i, 1)] = table[v, pl.ds(at, 1)]
            return carry

        lax.fori_loop(0, columns, step, 0, unroll=8)

    @pl.when(row == 0)
    def _():
        facing = (sector + even + 2) & (sectors - 1)
        first = (1 - (turn - even)) * columns

        def step(i, carry):
            at = first + i
            column = owner[(sector * columns + at) & (total - 1)]
            to = jnp.minimum((column - facing * columns) & (total - 1), columns)
            for v in range(V):
                landing[v, pl.ds(to, 1)] = table[v, pl.ds(at, 1)]
            return carry

        lax.fori_loop(0, 2 * columns, step, 0, unroll=8)

    for v in range(V):
        message[v] = landing[v, 0:columns]


def matrix_kernel(
    planes, flux, inverse, prefix_out, right, left, side, product, blocks, prefix, left_now, right_now,
):
    row = lax.axis_index("row")
    slab = lax.axis_index("slab")
    scaled = [[jnp.full((8, 128), flux[V * i + j], F32) for j in range(V)] for i in range(V)]

    def one_strip(step, carry):
        at = pl.ds(pl.multiple_of(step * 8, 8), 8)

        def factor(x):
            return lambda i, j: product[V * i + j, x, at]

        def flux_times(x):
            for i in range(V):
                entries = [inverse[0, i, k, x, at] for k in range(V)]
                for k in range(V):
                    blocks[V * i + k, x, at] = entries[k]
                for j in range(V):
                    acc = entries[0] * scaled[0][j]
                    for k in range(1, V):
                        acc = acc + entries[k] * scaled[k][j]
                    product[V * i + j, x, at] = acc

        def forward(x, carry):
            flux_times(x)
            for j in range(V):
                column = [prefix[x - 1, V * i + j] for i in range(V)]
                put_column(prefix.at[x], j, matvec(factor(x), column))
            return carry

        flux_times(0)
        for k in range(V * V):
            prefix[0, k] = product[k, 0, at]
        lax.fori_loop(1, planes, forward, 0)
        for k in range(V * V):
            prefix_out[k, at] = prefix[planes - 1, k]

        @pl.when(slab > 0)
        def _():
            for j in range(V):
                column = [prefix[planes - 2, V * i + j] for i in range(V)]
                put_column(left_now, j, matvec(factor(planes - 1), column))

            def backward(step, carry):
                x = planes - 1 - step
                for j in range(V):
                    column = [prefix[x - 1, V * i + j] - left_now[V * i + j] for i in range(V)]
                    put_column(left_now, j, matvec(factor(x), column))
                return carry

            lax.fori_loop(1, planes - 1, backward, 0)
            for j in range(V):
                column = [float(i == j) - left_now[V * i + j] for i in range(V)]
                put_column(left_now, j, matvec(factor(0), column))
            for k in range(V * V):
                left[k, at] = left_now[k]
                side[k, at] = left_now[k]

        @pl.when((slab == 1) | (slab == 2) | ((slab == 3) & (row == 0)))
        def _():
            for k in range(V * V):
                right_now[k] = product[k, planes - 1, at]

            def backward(step, carry):
                x = planes - 1 - step
                for j in range(V):
                    column = [right_now[V * i + j] for i in range(V)]
                    put_column(right_now, j, matvec(factor(x), column))
                return carry

            lax.fori_loop(1, planes, backward, 0)
            for k in range(V * V):
                right[k, at] = right_now[k]

        @pl.when(slab == 1)
        def _():
            for k in range(V * V):
                side[k, at] = right_now[k]

        return carry

    lax.fori_loop(0, inverse.shape[4] // 8, one_strip, 0)


def put_column(ref, j, values):
    for i in range(V):
        ref[V * i + j] = values[i]


def residual_kernel(
    planes, columns, flux, state, source, blocks, product, from_high, from_low, above, prefix_in,
    residual, started, up, down, wide, forward,
):
    for v in range(V):
        for x in range(planes):
            wide[v, x, 8 : 8 + columns] = state[0, v, x]
            wide[v, x, 7:8] = from_low[v, x : x + 1]
            wide[v, x, 8 + columns : 9 + columns] = from_high[v, x : x + 1]
    rows = lax.broadcasted_iota(jnp.int32, (8, 128), 0)
    lanes = lax.broadcasted_iota(jnp.int32, (8, 128), 1)
    ja = lambda i, j: flux[V * i + j]
    jb = lambda i, j: flux[V * V + V * i + j]
    jr = lambda i, j: flux[2 * V * V + V * i + j]

    def one_strip(step, carry):
        at = pl.ds(pl.multiple_of(step * 8, 8), 8)
        middle = pl.ds(pl.multiple_of(step * 8 + 8, 8), 8)
        high = pl.ds(pl.multiple_of(step * 8 + 16, 8), 8)
        previous = None
        for x in range(planes):
            along, around, outward = [], [], []
            for v in range(V):
                here = wide[v, x, middle]
                nearer = wide[v, x + 1, middle] if x + 1 < planes else above[v, at]
                along.append(nearer - wide[v, x - 1, middle] if x else nearer)
                plus = jnp.where(rows == 0, wide[v, x, high], here)
                minus = jnp.where(rows == 7, wide[v, x, at], here)
                around.append(pltpu.roll(plus, 7, 0) - pltpu.roll(minus, 1, 0))
                outward.append(
                    jnp.where(lanes == 127, 0.0, pltpu.roll(here, 127, 1))
                    - jnp.where(lanes == 0, 0.0, pltpu.roll(here, 1, 1))
                )
            one, two, three = matvec(ja, along), matvec(jb, around), matvec(jr, outward)
            values = [source[0, v, x, at] - (one[v] + two[v] + three[v]) for v in range(V)]
            for v in range(V):
                residual[v, x, at] = values[v]
            values = matvec(lambda i, j: blocks[V * i + j, x, at], values)
            for v in range(V):
                started[v, x, at] = values[v]
            if previous is not None:
                carried = matvec(lambda i, j: product[V * i + j, x, at], previous)
                values = [values[v] + carried[v] for v in range(V)]
            previous = values
            for v in range(V):
                forward[v, x] = previous[v]
        for v in range(V):
            last = wide[v, planes - 1, middle]
            up[v, at] = previous[v] + last
            up[V + v, at] = last
        for k in range(V * V):
            up[2 * V + k, at] = prefix_in[k, at]
        for x in range(planes - 2, -1, -1):
            carried = matvec(lambda i, j: product[V * i + j, x, at], previous)
            previous = [forward[v, x] - carried[v] for v in range(V)]
        for v in range(V):
            down[v, at] = previous[v]
        return carry

    lax.fori_loop(0, columns // 8, one_strip, 0)


def first_kernel(ghost, up, down, right, entry, message):
    slab = lax.axis_index("slab")
    for v in range(V):
        message[V + v] = up[V + v]

    @pl.when(slab == 0)
    def _():
        moved = matvec(stacked(up, 2 * V), planes_of(ghost, 0))
        for v in range(V):
            total = up[v] + moved[v]
            entry[v] = total
            message[v] = total

    @pl.when(slab == 3)
    def _():
        moved = matvec(stacked(right, 0), planes_of(ghost, 0))
        for v in range(V):
            message[v] = jnp.where(lax.axis_index("row") == 0, down[v] + moved[v], down[v])


def middle_kernel(
    came, came_side, up_other, left_other, up, down, right, left, lower, message, inflow, under, beyond,
):
    slab = lax.axis_index("slab")

    @pl.when(slab == 1)
    def _():
        moved = matvec(stacked(left, 0), planes_of(came_side, 0))
        put(lower, 0, [down[v] + moved[v] for v in range(V)])

    @pl.when(slab == 2)
    def _():
        moved = matvec(stacked(up_other, 2 * V), planes_of(came, 0))
        second = [up_other[v] + moved[v] for v in range(V)]
        moved = matvec(stacked(up, 2 * V), second)
        third = [up[v] + moved[v] for v in range(V)]
        moved = matvec(stacked(left_other, 0), third)
        top = [came_side[v] + moved[v] for v in range(V)]
        moved = matvec(stacked(left, 0), second)
        again = matvec(stacked(right, 0), top)
        put(lower, 0, [down[v] + moved[v] + again[v] for v in range(V)])
        put(message, 0, third)
        put(message, V, planes_of(up, V))
        put(inflow, 0, second)
        put(under, 0, planes_of(up_other, V))
        put(beyond, 0, top)


def last_kernel(
    planes, flux, ghost, came_side, to_third, to_zero, to_lower, second, under_second, top,
    right_other, partial, started, product, inverse, state, residual, new_state, forward, inflow, beyond,
    under,
):
    row = lax.axis_index("row")
    slab = lax.axis_index("slab")
    ja = lambda i, j: flux[V * i + j]
    has_top = jnp.where((row == 0) & (slab == 3), 1.0, 0.0)

    @pl.when(slab == 0)
    def _():
        inflow[...] = ghost[...]
        under[...] = ghost[...]

    @pl.when(slab == 1)
    def _():
        inflow[...] = came_side[0:V]
        under[...] = came_side[V:]
        beyond[...] = to_lower[...]

    @pl.when(slab == 2)
    def _():
        inflow[...] = second[...]
        under[...] = under_second[...]
        beyond[...] = top[...]

    @pl.when(slab == 3)
    def _():
        inflow[...] = to_third[0:V]
        under[...] = to_third[V:]
        beyond[...] = jnp.zeros_like(beyond)

    def one_strip(step, carry):
        at = pl.ds(pl.multiple_of(step * 8, 8), 8)

        @pl.when(slab == 0)
        def _():
            came = [to_zero[v, at] for v in range(V)]
            moved = matvec(lambda i, j: right_other[V * i + j, at], came)
            for v in range(V):
                beyond[v, at] = to_lower[v, at] + moved[v]

        previous = [inflow[v, at] for v in range(V)]
        for x in range(planes):
            values = [partial[v, x, at] for v in range(V)]
            begun = [started[v, x, at] for v in range(V)]
            if x == planes - 1:
                top_part = matvec(ja, [ghost[v, at] * has_top for v in range(V)])
                values = [values[v] - top_part[v] for v in range(V)]
                lost = matvec(lambda i, j: inverse[V * i + j, x, at], top_part)
                begun = [begun[v] - lost[v] for v in range(V)]
            if x == 0:
                bottom = matvec(ja, [under[v, at] for v in range(V)])
                values = [values[v] + bottom[v] for v in range(V)]
            for v in range(V):
                residual[0, v, x, at] = values[v]
            carried = matvec(lambda i, j: product[V * i + j, x, at], previous)
            previous = [begun[v] + carried[v] for v in range(V)]
            for v in range(V):
                forward[v, x] = previous[v]
        following = [beyond[v, at] for v in range(V)]
        for x in range(planes - 1, -1, -1):
            carried = matvec(lambda i, j: product[V * i + j, x, at], following)
            following = [forward[v, x] - carried[v] for v in range(V)]
            for v in range(V):
                new_state[0, v, x, at] = state[0, v, x, at] + following[v]
        return carry

    lax.fori_loop(0, state.shape[3] // 8, one_strip, 0)


def sds(*shape):
    return jax.ShapeDtypeStruct(shape, F32)


def full(shape):
    return pl.BlockSpec(shape, lambda *_: (0,) * len(shape))


def strip(lead):
    return pl.BlockSpec((lead, 8, 128), lambda i: (0, i, 0))


SCALARS = pl.BlockSpec(memory_space=pltpu.SMEM)
WHOLE = pl.BlockSpec(memory_space=pltpu.VMEM)


def params(**more):
    return pltpu.CompilerParams(vmem_limit_bytes=VMEM_BYTES, **more)


def cost(amount):
    return pl.CostEstimate(flops=amount, bytes_accessed=amount // 8, transcendentals=0)


def per_device(state, source, diag_inverse, jac_axial, jac_cross, owner):
    planes, columns, radial = state.shape[2:]
    sectors = lax.axis_size("sector")
    slabs = lax.axis_size("slab")
    strips = columns // 8
    plane = (V, columns, radial)
    cells = pl.BlockSpec((1, V, planes, 8, radial), lambda i: (0, 0, 0, i, 0))
    blocks = pl.BlockSpec((1, V, V, planes, 8, radial), lambda i: (0, 0, 0, 0, i, 0))
    inner = pl.BlockSpec((V, planes, 8, radial), lambda i: (0, 0, i, 0))
    size = slabs * sectors

    def device(row, sector, slab):
        return row * size + sector % sectors * slabs + slab

    def import_pairs(even):
        pairs = []
        for j in range(sectors):
            pairs.append((device(1, j, 0), device(0, j - even, slabs - 1)))
            pairs.append((device(0, j, slabs - 1), device(1, j + even + 2, 0)))
        return pairs

    two_down = []
    for j in range(sectors):
        two_down.append((device(0, j, slabs - 1), device(0, j - 2, slabs - 1)))
        two_down.append((device(1, j, 0), device(1, j - 2, 0)))

    total = sectors * columns
    assert total & (total - 1) == 0 and columns & (columns - 1) == 0
    flux = 0.5 * jnp.concatenate([jac_axial.reshape(-1), jac_cross.reshape(-1)])
    towards_low, interface, towards_high, lowest = pl.pallas_call(
        lambda *refs: pack_kernel(planes, columns, *refs),
        out_shape=(sds(V, planes + columns, radial), sds(*plane), sds(V, planes, radial), sds(*plane)),
        compiler_params=params(),
        name="pack",
    )(state)
    above = lax.ppermute(lowest, "slab", [(k, k - 1) for k in range(1, slabs)])
    from_low = lax.ppermute(towards_high, "sector", [(j, (j + 1) % sectors) for j in range(sectors)])
    from_second = lax.ppermute(interface, AXES, two_down)
    from_high = lax.ppermute(towards_low, "sector", [(j, (j - 1) % sectors) for j in range(sectors)])

    square = sds(V * V, columns, radial)
    cubic = sds(V * V, planes, columns, radial)
    prefix, right, left, side, product, blocks = pl.pallas_call(
        lambda *refs: matrix_kernel(planes, *refs),
        in_specs=[SCALARS, WHOLE],
        out_shape=(square, square, square, square, cubic, cubic),
        scratch_shapes=[
            pltpu.VMEM((planes, V * V, 8, radial), F32),
            pltpu.VMEM((V * V, 8, radial), F32),
            pltpu.VMEM((V * V, 8, radial), F32),
        ],
        compiler_params=params(),
        cost_estimate=cost(60_000_000),
        name="matrices",
    )(flux, diag_inverse)
    message, pair = pl.pallas_call(
        lambda *refs: window_kernel(planes, columns, sectors, *refs),
        in_specs=[SCALARS] + [WHOLE] * 3,
        out_specs=[WHOLE, SCALARS],
        out_shape=(sds(*plane), jax.ShapeDtypeStruct((1,), jnp.int32)),
        scratch_shapes=[
            pltpu.VMEM((V, 3 * columns, radial), F32),
            pltpu.VMEM((V, columns + 8, radial), F32),
        ],
        compiler_params=params(),
        name="window",
    )(owner, interface, from_high, from_second)

    def exchange(even, message, from_low, above, from_high, prefix, product, blocks):
        ghost = lax.ppermute(message, AXES, import_pairs(even))
        partial, started, up, down = pl.pallas_call(
            lambda *refs: residual_kernel(planes, columns, *refs),
            in_specs=[SCALARS] + [WHOLE] * 8,
            out_shape=(
                sds(V, planes, columns, radial), sds(V, planes, columns, radial),
                sds(2 * V + V * V, columns, radial), sds(*plane),
            ),
            scratch_shapes=[
                pltpu.VMEM((V, planes, columns + 16, radial), F32),
                pltpu.VMEM((V, planes, 8, radial), F32),
            ],
            compiler_params=params(),
            cost_estimate=cost(40_000_000),
            name="residual",
        )(flux, state, source, blocks, product, from_high, from_low, above, prefix)
        return ghost, partial, started, up, down

    ghost, partial, started, up, down = lax.switch(
        pair[0],
        [lambda *args, e=e: exchange(2 * e, *args) for e in range(sectors // 2)],
        message, from_low, above, from_high, prefix, product, blocks,
    )
    up_other = lax.ppermute(up, "slab", [(1, 2)])
    side_other = lax.ppermute(side, "slab", [(1, 0), (3, 2)])
    entry, side_message = pl.pallas_call(
        first_kernel,
        out_shape=(sds(*plane), sds(2 * V, columns, radial)),
        compiler_params=params(),
        name="first",
    )(ghost, up, down, right)
    came_side = lax.ppermute(side_message, "slab", [(0, 1), (3, 2)])
    came = lax.ppermute(entry, "slab", [(0, 2)])
    lower, onward, second, under, top = pl.pallas_call(
        middle_kernel,
        out_shape=(sds(*plane), sds(2 * V, columns, radial), sds(*plane), sds(*plane), sds(*plane)),
        compiler_params=params(),
        name="middle",
    )(came, came_side, up_other, side_other, up, down, right, left)
    to_lower = lax.ppermute(lower, "slab", [(2, 1), (1, 0)])
    to_third = lax.ppermute(onward, "slab", [(2, 3)])
    to_zero = lax.ppermute(lower, "slab", [(2, 0)])

    residual, new_state = pl.pallas_call(
        lambda *refs: last_kernel(planes, *refs),
        in_specs=[SCALARS] + [WHOLE] * 14,
        out_shape=(sds(*state.shape), sds(*state.shape)),
        scratch_shapes=[pltpu.VMEM((V, planes, 8, radial), F32)] + [pltpu.VMEM(plane, F32)] * 3,
        compiler_params=params(),
        name="last",
    )(
        flux, ghost, came_side, to_third, to_zero, to_lower, second, under, top,
        side_other, partial, started, product, blocks, state,
    )
    return residual, new_state


def solution(mesh):
    return jax.shard_map(
        per_device,
        mesh=mesh,
        in_specs=(
            P("row", None, "slab", "sector", None),
            P("row", None, "slab", "sector", None),
            P("row", None, None, "slab", "sector", None),
            P("row", None, None),
            P("row", None, None, None),
            P(),
        ),
        out_specs=(P("row", None, "slab", "sector", None), P("row", None, "slab", "sector", None)),
        check_vma=False,
    )
```

time: 66.4 us -> 72 us (1.084)
  the two profiles are of different devices: /device:TPU:2 before, /device:TPU:8 now
where the time goes in v3:
time: 72 us; the launch traced here: 71 us
  Pallas kernels  22.6 us (31%)
  starting transfers between devices  22.1 us (31%)
  waiting for transfers between devices  21.3 us (30%)
  local copies, waits for them, and re-layouts  2.8 us (4%)
  between operations  1.44 us (2%)
  other arithmetic  0.77 us (1%)
    ppermute x1, waiting for transfers between devices, per_device(): to_zero = lax.ppermute(lower, 'slab', [(2, 0)])  12.8 us
    ppermute x1, starting transfers between devices, per_device(): came_side = lax.ppermute(side_message, 'slab', [(0, 1), (3, 2)])  9.78 us
    pallas_call x1, Pallas kernels, exchange(): pl.pallas_call(lambda *refs: residual_kernel(planes, columns, *refs), in_...  6.47 us
    ppermute x1, waiting for transfers between devices, per_device(): to_lower = lax.ppermute(lower, 'slab', [(2, 1), (1, 0)])  6.12 us
    pallas_call x1, Pallas kernels, per_device(): pl.pallas_call(lambda *refs: matrix_kernel(planes, *refs), in_specs=[SCAL...  6.07 us
    pallas_call x1, Pallas kernels, per_device(): pl.pallas_call(lambda *refs: last_kernel(planes, *refs), in_specs=[SCALAR...  5.17 us
    unnamed x13, local copies, waits for them, and re-layouts  2.64 us
    ppermute x1, waiting for transfers between devices, per_device(): came = lax.ppermute(entry, 'slab', [(0, 2)])  2.39 us
  transfers between devices with their start and end apart: 12, of which 3 were waited for; matrix products, arithmetic and copies ran while one was open for 2% of the time, Pallas kernels for 21%

profile of v3, /device:TPU:8, one launch (start us, length us, event | category | flops | bytes accessed | tf_op | source)
XLA Modules:
  0.0 71.0 jit_solution(5024884557539713971)
XLA Ops:
  0.6 0.0 copy-start.2
  0.6 0.0 copy-start.1
  0.6 1.2 %pack.1 = (f32[5,40,128]{2,1,0:T(8,128)S(1)}, f32[5,32,128]{2,1,0:T(8,128)S(1)}, f32[5,8,128]{2,1,0:T(8,128)S(1)}, f32[5,32,128]{2,1,0:T(8,128)S(1)}) custom-call(f32[1,5,8,32,128]{4,3,2,1,0:T(8,128)} %refs_14_.1), custom_call_target="tpu_custom_call" | custom-call | tf_op jit(solution)/shard_map/pack/pallas_call | solution.py:428
  1.9 1.7 %collective-permute-start.18 = (f32[5,8,128]{2,1,0:T(8,128)S(1)}, f32[5,8,128]{2,1,0:T(8,128)S(1)}, u32[]{:S(2)}, u32[]{:S(2)}) collective-permute-start(f32[5,8,128]{2,1,0:T(8,128)S(1)} %get-tuple-element.576), channel_id=1, source_target_pairs={{0,4},{4,8},{8,12},{12,16},{16,20},{20,24},{24,28},{28,32},{32,36}... | collective-permute-start | bytes 61448 | tf_op jit(solution)/shard_map/ppermute | solution.py:435
  3.5 1.3 %collective-permute-start.19 = (f32[5,32,128]{2,1,0:T(8,128)S(1)}, f32[5,32,128]{2,1,0:T(8,128)S(1)}, u32[]{:S(2)}, u32[]{:S(2)}) collective-permute-start(f32[5,32,128]{2,1,0:T(8,128)S(1)} %get-tuple-element.577), channel_id=1, source_target_pairs={{1,0},{2,1},{3,2},{5,4},{6,5},{7,6},{9,8},{10,9},{11,10},{13,12},{... | collective-permute-start | bytes 245768 | tf_op jit(solution)/shard_map/ppermute | solution.py:434
  4.8 0.7 collective-permute-start.17
  5.5 0.7 %collective-permute-start.16 = (f32[5,40,128]{2,1,0:T(8,128)S(1)}, f32[5,40,128]{2,1,0:T(8,128)S(1)}, u32[]{:S(2)}, u32[]{:S(2)}) collective-permute-start(f32[5,40,128]{2,1,0:T(8,128)S(1)} %get-tuple-element.571), channel_id=1, source_target_pairs={{0,124},{4,0},{8,4},{12,8},{16,12},{20,16},{24,20},{28,24},{32,28}... | collective-permute-start | bytes 307208 | tf_op jit(solution)/shard_map/ppermute | solution.py:437
  6.2 0.7 reduce
  6.9 0.1 reshape.13
  7.0 0.7 copy.9
  7.7 0.1 reshape.14
  7.7 0.1 maximum_multiply_fusion.refs_0_
  7.8 0.0 copy-start
  7.8 1.9 %copy-done = f32[1,5,5,8,32,128]{5,4,3,2,1,0:T(8,128)S(1)} copy-done((f32[1,5,5,8,32,128]{5,4,3,2,1,0:T(8,128)S(1)}, f32[1,5,5,8,32,128]{5,4,3,2,1,0:T(8,128)}, u32[]{:S(2)}) %copy-start) | copy-done | bytes 3276824
  9.7 0.0 copy-start.3
  9.7 6.1 %matrices.1 = (f32[25,32,128]{2,1,0:T(8,128)S(1)}, f32[25,32,128]{2,1,0:T(8,128)S(1)}, f32[25,32,128]{2,1,0:T(8,128)S(1)}, f32[25,32,128]{2,1,0:T(8,128)S(1)}, f...) custom-call(f32[75]{0:T(128)S(1)} %maximum_multiply_fusion.refs_0_, f32[1,5,5,8,32,128]{5,4,3,2,1,0:T(8,128)S(1)} %copy-done), custom_call_target="tpu_custom_call" | custom-call | flops 60000000 | bytes 7500000 | tf_op jit(solution)/shard_map/matrices/pallas_call | solution.py:441
  15.8 0.0 collective-permute-done.17.refs_3_
  15.8 0.0 collective-permute-done.16.refs_2_
  15.8 0.0 copy-done.1
  15.8 1.4 %window.1 = (f32[5,32,128]{2,1,0:T(8,128)S(1)}, s32[1]{0:T(128)}) custom-call(s32[1024]{0:T(1024)S(1)} %copy-done.1, f32[5,32,128]{2,1,0:T(8,128)S(1)} %get-tuple-element.570.refs_1_, f32[5,40,128]{2,1,0:T(8,128)S(1)} %collective-permute-done.16.refs_2_, f32[5,32,128]{2,1,0:T(8,128)S(1)} %collective-permute-done.17.refs_3_), custom_call_target="tpu_custom_call" | custom-call | tf_op jit(solution)/shard_map/window/pallas_call | solution.py:454
  17.9 0.0 collective-permute-done.18
  17.9 0.0 collective-permute-done.19
  17.9 0.0 copy-done.2
  18.0 0.0 copy-done.3
  18.0 7.8 %conditional.1 = (f32[5,32,128]{2,1,0:T(8,128)}, f32[5,8,32,128]{3,2,1,0:T(8,128)}, f32[5,8,32,128]{3,2,1,0:T(8,128)}, f32[35,32,128]{2,1,0:T(8,128)}, f32[5,32,128]{2,1,0:T(8,128)S(1)}) conditional(s32[]{:T(128)} %bitcast, (f32[5,32,128]{2,1,0:T(8,128)S(1)}, f32[75]{0:T(128)S(1)}, ...), branch_computations={%region_0.0_spmd, %region_1.0_spmd, %region_2.0_spmd, %region_3.0_... | conditional | flops 40000000 | bytes 5327760 | solution.py:486
  18.0 1.3 %collective-permute-start.13 = (f32[5,32,128]{2,1,0:T(8,128)S(1)}, f32[5,32,128]{2,1,0:T(8,128)}, u32[]{:S(2)}, u32[]{:S(2)}) collective-permute-start(f32[5,32,128]{2,1,0:T(8,128)S(1)} %get-tuple-element.502), channel_id=1, source_target_pairs={{128,27},{3,240},{132,31},{7,244},{136,35},{11,248},{140,39},{15,2... | collective-permute-start | bytes 245768 | tf_op jit(solution)/shard_map/cond/branch_13_fun/ppermute | solution.py:468
  19.3 6.5 %residual.29 = (f32[5,8,32,128]{3,2,1,0:T(8,128)}, f32[5,8,32,128]{3,2,1,0:T(8,128)}, f32[35,32,128]{2,1,0:T(8,128)}, f32[5,32,128]{2,1,0:T(8,128)S(1)}) custom-call(f32[75]{0:T(128)S(1)} %get-tuple-element.503.refs_0_, f32[1,5,8,32,128]{4,3,2,1,0:T(8,128)S(1)} %get-tuple-element.504.refs_1_, f32[1,5,8,32,128]{4,3,2,1,0:T(8,128)S(1)} %get-tuple-element.505.refs_2_, ...), custom_call_target="tpu_custom_call" | custom-call | flops 40000000 | bytes 5000000 | tf_op jit(solution)/shard_map/cond/branch_13_fun/residual/pallas_call | solution.py:469
  25.8 0.0 collective-permute-done.13
  25.8 0.0 copy-start.4
  25.8 0.8 %collective-permute-start.22 = (f32[35,32,128]{2,1,0:T(8,128)}, f32[35,32,128]{2,1,0:T(8,128)S(1)}, u32[]{:S(2)}, u32[]{:S(2)}) collective-permute-start(f32[35,32,128]{2,1,0:T(8,128)} %get-tuple-element.580.up), channel_id=1, source_target_pairs={{1,2},{5,6},{9,10},{13,14},{17,18},{21,22},{25,26},{29,30},{33,34}... | collective-permute-start | bytes 1720328 | tf_op jit(solution)/shard_map/ppermute | solution.py:491
  26.7 1.3 %collective-permute-start.23 = (f32[25,32,128]{2,1,0:T(8,128)S(1)}, f32[25,32,128]{2,1,0:T(8,128)S(1)}, u32[]{:S(2)}, u32[]{:S(2)}) collective-permute-start(f32[25,32,128]{2,1,0:T(8,128)S(1)} %get-tuple-element.585), channel_id=1, source_target_pairs={{1,0},{3,2},{5,4},{7,6},{9,8},{11,10},{13,12},{15,14},{17,16},{19,... | collective-permute-start | bytes 1228808 | tf_op jit(solution)/shard_map/ppermute | solution.py:492
  28.0 1.2 %first.1 = (f32[5,32,128]{2,1,0:T(8,128)S(1)}, f32[10,32,128]{2,1,0:T(8,128)S(1)}) custom-call(f32[5,32,128]{2,1,0:T(8,128)} %get-tuple-element.579.ghost.refs_1_, f32[35,32,128]{2,1,0:T(8,128)} %get-tuple-element.580.up, f32[5,32,128]{2,1,0:T(8,128)S(1)} %get-tuple-element.581.down, f32[25,32,128]{2,1,0:T(8,128)S(1)} %get-tuple-element.582.right), custom_call_target="tpu_custom_call" | custom-call | tf_op jit(solution)/shard_map/first/pallas_call | solution.py:493
  29.1 9.8 %collective-permute-start.20 = (f32[10,32,128]{2,1,0:T(8,128)S(1)}, f32[10,32,128]{2,1,0:T(8,128)S(1)}, u32[]{:S(2)}, u32[]{:S(2)}) collective-permute-start(f32[10,32,128]{2,1,0:T(8,128)S(1)} %get-tuple-element.583), channel_id=1, source_target_pairs={{0,1},{3,2},{4,5},{7,6},{8,9},{11,10},{12,13},{15,14},{16,17},{19,... | collective-permute-start | bytes 491528 | tf_op jit(solution)/shard_map/ppermute | solution.py:499
  38.9 1.3 %collective-permute-start.21 = (f32[5,32,128]{2,1,0:T(8,128)S(1)}, f32[5,32,128]{2,1,0:T(8,128)S(1)}, u32[]{:S(2)}, u32[]{:S(2)}) collective-permute-start(f32[5,32,128]{2,1,0:T(8,128)S(1)} %get-tuple-element.584), channel_id=1, source_target_pairs={{0,2},{4,6},{8,10},{12,14},{16,18},{20,22},{24,26},{28,30},{32,34}... | collective-permute-start | bytes 245768 | tf_op jit(solution)/shard_map/ppermute | solution.py:500
  40.2 2.4 %collective-permute-done.21.came = f32[5,32,128]{2,1,0:T(8,128)S(1)} collective-permute-done((f32[5,32,128]{2,1,0:T(8,128)S(1)}, f32[5,32,128]{2,1,0:T(8,128)S(1)}, u32[]{:S(2)}, u32[]{:S(2)}) %collective-permute-start.21) | collective-permute-done | bytes 81952 | tf_op jit(solution)/shard_map/ppermute | solution.py:500
  42.6 0.0 collective-permute-done.20.came_side.refs_2_
  42.6 0.0 collective-permute-done.23.left_other.refs_9_
  42.6 0.0 collective-permute-done.22.up_other
  42.6 1.1 %middle.1 = (f32[5,32,128]{2,1,0:T(8,128)S(1)}, f32[10,32,128]{2,1,0:T(8,128)S(1)}, f32[5,32,128]{2,1,0:T(8,128)S(1)}, f32[5,32,128]{2,1,0:T(8,128)S(1)}, f32[5,32,128]{2,1,0:T(8,128)S(1)}) custom-call(f32[5,32,128]{2,1,0:T(8,128)S(1)} %collective-permute-done.21.came, f32[10,32,128]{2,1,0:T(8,128)S(1)} %collective-permute-done.20.came_side.refs_2_, ...), custom_call_target="tpu_custom_call" | custom-call | tf_op jit(solution)/shard_map/middle/pallas_call | solution.py:501
  43.7 0.7 collective-permute-start.24
  44.3 1.3 %collective-permute-start.26 = (f32[5,32,128]{2,1,0:T(8,128)S(1)}, f32[5,32,128]{2,1,0:T(8,128)S(1)}, u32[]{:S(2)}, u32[]{:S(2)}) collective-permute-start(f32[5,32,128]{2,1,0:T(8,128)S(1)} %get-tuple-element.588), channel_id=1, source_target_pairs={{2,1},{1,0},{6,5},{5,4},{10,9},{9,8},{14,13},{13,12},{18,17},{17,1... | collective-permute-start | bytes 245768 | tf_op jit(solution)/shard_map/ppermute | solution.py:507
  45.6 1.3 %collective-permute-start.25 = (f32[5,32,128]{2,1,0:T(8,128)S(1)}, f32[5,32,128]{2,1,0:T(8,128)S(1)}, u32[]{:S(2)}, u32[]{:S(2)}) collective-permute-start(f32[5,32,128]{2,1,0:T(8,128)S(1)} %get-tuple-element.588), channel_id=1, source_target_pairs={{2,0},{6,4},{10,8},{14,12},{18,16},{22,20},{26,24},{30,28},{34,32}... | collective-permute-start | bytes 245768 | tf_op jit(solution)/shard_map/ppermute | solution.py:509
  46.9 6.1 %collective-permute-done.26.refs_5_ = f32[5,32,128]{2,1,0:T(8,128)S(1)} collective-permute-done((f32[5,32,128]{2,1,0:T(8,128)S(1)}, f32[5,32,128]{2,1,0:T(8,128)S(1)}, u32[]{:S(2)}, u32[]{:S(2)}) %collective-permute-start.26) | collective-permute-done | bytes 81952 | tf_op jit(solution)/shard_map/ppermute | solution.py:507
  53.1 12.8 %collective-permute-done.25.refs_4_ = f32[5,32,128]{2,1,0:T(8,128)S(1)} collective-permute-done((f32[5,32,128]{2,1,0:T(8,128)S(1)}, f32[5,32,128]{2,1,0:T(8,128)S(1)}, u32[]{:S(2)}, u32[]{:S(2)}) %collective-permute-start.25) | collective-permute-done | bytes 81952 | tf_op jit(solution)/shard_map/ppermute | solution.py:509
  65.9 0.0 collective-permute-done.24.refs_3_
  65.9 0.0 copy-done.4
  65.9 0.0 copy-done.5
  65.9 5.2 %last.1 = (f32[1,5,8,32,128]{4,3,2,1,0:T(8,128)}, f32[1,5,8,32,128]{4,3,2,1,0:T(8,128)}) custom-call(f32[75]{0:T(128)S(1)} %maximum_multiply_fusion.refs_0_, f32[5,32,128]{2,1,0:T(8,128)} %get-tuple-element.579.ghost.refs_1_, f32[10,32,128]{2,1,0:T(8,128)S(1)} %collective-permute-done.20.came_side.refs_2_, ...), custom_call_target="tpu_custom_call" | custom-call | tf_op jit(solution)/shard_map/last/pallas_call | solution.py:511
  (1 shorter events, 0.0 us)
Async XLA Ops:
  0.6 17.3 %copy-start.2 = (f32[1,5,8,32,128]{4,3,2,1,0:T(8,128)S(1)}, f32[1,5,8,32,128]{4,3,2,1,0:T(8,128)}, u32[]{:S(2)}) copy-start(f32[1,5,8,32,128]{4,3,2,1,0:T(8,128)} %refs_14_.1) | copy-start | bytes 1966084
  0.6 15.2 %copy-start.1 = (s32[1024]{0:T(1024)S(1)}, s32[1024]{0:T(1024)}, u32[]{:S(2)}) copy-start(s32[1024]{0:T(1024)} %refs_0_.3) | copy-start | bytes 12292
  1.9 16.1 %collective-permute-start.18 = (f32[5,8,128]{2,1,0:T(8,128)S(1)}, f32[5,8,128]{2,1,0:T(8,128)S(1)}, u32[]{:S(2)}, u32[]{:S(2)}) collective-permute-start(f32[5,8,128]{2,1,0:T(8,128)S(1)} %get-tuple-element.576), channel_id=1, source_target_pairs={{0,4},{4,8},{8,12},{12,16},{16,20},{20,24},{24,28},{28,32},{32,36}... | collective-permute-start | bytes 61448 | tf_op jit(solution)/shard_map/ppermute | solution.py:435
  3.5 14.4 %collective-permute-start.19 = (f32[5,32,128]{2,1,0:T(8,128)S(1)}, f32[5,32,128]{2,1,0:T(8,128)S(1)}, u32[]{:S(2)}, u32[]{:S(2)}) collective-permute-start(f32[5,32,128]{2,1,0:T(8,128)S(1)} %get-tuple-element.577), channel_id=1, source_target_pairs={{1,0},{2,1},{3,2},{5,4},{6,5},{7,6},{9,8},{10,9},{11,10},{13,12},{... | collective-permute-start | bytes 245768 | tf_op jit(solution)/shard_map/ppermute | solution.py:434
  4.8 11.0 %collective-permute-start.17 = (f32[5,32,128]{2,1,0:T(8,128)S(1)}, f32[5,32,128]{2,1,0:T(8,128)S(1)}, u32[]{:S(2)}, u32[]{:S(2)}) collective-permute-start(f32[5,32,128]{2,1,0:T(8,128)S(1)} %get-tuple-element.570.refs_1_), channel_id=1, source_target_pairs={{3,123},{128,248},{7,127},{132,252},{11,3},{136,128},{15,7},{140,1... | collective-permute-start | bytes 245768 | tf_op jit(solution)/shard_map/ppermute | solution.py:436
  5.5 10.4 %collective-permute-start.16 = (f32[5,40,128]{2,1,0:T(8,128)S(1)}, f32[5,40,128]{2,1,0:T(8,128)S(1)}, u32[]{:S(2)}, u32[]{:S(2)}) collective-permute-start(f32[5,40,128]{2,1,0:T(8,128)S(1)} %get-tuple-element.571), channel_id=1, source_target_pairs={{0,124},{4,0},{8,4},{12,8},{16,12},{20,16},{24,20},{28,24},{32,28}... | collective-permute-start | bytes 307208 | tf_op jit(solution)/shard_map/ppermute | solution.py:437
  7.8 1.9 %copy-start = (f32[1,5,5,8,32,128]{5,4,3,2,1,0:T(8,128)S(1)}, f32[1,5,5,8,32,128]{5,4,3,2,1,0:T(8,128)}, u32[]{:S(2)}) copy-start(f32[1,5,5,8,32,128]{5,4,3,2,1,0:T(8,128)} %refs_1_.1) | copy-start | bytes 9830404
  9.7 8.2 %copy-start.3 = (f32[1,5,8,32,128]{4,3,2,1,0:T(8,128)S(1)}, f32[1,5,8,32,128]{4,3,2,1,0:T(8,128)}, u32[]{:S(2)}) copy-start(f32[1,5,8,32,128]{4,3,2,1,0:T(8,128)} %param.23) | copy-start | bytes 1966084
  18.0 7.8 %collective-permute-start.13 = (f32[5,32,128]{2,1,0:T(8,128)S(1)}, f32[5,32,128]{2,1,0:T(8,128)}, u32[]{:S(2)}, u32[]{:S(2)}) collective-permute-start(f32[5,32,128]{2,1,0:T(8,128)S(1)} %get-tuple-element.502), channel_id=1, source_target_pairs={{128,27},{3,240},{132,31},{7,244},{136,35},{11,248},{140,39},{15,2... | collective-permute-start | bytes 245768 | tf_op jit(solution)/shard_map/cond/branch_13_fun/ppermute | solution.py:468
  25.8 40.1 %copy-start.4 = (f32[5,8,32,128]{3,2,1,0:T(8,128)S(1)}, f32[5,8,32,128]{3,2,1,0:T(8,128)}, u32[]{:S(2)}) copy-start(f32[5,8,32,128]{3,2,1,0:T(8,128)} %get-tuple-element.592.refs_10_) | copy-start | bytes 1966084
  25.8 40.1 %copy-start.5 = (f32[5,8,32,128]{3,2,1,0:T(8,128)S(1)}, f32[5,8,32,128]{3,2,1,0:T(8,128)}, u32[]{:S(2)}) copy-start(f32[5,8,32,128]{3,2,1,0:T(8,128)} %get-tuple-element.593.refs_11_) | copy-start | bytes 1966084
  25.8 16.8 %collective-permute-start.22 = (f32[35,32,128]{2,1,0:T(8,128)}, f32[35,32,128]{2,1,0:T(8,128)S(1)}, u32[]{:S(2)}, u32[]{:S(2)}) collective-permute-start(f32[35,32,128]{2,1,0:T(8,128)} %get-tuple-element.580.up), channel_id=1, source_target_pairs={{1,2},{5,6},{9,10},{13,14},{17,18},{21,22},{25,26},{29,30},{33,34}... | collective-permute-start | bytes 1720328 | tf_op jit(solution)/shard_map/ppermute | solution.py:491
  26.7 15.9 %collective-permute-start.23 = (f32[25,32,128]{2,1,0:T(8,128)S(1)}, f32[25,32,128]{2,1,0:T(8,128)S(1)}, u32[]{:S(2)}, u32[]{:S(2)}) collective-permute-start(f32[25,32,128]{2,1,0:T(8,128)S(1)} %get-tuple-element.585), channel_id=1, source_target_pairs={{1,0},{3,2},{5,4},{7,6},{9,8},{11,10},{13,12},{15,14},{17,16},{19,... | collective-permute-start | bytes 1228808 | tf_op jit(solution)/shard_map/ppermute | solution.py:492
  29.1 13.5 %collective-permute-start.20 = (f32[10,32,128]{2,1,0:T(8,128)S(1)}, f32[10,32,128]{2,1,0:T(8,128)S(1)}, u32[]{:S(2)}, u32[]{:S(2)}) collective-permute-start(f32[10,32,128]{2,1,0:T(8,128)S(1)} %get-tuple-element.583), channel_id=1, source_target_pairs={{0,1},{3,2},{4,5},{7,6},{8,9},{11,10},{12,13},{15,14},{16,17},{19,... | collective-permute-start | bytes 491528 | tf_op jit(solution)/shard_map/ppermute | solution.py:499
  38.9 3.7 %collective-permute-start.21 = (f32[5,32,128]{2,1,0:T(8,128)S(1)}, f32[5,32,128]{2,1,0:T(8,128)S(1)}, u32[]{:S(2)}, u32[]{:S(2)}) collective-permute-start(f32[5,32,128]{2,1,0:T(8,128)S(1)} %get-tuple-element.584), channel_id=1, source_target_pairs={{0,2},{4,6},{8,10},{12,14},{16,18},{20,22},{24,26},{28,30},{32,34}... | collective-permute-start | bytes 245768 | tf_op jit(solution)/shard_map/ppermute | solution.py:500
  43.7 22.2 %collective-permute-start.24 = (f32[10,32,128]{2,1,0:T(8,128)S(1)}, f32[10,32,128]{2,1,0:T(8,128)S(1)}, u32[]{:S(2)}, u32[]{:S(2)}) collective-permute-start(f32[10,32,128]{2,1,0:T(8,128)S(1)} %get-tuple-element.587), channel_id=1, source_target_pairs={{2,3},{6,7},{10,11},{14,15},{18,19},{22,23},{26,27},{30,31},{34,35... | collective-permute-start | bytes 491528 | tf_op jit(solution)/shard_map/ppermute | solution.py:508
  44.3 8.7 %collective-permute-start.26 = (f32[5,32,128]{2,1,0:T(8,128)S(1)}, f32[5,32,128]{2,1,0:T(8,128)S(1)}, u32[]{:S(2)}, u32[]{:S(2)}) collective-permute-start(f32[5,32,128]{2,1,0:T(8,128)S(1)} %get-tuple-element.588), channel_id=1, source_target_pairs={{2,1},{1,0},{6,5},{5,4},{10,9},{9,8},{14,13},{13,12},{18,17},{17,1... | collective-permute-start | bytes 245768 | tf_op jit(solution)/shard_map/ppermute | solution.py:507
  45.6 20.2 %collective-permute-start.25 = (f32[5,32,128]{2,1,0:T(8,128)S(1)}, f32[5,32,128]{2,1,0:T(8,128)S(1)}, u32[]{:S(2)}, u32[]{:S(2)}) collective-permute-start(f32[5,32,128]{2,1,0:T(8,128)S(1)} %get-tuple-element.588), channel_id=1, source_target_pairs={{2,0},{6,4},{10,8},{14,12},{18,16},{22,20},{26,24},{30,28},{34,32}... | collective-permute-start | bytes 245768 | tf_op jit(solution)/shard_map/ppermute | solution.py:509

commit v4 on v3

--- a/solution.py
+++ b/solution.py
@@ -43,7 +43,11 @@
     return (lead + lax.fori_loop(1, columns, lower, jnp.int32(0), unroll=True)) & (total - 1)
 
 
-def pack_kernel(planes, columns, state, towards_low, interface, towards_high, lowest):
+def pack_kernel(
+    planes, columns, state, inverse, towards_low, interface, towards_high, lowest, highest, blocks, arrived,
+):
+    copy = pltpu.make_async_copy(inverse, blocks, arrived)
+    copy.start()
     row = lax.axis_index("row")
     face = jnp.where(row == 0, planes - 1, 0)
     for v in range(V):
@@ -51,9 +55,19 @@
         interface[v] = plane
         towards_low[v, planes:] = plane
         lowest[v] = state[0, v, 0]
+        highest[v] = state[0, v, planes - 1]
         for x in range(planes):
             towards_low[v, x : x + 1] = state[0, v, x, 0:1]
             towards_high[v, x : x + 1] = state[0, v, x, columns - 1 : columns]
+    copy.wait()
+
+
+def halved(ref, which=0):
+    entries = [
+        [jnp.broadcast_to(0.5 * ref[i, which : which + 1, j : j + 1], (8, 128)) for j in range(V)]
+        for i in range(V)
+    ]
+    return lambda i, j: entries[i][j]
 
 
 def window_kernel(planes, columns, sectors, owner, own, next_one, next_two, message, pair, table, landing):
@@ -101,28 +115,26 @@
 
 
 def matrix_kernel(
-    planes, flux, inverse, prefix_out, right, left, side, product, blocks, prefix, left_now, right_now,
+    planes, axial, inverse, prefix_out, right, left, product, prefix, left_now, right_now,
 ):
     row = lax.axis_index("row")
     slab = lax.axis_index("slab")
-    scaled = [[jnp.full((8, 128), flux[V * i + j], F32) for j in range(V)] for i in range(V)]
+    scaled = halved(axial)
 
     def one_strip(step, carry):
         at = pl.ds(pl.multiple_of(step * 8, 8), 8)
 
         def factor(x):
-            return lambda i, j: product[V * i + j, x, at]
+            return lambda i, j: product[x, V * i + j]
 
         def flux_times(x):
             for i in range(V):
                 entries = [inverse[0, i, k, x, at] for k in range(V)]
-                for k in range(V):
-                    blocks[V * i + k, x, at] = entries[k]
                 for j in range(V):
-                    acc = entries[0] * scaled[0][j]
+                    acc = entries[0] * scaled(0, j)
                     for k in range(1, V):
-                        acc = acc + entries[k] * scaled[k][j]
-                    product[V * i + j, x, at] = acc
+                        acc = acc + entries[k] * scaled(k, j)
+                    product[x, V * i + j] = acc
 
         def forward(x, carry):
             flux_times(x)
@@ -133,7 +145,7 @@
 
         flux_times(0)
         for k in range(V * V):
-            prefix[0, k] = product[k, 0, at]
+            prefix[0, k] = product[0, k]
         lax.fori_loop(1, planes, forward, 0)
         for k in range(V * V):
             prefix_out[k, at] = prefix[planes - 1, k]
@@ -157,12 +169,11 @@
                 put_column(left_now, j, matvec(factor(0), column))
             for k in range(V * V):
                 left[k, at] = left_now[k]
-                side[k, at] = left_now[k]
 
         @pl.when((slab == 1) | (slab == 2) | ((slab == 3) & (row == 0)))
         def _():
             for k in range(V * V):
-                right_now[k] = product[k, planes - 1, at]
+                right_now[k] = product[planes - 1, k]
 
             def backward(step, carry):
                 x = planes - 1 - step
@@ -175,11 +186,6 @@
             for k in range(V * V):
                 right[k, at] = right_now[k]
 
-        @pl.when(slab == 1)
-        def _():
-            for k in range(V * V):
-                side[k, at] = right_now[k]
-
         return carry
 
     lax.fori_loop(0, inverse.shape[4] // 8, one_strip, 0)
@@ -191,8 +197,8 @@
 
 
 def residual_kernel(
-    planes, columns, flux, state, source, blocks, product, from_high, from_low, above, prefix_in,
-    residual, started, up, down, wide, forward,
+    planes, columns, axial, cross, state, source, inverse, from_high, from_low, above, prefix_in,
+    residual, up, down, wide, forward,
 ):
     for v in range(V):
         for x in range(planes):
@@ -201,9 +207,9 @@
             wide[v, x, 8 + columns : 9 + columns] = from_high[v, x : x + 1]
     rows = lax.broadcasted_iota(jnp.int32, (8, 128), 0)
     lanes = lax.broadcasted_iota(jnp.int32, (8, 128), 1)
-    ja = lambda i, j: flux[V * i + j]
-    jb = lambda i, j: flux[V * V + V * i + j]
-    jr = lambda i, j: flux[2 * V * V + V * i + j]
+    ja = halved(axial)
+    jb = halved(cross)
+    jr = halved(cross, 1)
 
     def one_strip(step, carry):
         at = pl.ds(pl.multiple_of(step * 8, 8), 8)
@@ -227,23 +233,19 @@
             values = [source[0, v, x, at] - (one[v] + two[v] + three[v]) for v in range(V)]
             for v in range(V):
                 residual[v, x, at] = values[v]
-            values = matvec(lambda i, j: blocks[V * i + j, x, at], values)
-            for v in range(V):
-                started[v, x, at] = values[v]
             if previous is not None:
-                carried = matvec(lambda i, j: product[V * i + j, x, at], previous)
+                carried = matvec(ja, previous)
                 values = [values[v] + carried[v] for v in range(V)]
-            previous = values
+            previous = matvec(lambda i, j: inverse[0, i, j, x, at], values)
             for v in range(V):
                 forward[v, x] = previous[v]
         for v in range(V):
             last = wide[v, planes - 1, middle]
             up[v, at] = previous[v] + last
-            up[V + v, at] = last
         for k in range(V * V):
-            up[2 * V + k, at] = prefix_in[k, at]
+            up[V + k, at] = prefix_in[k, at]
         for x in range(planes - 2, -1, -1):
-            carried = matvec(lambda i, j: product[V * i + j, x, at], previous)
+            carried = matvec(lambda i, j: inverse[0, i, j, x, at], matvec(ja, previous))
             previous = [forward[v, x] - carried[v] for v in range(V)]
         for v in range(V):
             down[v, at] = previous[v]
@@ -254,12 +256,10 @@
 
 def first_kernel(ghost, up, down, right, entry, message):
     slab = lax.axis_index("slab")
-    for v in range(V):
-        message[V + v] = up[V + v]
 
     @pl.when(slab == 0)
     def _():
-        moved = matvec(stacked(up, 2 * V), planes_of(ghost, 0))
+        moved = matvec(stacked(up, V), planes_of(ghost, 0))
         for v in range(V):
             total = up[v] + moved[v]
             entry[v] = total
@@ -272,9 +272,7 @@
             message[v] = jnp.where(lax.axis_index("row") == 0, down[v] + moved[v], down[v])
 
 
-def middle_kernel(
-    came, came_side, up_other, left_other, up, down, right, left, lower, message, inflow, under, beyond,
-):
+def middle_kernel(came, came_side, up_other, left_other, up, down, right, left, lower, third, second, top):
     slab = lax.axis_index("slab")
 
     @pl.when(slab == 1)
@@ -284,30 +282,27 @@
 
     @pl.when(slab == 2)
     def _():
-        moved = matvec(stacked(up_other, 2 * V), planes_of(came, 0))
-        second = [up_other[v] + moved[v] for v in range(V)]
-        moved = matvec(stacked(up, 2 * V), second)
-        third = [up[v] + moved[v] for v in range(V)]
-        moved = matvec(stacked(left_other, 0), third)
-        top = [came_side[v] + moved[v] for v in range(V)]
-        moved = matvec(stacked(left, 0), second)
-        again = matvec(stacked(right, 0), top)
+        moved = matvec(stacked(up_other, V), planes_of(came, 0))
+        inflow = [up_other[v] + moved[v] for v in range(V)]
+        moved = matvec(stacked(up, V), inflow)
+        onward = [up[v] + moved[v] for v in range(V)]
+        moved = matvec(stacked(left_other, 0), onward)
+        beyond = [came_side[v] + moved[v] for v in range(V)]
+        moved = matvec(stacked(left, 0), inflow)
+        again = matvec(stacked(right, 0), beyond)
         put(lower, 0, [down[v] + moved[v] + again[v] for v in range(V)])
-        put(message, 0, third)
-        put(message, V, planes_of(up, V))
-        put(inflow, 0, second)
-        put(under, 0, planes_of(up_other, V))
-        put(beyond, 0, top)
+        put(third, 0, onward)
+        put(second, 0, inflow)
+        put(top, 0, beyond)
 
 
 def last_kernel(
-    planes, flux, ghost, came_side, to_third, to_zero, to_lower, second, under_second, top,
-    right_other, partial, started, product, inverse, state, residual, new_state, forward, inflow, beyond,
-    under,
+    planes, axial, ghost, below, came_side, to_third, to_zero, to_lower, second, top,
+    right_other, partial, inverse, state, residual, new_state, forward, inflow, beyond, under,
 ):
     row = lax.axis_index("row")
     slab = lax.axis_index("slab")
-    ja = lambda i, j: flux[V * i + j]
+    ja = halved(axial)
     has_top = jnp.where((row == 0) & (slab == 3), 1.0, 0.0)
 
     @pl.when(slab == 0)
@@ -315,22 +310,23 @@
         inflow[...] = ghost[...]
         under[...] = ghost[...]
 
+    @pl.when(slab != 0)
+    def _():
+        under[...] = below[...]
+
     @pl.when(slab == 1)
     def _():
-        inflow[...] = came_side[0:V]
-        under[...] = came_side[V:]
+        inflow[...] = came_side[...]
         beyond[...] = to_lower[...]
 
     @pl.when(slab == 2)
     def _():
         inflow[...] = second[...]
-        under[...] = under_second[...]
         beyond[...] = top[...]
 
     @pl.when(slab == 3)
     def _():
-        inflow[...] = to_third[0:V]
-        under[...] = to_third[V:]
+        inflow[...] = to_third[...]
         beyond[...] = jnp.zeros_like(beyond)
 
     def one_strip(step, carry):
@@ -346,24 +342,24 @@
         previous = [inflow[v, at] for v in range(V)]
         for x in range(planes):
             values = [partial[v, x, at] for v in range(V)]
-            begun = [started[v, x, at] for v in range(V)]
             if x == planes - 1:
                 top_part = matvec(ja, [ghost[v, at] * has_top for v in range(V)])
                 values = [values[v] - top_part[v] for v in range(V)]
-                lost = matvec(lambda i, j: inverse[V * i + j, x, at], top_part)
-                begun = [begun[v] - lost[v] for v in range(V)]
             if x == 0:
                 bottom = matvec(ja, [under[v, at] for v in range(V)])
-                values = [values[v] + bottom[v] for v in range(V)]
-            for v in range(V):
-                residual[0, v, x, at] = values[v]
-            carried = matvec(lambda i, j: product[V * i + j, x, at], previous)
-            previous = [begun[v] + carried[v] for v in range(V)]
+                for v in range(V):
+                    residual[0, v, x, at] = values[v] + bottom[v]
+            else:
+                for v in range(V):
+                    residual[0, v, x, at] = values[v]
+            carried = matvec(ja, previous)
+            values = [values[v] + carried[v] for v in range(V)]
+            previous = matvec(lambda i, j: inverse[0, i, j, x, at], values)
             for v in range(V):
                 forward[v, x] = previous[v]
         following = [beyond[v, at] for v in range(V)]
         for x in range(planes - 1, -1, -1):
-            carried = matvec(lambda i, j: product[V * i + j, x, at], following)
+            carried = matvec(lambda i, j: inverse[0, i, j, x, at], matvec(ja, following))
             following = [forward[v, x] - carried[v] for v in range(V)]
             for v in range(V):
                 new_state[0, v, x, at] = state[0, v, x, at] + following[v]
@@ -374,14 +370,6 @@
 
 def sds(*shape):
     return jax.ShapeDtypeStruct(shape, F32)
-
-
-def full(shape):
-    return pl.BlockSpec(shape, lambda *_: (0,) * len(shape))
-
-
-def strip(lead):
-    return pl.BlockSpec((lead, 8, 128), lambda i: (0, i, 0))
 
 
 SCALARS = pl.BlockSpec(memory_space=pltpu.SMEM)
@@ -400,11 +388,7 @@
     planes, columns, radial = state.shape[2:]
     sectors = lax.axis_size("sector")
     slabs = lax.axis_size("slab")
-    strips = columns // 8
     plane = (V, columns, radial)
-    cells = pl.BlockSpec((1, V, planes, 8, radial), lambda i: (0, 0, 0, i, 0))
-    blocks = pl.BlockSpec((1, V, V, planes, 8, radial), lambda i: (0, 0, 0, 0, i, 0))
-    inner = pl.BlockSpec((V, planes, 8, radial), lambda i: (0, 0, i, 0))
     size = slabs * sectors
 
     def device(row, sector, slab):
@@ -424,33 +408,26 @@
 
     total = sectors * columns
     assert total & (total - 1) == 0 and columns & (columns - 1) == 0
-    flux = 0.5 * jnp.concatenate([jac_axial.reshape(-1), jac_cross.reshape(-1)])
-    towards_low, interface, towards_high, lowest = pl.pallas_call(
+    axial = jnp.transpose(jac_axial, (1, 0, 2))
+    cross = jnp.transpose(jac_cross[0], (1, 0, 2))
+    towards_low, interface, towards_high, lowest, highest, blocks = pl.pallas_call(
         lambda *refs: pack_kernel(planes, columns, *refs),
-        out_shape=(sds(V, planes + columns, radial), sds(*plane), sds(V, planes, radial), sds(*plane)),
+        in_specs=[WHOLE, pl.BlockSpec(memory_space=pltpu.HBM)],
+        out_specs=[WHOLE] * 6,
+        out_shape=(
+            sds(V, planes + columns, radial), sds(*plane), sds(V, planes, radial), sds(*plane),
+            sds(*plane), pltpu.VMEM(diag_inverse.shape, F32),
+        ),
+        scratch_shapes=[pltpu.SemaphoreType.DMA],
         compiler_params=params(),
         name="pack",
-    )(state)
+    )(state, pltpu.with_memory_space_constraint(diag_inverse, pltpu.HBM))
     above = lax.ppermute(lowest, "slab", [(k, k - 1) for k in range(1, slabs)])
     from_low = lax.ppermute(towards_high, "sector", [(j, (j + 1) % sectors) for j in range(sectors)])
     from_second = lax.ppermute(interface, AXES, two_down)
     from_high = lax.ppermute(towards_low, "sector", [(j, (j - 1) % sectors) for j in range(sectors)])
 
     square = sds(V * V, columns, radial)
-    cubic = sds(V * V, planes, columns, radial)
-    prefix, right, left, side, product, blocks = pl.pallas_call(
-        lambda *refs: matrix_kernel(planes, *refs),
-        in_specs=[SCALARS, WHOLE],
-        out_shape=(square, square, square, square, cubic, cubic),
-        scratch_shapes=[
-            pltpu.VMEM((planes, V * V, 8, radial), F32),
-            pltpu.VMEM((V * V, 8, radial), F32),
-            pltpu.VMEM((V * V, 8, radial), F32),
-        ],
-        compiler_params=params(),
-        cost_estimate=cost(60_000_000),
-        name="matrices",
-    )(flux, diag_inverse)
     message, pair = pl.pallas_call(
         lambda *refs: window_kernel(planes, columns, sectors, *refs),
         in_specs=[SCALARS] + [WHOLE] * 3,
@@ -464,14 +441,28 @@
         name="window",
     )(owner, interface, from_high, from_second)
 
-    def exchange(even, message, from_low, above, from_high, prefix, product, blocks):
+    def exchange(even, message, from_low, above, from_high, blocks, highest):
         ghost = lax.ppermute(message, AXES, import_pairs(even))
-        partial, started, up, down = pl.pallas_call(
+        below = lax.ppermute(highest, "slab", [(k, k + 1) for k in range(slabs - 1)])
+        prefix, right, left = pl.pallas_call(
+            lambda *refs: matrix_kernel(planes, *refs),
+            in_specs=[WHOLE, WHOLE],
+            out_shape=(square, square, square),
+            scratch_shapes=[
+                pltpu.VMEM((planes, V * V, 8, radial), F32),
+                pltpu.VMEM((planes, V * V, 8, radial), F32),
+                pltpu.VMEM((V * V, 8, radial), F32),
+                pltpu.VMEM((V * V, 8, radial), F32),
+            ],
+            compiler_params=params(),
+            cost_estimate=cost(60_000_000),
+            name="matrices",
+        )(axial, blocks)
+        partial, up, down = pl.pallas_call(
             lambda *refs: residual_kernel(planes, columns, *refs),
-            in_specs=[SCALARS] + [WHOLE] * 8,
+            in_specs=[WHOLE] * 9,
             out_shape=(
-                sds(V, planes, columns, radial), sds(V, planes, columns, radial),
-                sds(2 * V + V * V, columns, radial), sds(*plane),
+                sds(V, planes, columns, radial), sds(V + V * V, columns, radial), sds(*plane),
             ),
             scratch_shapes=[
                 pltpu.VMEM((V, planes, columns + 16, radial), F32),
@@ -480,44 +471,46 @@
             compiler_params=params(),
             cost_estimate=cost(40_000_000),
             name="residual",
-        )(flux, state, source, blocks, product, from_high, from_low, above, prefix)
-        return ghost, partial, started, up, down
-
-    ghost, partial, started, up, down = lax.switch(
+        )(axial, cross, state, source, blocks, from_high, from_low, above, prefix)
+        return ghost, below, partial, up, down, right, left
+
+    ghost, below, partial, up, down, right, left = lax.switch(
         pair[0],
         [lambda *args, e=e: exchange(2 * e, *args) for e in range(sectors // 2)],
-        message, from_low, above, from_high, prefix, product, blocks,
+        message, from_low, above, from_high, blocks, highest,
     )
     up_other = lax.ppermute(up, "slab", [(1, 2)])
-    side_other = lax.ppermute(side, "slab", [(1, 0), (3, 2)])
+    left_other = lax.ppermute(left, "slab", [(3, 2)])
     entry, side_message = pl.pallas_call(
         first_kernel,
-        out_shape=(sds(*plane), sds(2 * V, columns, radial)),
+        out_shape=(sds(*plane), sds(*plane)),
         compiler_params=params(),
         name="first",
     )(ghost, up, down, right)
     came_side = lax.ppermute(side_message, "slab", [(0, 1), (3, 2)])
     came = lax.ppermute(entry, "slab", [(0, 2)])
-    lower, onward, second, under, top = pl.pallas_call(
+    right, came, came_side = lax.optimization_barrier((right, came, came_side))
+    right_other = lax.ppermute(right, "slab", [(1, 0)])
+    lower, onward, second, top = pl.pallas_call(
         middle_kernel,
-        out_shape=(sds(*plane), sds(2 * V, columns, radial), sds(*plane), sds(*plane), sds(*plane)),
+        out_shape=(sds(*plane),) * 4,
         compiler_params=params(),
         name="middle",
-    )(came, came_side, up_other, side_other, up, down, right, left)
+    )(came, came_side, up_other, left_other, up, down, right, left)
     to_lower = lax.ppermute(lower, "slab", [(2, 1), (1, 0)])
     to_third = lax.ppermute(onward, "slab", [(2, 3)])
     to_zero = lax.ppermute(lower, "slab", [(2, 0)])
 
     residual, new_state = pl.pallas_call(
         lambda *refs: last_kernel(planes, *refs),
-        in_specs=[SCALARS] + [WHOLE] * 14,
+        in_specs=[WHOLE] * 13,
         out_shape=(sds(*state.shape), sds(*state.shape)),
         scratch_shapes=[pltpu.VMEM((V, planes, 8, radial), F32)] + [pltpu.VMEM(plane, F32)] * 3,
         compiler_params=params(),
         name="last",
     )(
-        flux, ghost, came_side, to_third, to_zero, to_lower, second, under, top,
-        side_other, partial, started, product, blocks, state,
+        axial, ghost, below, came_side, to_third, to_zero, to_lower, second, top,
+        right_other, partial, blocks, state,
     )
     return residual, new_state
 

time: 72 us -> 66.9 us (0.929)
  the two profiles are of different devices: /device:TPU:8 before, /device:TPU:0 now
where the time goes in v4:
time: 66.9 us; the launch traced here: 66.6 us
  starting transfers between devices  30.7 us (46%)
  Pallas kernels  17.1 us (26%)
  waiting for transfers between devices  17.1 us (26%)
  between operations  1.5 us (2%)
    ppermute x1, starting transfers between devices, per_device(): came = lax.ppermute(entry, 'slab', [(0, 2)])  8.14 us
    ppermute x1, starting transfers between devices, per_device(): lax.ppermute(towards_low, 'sector', [(j, (j - 1) % sectors) for j in rang...  6.65 us
    ppermute x1, starting transfers between devices, exchange(): lax.ppermute(highest, 'slab', [(k, k + 1) for k in range(slabs - 1)])  5.25 us
    ppermute x1, waiting for transfers between devices, per_device(): lax.ppermute(towards_high, 'sector', [(j, (j + 1) % sectors) for j in ran...  4.83 us
    ppermute x1, waiting for transfers between devices, per_device(): to_zero = lax.ppermute(lower, 'slab', [(2, 0)])  4.78 us
    ppermute x1, waiting for transfers between devices, per_device(): right_other = lax.ppermute(right, 'slab', [(1, 0)])  4.36 us
    pallas_call x1, Pallas kernels, per_device(): pl.pallas_call(lambda *refs: last_kernel(planes, *refs), in_specs=[WHOLE]...  3.52 us
    pallas_call x1, Pallas kernels, exchange(): pl.pallas_call(lambda *refs: matrix_kernel(planes, *refs), in_specs=[WHOL...  3.5 us
  transfers between devices with their start and end apart: 14, of which 6 were waited for; matrix products, arithmetic and copies ran while one was open for 0% of the time, Pallas kernels for 16%

profile of v4, /device:TPU:0, one launch (start us, length us, event | category | flops | bytes accessed | tf_op | source)
XLA Modules:
  0.0 66.6 jit_solution(1158019737614360996)
XLA Ops:
  0.6 0.0 copy-start.1
  0.6 0.0 copy-start
  0.7 0.0 copy-start.5
  0.7 0.0 copy-start.4
  0.7 0.0 copy-start.3
  0.7 3.1 %pack.1 = (f32[5,40,128]{2,1,0:T(8,128)S(1)}, f32[5,32,128]{2,1,0:T(8,128)S(1)}, f32[5,8,128]{2,1,0:T(8,128)S(1)}, f32[5,32,128]{2,1,0:T(8,128)S(1)}, f32[5,32,1...) custom-call(f32[1,5,8,32,128]{4,3,2,1,0:T(8,128)} %refs_12_.1, f32[1,5,5,8,32,128]{5,4,3,2,1,0:T(8,128)} %refs_1_.1), custom_call_target="tpu_custom_call" | custom-call | tf_op jit(solution)/shard_map/pack/pallas_call | solution.py:413
  3.8 6.6 %collective-permute-start.32 = (f32[5,40,128]{2,1,0:T(8,128)S(1)}, f32[5,40,128]{2,1,0:T(8,128)S(1)}, u32[]{:S(2)}, u32[]{:S(2)}) collective-permute-start(f32[5,40,128]{2,1,0:T(8,128)S(1)} %get-tuple-element.603), channel_id=1, source_target_pairs={{0,124},{4,0},{8,4},{12,8},{16,12},{20,16},{24,20},{28,24},{32,28}... | collective-permute-start | bytes 307208 | tf_op jit(solution)/shard_map/ppermute | solution.py:428
  10.5 0.7 collective-permute-start.33
  11.1 1.3 %collective-permute-start.35 = (f32[5,32,128]{2,1,0:T(8,128)S(1)}, f32[5,32,128]{2,1,0:T(8,128)S(1)}, u32[]{:S(2)}, u32[]{:S(2)}) collective-permute-start(f32[5,32,128]{2,1,0:T(8,128)S(1)} %get-tuple-element.609), channel_id=1, source_target_pairs={{1,0},{2,1},{3,2},{5,4},{6,5},{7,6},{9,8},{10,9},{11,10},{13,12},{... | collective-permute-start | bytes 245768 | tf_op jit(solution)/shard_map/ppermute | solution.py:425
  12.4 0.1 collective-permute-start.34
  12.5 0.0 collective-permute-done.33.refs_3_
  12.5 0.2 collective-permute-done.32.refs_2_
  12.7 0.0 copy-done
  12.7 1.4 %window.1 = (f32[5,32,128]{2,1,0:T(8,128)S(1)}, s32[1]{0:T(128)}) custom-call(s32[1024]{0:T(1024)S(1)} %copy-done, f32[5,32,128]{2,1,0:T(8,128)S(1)} %get-tuple-element.602.refs_1_, f32[5,40,128]{2,1,0:T(8,128)S(1)} %collective-permute-done.32.refs_2_, f32[5,32,128]{2,1,0:T(8,128)S(1)} %collective-permute-done.33.refs_3_), custom_call_target="tpu_custom_call" | custom-call | tf_op jit(solution)/shard_map/window/pallas_call | solution.py:431
  14.8 4.8 %collective-permute-done.34 = f32[5,8,128]{2,1,0:T(8,128)S(1)} collective-permute-done((f32[5,8,128]{2,1,0:T(8,128)S(1)}, f32[5,8,128]{2,1,0:T(8,128)S(1)}, u32[]{:S(2)}, u32[]{:S(2)}) %collective-permute-start.34) | collective-permute-done | bytes 20512 | tf_op jit(solution)/shard_map/ppermute | solution.py:426
  19.6 0.0 collective-permute-done.35
  19.6 0.0 copy-done.1
  19.6 0.0 copy-done.5
  19.6 0.0 copy-done.4
  19.7 0.0 copy-done.3
  19.7 13.2 %conditional.1 = (f32[5,32,128]{2,1,0:T(8,128)}, f32[5,32,128]{2,1,0:T(8,128)}, f32[5,8,32,128]{3,2,1,0:T(8,128)}, f32[30,32,128]{2,1,0:T(8,128)}, f32[5,32,128]...) conditional(s32[]{:T(128)} %bitcast.1, ...), branch_computations={%region_0.0_spmd, %region_1.0_spmd, %region_2.0_spmd, %region_3.0_... | conditional | flops 100000000 | bytes 13155496 | solution.py:477
  19.7 1.3 %collective-permute-start.18 = (f32[5,32,128]{2,1,0:T(8,128)S(1)}, f32[5,32,128]{2,1,0:T(8,128)}, u32[]{:S(2)}, u32[]{:S(2)}) collective-permute-start(f32[5,32,128]{2,1,0:T(8,128)S(1)} %get-tuple-element.464), channel_id=1, source_target_pairs={{128,59},{3,208},{132,63},{7,212},{136,67},{11,216},{140,71},{15,2... | collective-permute-start | bytes 245768 | tf_op jit(solution)/shard_map/cond/branch_9_fun/ppermute | solution.py:445
  21.0 5.3 %collective-permute-start.19 = (f32[5,32,128]{2,1,0:T(8,128)S(1)}, f32[5,32,128]{2,1,0:T(8,128)}, u32[]{:S(2)}, u32[]{:S(2)}) collective-permute-start(f32[5,32,128]{2,1,0:T(8,128)S(1)} %get-tuple-element.465), channel_id=1, source_target_pairs={{0,1},{1,2},{2,3},{4,5},{5,6},{6,7},{8,9},{9,10},{10,11},{12,13},{... | collective-permute-start | bytes 245768 | tf_op jit(solution)/shard_map/cond/branch_9_fun/ppermute | solution.py:446
  26.3 3.5 %matrices.25 = (f32[25,32,128]{2,1,0:T(8,128)S(1)}, f32[25,32,128]{2,1,0:T(8,128)}, f32[25,32,128]{2,1,0:T(8,128)}) custom-call(f32[5,1,5]{2,1,0:T(1,128)S(1)} %get-tuple-element.466.refs_0_, f32[1,5,5,8,32,128]{5,4,3,2,1,0:T(8,128)S(1)} %get-tuple-element.470.refs_1_.refs_4_), custom_call_target="tpu_custom_call" | custom-call | flops 60000000 | bytes 7500000 | tf_op jit(solution)/shard_map/cond/branch_9_fun/matrices/pallas_call | solution.py:447
  29.8 3.0 %residual.25 = (f32[5,8,32,128]{3,2,1,0:T(8,128)}, f32[30,32,128]{2,1,0:T(8,128)}, f32[5,32,128]{2,1,0:T(8,128)}) custom-call(f32[5,1,5]{2,1,0:T(1,128)S(1)} %get-tuple-element.466.refs_0_, f32[5,2,5]{2,1,0:T(2,128)S(1)} %get-tuple-element.467.refs_1_, f32[1,5,8,32,128]{4,3,2,1,0:T(8,128)S(1)} %get-tuple-element.468.refs_2_, ...), custom_call_target="tpu_custom_call" | custom-call | flops 40000000 | bytes 5000000 | tf_op jit(solution)/shard_map/cond/branch_9_fun/residual/pallas_call | solution.py:461
  32.7 0.0 collective-permute-done.18
  32.7 0.0 collective-permute-done.19
  32.9 0.0 copy-start.2
  32.9 0.8 %collective-permute-start.38 = (f32[30,32,128]{2,1,0:T(8,128)}, f32[30,32,128]{2,1,0:T(8,128)S(1)}, u32[]{:S(2)}, u32[]{:S(2)}) collective-permute-start(f32[30,32,128]{2,1,0:T(8,128)} %get-tuple-element.613.up), channel_id=1, source_target_pairs={{1,2},{5,6},{9,10},{13,14},{17,18},{21,22},{25,26},{29,30},{33,34}... | collective-permute-start | bytes 1474568 | tf_op jit(solution)/shard_map/ppermute | solution.py:482
  33.7 1.3 %first.1 = (f32[5,32,128]{2,1,0:T(8,128)S(1)}, f32[5,32,128]{2,1,0:T(8,128)S(1)}) custom-call(f32[5,32,128]{2,1,0:T(8,128)} %get-tuple-element.610.ghost.refs_1_, f32[30,32,128]{2,1,0:T(8,128)} %get-tuple-element.613.up, f32[5,32,128]{2,1,0:T(8,128)} %get-tuple-element.614.down, f32[25,32,128]{2,1,0:T(8,128)} %get-tuple-element.620.right), custom_call_target="tpu_custom_call" | custom-call | tf_op jit(solution)/shard_map/first/pallas_call | solution.py:484
  35.0 8.1 %collective-permute-start.36 = (f32[5,32,128]{2,1,0:T(8,128)S(1)}, f32[5,32,128]{2,1,0:T(8,128)S(1)}, u32[]{:S(2)}, u32[]{:S(2)}) collective-permute-start(f32[5,32,128]{2,1,0:T(8,128)S(1)} %get-tuple-element.615), channel_id=1, source_target_pairs={{0,2},{4,6},{8,10},{12,14},{16,18},{20,22},{24,26},{28,30},{32,34}... | collective-permute-start | bytes 245768 | tf_op jit(solution)/shard_map/ppermute | solution.py:491
  43.1 0.7 %collective-permute-start.39 = (f32[25,32,128]{2,1,0:T(8,128)}, f32[25,32,128]{2,1,0:T(8,128)S(1)}, u32[]{:S(2)}, u32[]{:S(2)}) collective-permute-start(f32[25,32,128]{2,1,0:T(8,128)} %get-tuple-element.619.left), channel_id=1, source_target_pairs={{3,2},{7,6},{11,10},{15,14},{19,18},{23,22},{27,26},{31,30},{35,34... | collective-permute-start | bytes 1228808 | tf_op jit(solution)/shard_map/ppermute | solution.py:483
  43.8 1.3 %collective-permute-start.37 = (f32[5,32,128]{2,1,0:T(8,128)S(1)}, f32[5,32,128]{2,1,0:T(8,128)S(1)}, u32[]{:S(2)}, u32[]{:S(2)}) collective-permute-start(f32[5,32,128]{2,1,0:T(8,128)S(1)} %get-tuple-element.616), channel_id=1, source_target_pairs={{0,1},{3,2},{4,5},{7,6},{8,9},{11,10},{12,13},{15,14},{16,17},{19,... | collective-permute-start | bytes 245768 | tf_op jit(solution)/shard_map/ppermute | solution.py:490
  45.1 0.0 collective-permute-done.36.came
  45.2 2.0 %collective-permute-done.37.came_side.refs_3_ = f32[5,32,128]{2,1,0:T(8,128)S(1)} collective-permute-done((f32[5,32,128]{2,1,0:T(8,128)S(1)}, f32[5,32,128]{2,1,0:T(8,128)S(1)}, u32[]{:S(2)}, u32[]{:S(2)}) %collective-permute-start.37) | collective-permute-done | bytes 81952 | tf_op jit(solution)/shard_map/ppermute | solution.py:490
  47.2 1.3 %collective-permute-start.43 = (f32[25,32,128]{2,1,0:T(8,128)}, f32[25,32,128]{2,1,0:T(8,128)S(1)}, u32[]{:S(2)}, u32[]{:S(2)}) collective-permute-start(f32[25,32,128]{2,1,0:T(8,128)} %get-tuple-element.620.right), channel_id=1, source_target_pairs={{1,0},{5,4},{9,8},{13,12},{17,16},{21,20},{25,24},{29,28},{33,32},... | collective-permute-start | bytes 1228808 | tf_op jit(solution)/shard_map/ppermute | solution.py:493
  48.4 0.0 collective-permute-done.39.left_other
  48.5 0.0 collective-permute-done.38.up_other
  48.5 1.3 %middle.1 = (f32[5,32,128]{2,1,0:T(8,128)S(1)}, f32[5,32,128]{2,1,0:T(8,128)S(1)}, f32[5,32,128]{2,1,0:T(8,128)S(1)}, f32[5,32,128]{2,1,0:T(8,128)S(1)}) custom-call(f32[5,32,128]{2,1,0:T(8,128)S(1)} %collective-permute-done.36.came, f32[5,32,128]{2,1,0:T(8,128)S(1)} %collective-permute-done.37.came_side.refs_3_, ...), custom_call_target="tpu_custom_call" | custom-call | tf_op jit(solution)/shard_map/middle/pallas_call | solution.py:494
  49.8 0.7 collective-permute-start.40
  50.5 1.3 %collective-permute-start.42 = (f32[5,32,128]{2,1,0:T(8,128)S(1)}, f32[5,32,128]{2,1,0:T(8,128)S(1)}, u32[]{:S(2)}, u32[]{:S(2)}) collective-permute-start(f32[5,32,128]{2,1,0:T(8,128)S(1)} %get-tuple-element.622), channel_id=1, source_target_pairs={{2,1},{1,0},{6,5},{5,4},{10,9},{9,8},{14,13},{13,12},{18,17},{17,1... | collective-permute-start | bytes 245768 | tf_op jit(solution)/shard_map/ppermute | solution.py:500
  51.8 1.3 %collective-permute-start.41 = (f32[5,32,128]{2,1,0:T(8,128)S(1)}, f32[5,32,128]{2,1,0:T(8,128)S(1)}, u32[]{:S(2)}, u32[]{:S(2)}) collective-permute-start(f32[5,32,128]{2,1,0:T(8,128)S(1)} %get-tuple-element.622), channel_id=1, source_target_pairs={{2,0},{6,4},{10,8},{14,12},{18,16},{22,20},{26,24},{30,28},{34,32}... | collective-permute-start | bytes 245768 | tf_op jit(solution)/shard_map/ppermute | solution.py:502
  53.1 4.4 %collective-permute-done.43.refs_9_ = f32[25,32,128]{2,1,0:T(8,128)S(1)} collective-permute-done((f32[25,32,128]{2,1,0:T(8,128)}, f32[25,32,128]{2,1,0:T(8,128)S(1)}, u32[]{:S(2)}, u32[]{:S(2)}) %collective-permute-start.43) | collective-permute-done | bytes 409632 | tf_op jit(solution)/shard_map/ppermute | solution.py:493
  57.4 0.0 collective-permute-done.40.refs_4_
  57.4 0.9 %collective-permute-done.42.refs_6_ = f32[5,32,128]{2,1,0:T(8,128)S(1)} collective-permute-done((f32[5,32,128]{2,1,0:T(8,128)S(1)}, f32[5,32,128]{2,1,0:T(8,128)S(1)}, u32[]{:S(2)}, u32[]{:S(2)}) %collective-permute-start.42) | collective-permute-done | bytes 81952 | tf_op jit(solution)/shard_map/ppermute | solution.py:500
  58.3 4.8 %collective-permute-done.41.refs_5_ = f32[5,32,128]{2,1,0:T(8,128)S(1)} collective-permute-done((f32[5,32,128]{2,1,0:T(8,128)S(1)}, f32[5,32,128]{2,1,0:T(8,128)S(1)}, u32[]{:S(2)}, u32[]{:S(2)}) %collective-permute-start.41) | collective-permute-done | bytes 81952 | tf_op jit(solution)/shard_map/ppermute | solution.py:502
  63.1 0.0 copy-done.2
  63.1 3.5 %last.1 = (f32[1,5,8,32,128]{4,3,2,1,0:T(8,128)}, f32[1,5,8,32,128]{4,3,2,1,0:T(8,128)}) custom-call(f32[5,1,5]{2,1,0:T(1,128)S(1)} %bitcast.21, f32[5,32,128]{2,1,0:T(8,128)} %get-tuple-element.610.ghost.refs_1_, f32[5,32,128]{2,1,0:T(8,128)} %get-tuple-element.611.refs_2_, f32[5,32,128]{2,1,0:T(8,128)S(1)} %collective-permute-done.37.came_side.refs_3_, ...), custom_call_target="tpu_custom_call" | custom-call | tf_op jit(solution)/shard_map/last/pallas_call | solution.py:504
Async XLA Ops:
  0.6 19.0 %copy-start.1 = (f32[1,5,8,32,128]{4,3,2,1,0:T(8,128)S(1)}, f32[1,5,8,32,128]{4,3,2,1,0:T(8,128)}, u32[]{:S(2)}) copy-start(f32[1,5,8,32,128]{4,3,2,1,0:T(8,128)} %refs_12_.1) | copy-start | bytes 1966084
  0.6 12.1 %copy-start = (s32[1024]{0:T(1024)S(1)}, s32[1024]{0:T(1024)}, u32[]{:S(2)}) copy-start(s32[1024]{0:T(1024)} %refs_0_.3) | copy-start | bytes 12292
  0.7 19.0 %copy-start.5 = (f32[1,2,5,5]{3,1,2,0:T(2,128)S(1)}, f32[1,2,5,5]{3,1,2,0:T(2,128)}, u32[]{:S(2)}) copy-start(f32[1,2,5,5]{3,1,2,0:T(2,128)} %param.26) | copy-start | bytes 604
  0.7 19.0 %copy-start.4 = (f32[1,5,5]{2,0,1:T(1,128)S(1)}, f32[1,5,5]{2,0,1:T(1,128)}, u32[]{:S(2)}) copy-start(f32[1,5,5]{2,0,1:T(1,128)} %param.25) | copy-start | bytes 304
  0.7 19.0 %copy-start.3 = (f32[1,5,8,32,128]{4,3,2,1,0:T(8,128)S(1)}, f32[1,5,8,32,128]{4,3,2,1,0:T(8,128)}, u32[]{:S(2)}) copy-start(f32[1,5,8,32,128]{4,3,2,1,0:T(8,128)} %param.23) | copy-start | bytes 1966084
  3.8 8.9 %collective-permute-start.32 = (f32[5,40,128]{2,1,0:T(8,128)S(1)}, f32[5,40,128]{2,1,0:T(8,128)S(1)}, u32[]{:S(2)}, u32[]{:S(2)}) collective-permute-start(f32[5,40,128]{2,1,0:T(8,128)S(1)} %get-tuple-element.603), channel_id=1, source_target_pairs={{0,124},{4,0},{8,4},{12,8},{16,12},{20,16},{24,20},{28,24},{32,28}... | collective-permute-start | bytes 307208 | tf_op jit(solution)/shard_map/ppermute | solution.py:428
  10.5 2.1 %collective-permute-start.33 = (f32[5,32,128]{2,1,0:T(8,128)S(1)}, f32[5,32,128]{2,1,0:T(8,128)S(1)}, u32[]{:S(2)}, u32[]{:S(2)}) collective-permute-start(f32[5,32,128]{2,1,0:T(8,128)S(1)} %get-tuple-element.602.refs_1_), channel_id=1, source_target_pairs={{3,123},{128,248},{7,127},{132,252},{11,3},{136,128},{15,7},{140,1... | collective-permute-start | bytes 245768 | tf_op jit(solution)/shard_map/ppermute | solution.py:427
  11.1 8.5 %collective-permute-start.35 = (f32[5,32,128]{2,1,0:T(8,128)S(1)}, f32[5,32,128]{2,1,0:T(8,128)S(1)}, u32[]{:S(2)}, u32[]{:S(2)}) collective-permute-start(f32[5,32,128]{2,1,0:T(8,128)S(1)} %get-tuple-element.609), channel_id=1, source_target_pairs={{1,0},{2,1},{3,2},{5,4},{6,5},{7,6},{9,8},{10,9},{11,10},{13,12},{... | collective-permute-start | bytes 245768 | tf_op jit(solution)/shard_map/ppermute | solution.py:425
  12.4 7.2 %collective-permute-start.34 = (f32[5,8,128]{2,1,0:T(8,128)S(1)}, f32[5,8,128]{2,1,0:T(8,128)S(1)}, u32[]{:S(2)}, u32[]{:S(2)}) collective-permute-start(f32[5,8,128]{2,1,0:T(8,128)S(1)} %get-tuple-element.608), channel_id=1, source_target_pairs={{0,4},{4,8},{8,12},{12,16},{16,20},{20,24},{24,28},{28,32},{32,36}... | collective-permute-start | bytes 61448 | tf_op jit(solution)/shard_map/ppermute | solution.py:426
  19.7 13.0 %collective-permute-start.18 = (f32[5,32,128]{2,1,0:T(8,128)S(1)}, f32[5,32,128]{2,1,0:T(8,128)}, u32[]{:S(2)}, u32[]{:S(2)}) collective-permute-start(f32[5,32,128]{2,1,0:T(8,128)S(1)} %get-tuple-element.464), channel_id=1, source_target_pairs={{128,59},{3,208},{132,63},{7,212},{136,67},{11,216},{140,71},{15,2... | collective-permute-start | bytes 245768 | tf_op jit(solution)/shard_map/cond/branch_9_fun/ppermute | solution.py:445
  21.0 11.7 %collective-permute-start.19 = (f32[5,32,128]{2,1,0:T(8,128)S(1)}, f32[5,32,128]{2,1,0:T(8,128)}, u32[]{:S(2)}, u32[]{:S(2)}) collective-permute-start(f32[5,32,128]{2,1,0:T(8,128)S(1)} %get-tuple-element.465), channel_id=1, source_target_pairs={{0,1},{1,2},{2,3},{4,5},{5,6},{6,7},{8,9},{9,10},{10,11},{12,13},{... | collective-permute-start | bytes 245768 | tf_op jit(solution)/shard_map/cond/branch_9_fun/ppermute | solution.py:446
  32.9 30.2 %copy-start.2 = (f32[1,5,8,32,128]{4,3,2,1,0:T(8,128)S(1)}, f32[1,5,8,32,128]{4,3,2,1,0:T(8,128)}, u32[]{:S(2)}) copy-start(f32[1,5,8,32,128]{4,3,2,1,0:T(8,128)} %refs_12_.1) | copy-start | bytes 1966084
  32.9 15.6 %collective-permute-start.38 = (f32[30,32,128]{2,1,0:T(8,128)}, f32[30,32,128]{2,1,0:T(8,128)S(1)}, u32[]{:S(2)}, u32[]{:S(2)}) collective-permute-start(f32[30,32,128]{2,1,0:T(8,128)} %get-tuple-element.613.up), channel_id=1, source_target_pairs={{1,2},{5,6},{9,10},{13,14},{17,18},{21,22},{25,26},{29,30},{33,34}... | collective-permute-start | bytes 1474568 | tf_op jit(solution)/shard_map/ppermute | solution.py:482
  35.0 10.2 %collective-permute-start.36 = (f32[5,32,128]{2,1,0:T(8,128)S(1)}, f32[5,32,128]{2,1,0:T(8,128)S(1)}, u32[]{:S(2)}, u32[]{:S(2)}) collective-permute-start(f32[5,32,128]{2,1,0:T(8,128)S(1)} %get-tuple-element.615), channel_id=1, source_target_pairs={{0,2},{4,6},{8,10},{12,14},{16,18},{20,22},{24,26},{28,30},{32,34}... | collective-permute-start | bytes 245768 | tf_op jit(solution)/shard_map/ppermute | solution.py:491
  43.1 5.3 %collective-permute-start.39 = (f32[25,32,128]{2,1,0:T(8,128)}, f32[25,32,128]{2,1,0:T(8,128)S(1)}, u32[]{:S(2)}, u32[]{:S(2)}) collective-permute-start(f32[25,32,128]{2,1,0:T(8,128)} %get-tuple-element.619.left), channel_id=1, source_target_pairs={{3,2},{7,6},{11,10},{15,14},{19,18},{23,22},{27,26},{31,30},{35,34... | collective-permute-start | bytes 1228808 | tf_op jit(solution)/shard_map/ppermute | solution.py:483
  43.8 3.3 %collective-permute-start.37 = (f32[5,32,128]{2,1,0:T(8,128)S(1)}, f32[5,32,128]{2,1,0:T(8,128)S(1)}, u32[]{:S(2)}, u32[]{:S(2)}) collective-permute-start(f32[5,32,128]{2,1,0:T(8,128)S(1)} %get-tuple-element.616), channel_id=1, source_target_pairs={{0,1},{3,2},{4,5},{7,6},{8,9},{11,10},{12,13},{15,14},{16,17},{19,... | collective-permute-start | bytes 245768 | tf_op jit(solution)/shard_map/ppermute | solution.py:490
  47.2 10.3 %collective-permute-start.43 = (f32[25,32,128]{2,1,0:T(8,128)}, f32[25,32,128]{2,1,0:T(8,128)S(1)}, u32[]{:S(2)}, u32[]{:S(2)}) collective-permute-start(f32[25,32,128]{2,1,0:T(8,128)} %get-tuple-element.620.right), channel_id=1, source_target_pairs={{1,0},{5,4},{9,8},{13,12},{17,16},{21,20},{25,24},{29,28},{33,32},... | collective-permute-start | bytes 1228808 | tf_op jit(solution)/shard_map/ppermute | solution.py:493
  49.8 7.6 %collective-permute-start.40 = (f32[5,32,128]{2,1,0:T(8,128)S(1)}, f32[5,32,128]{2,1,0:T(8,128)S(1)}, u32[]{:S(2)}, u32[]{:S(2)}) collective-permute-start(f32[5,32,128]{2,1,0:T(8,128)S(1)} %get-tuple-element.621), channel_id=1, source_target_pairs={{2,3},{6,7},{10,11},{14,15},{18,19},{22,23},{26,27},{30,31},{34,35... | collective-permute-start | bytes 245768 | tf_op jit(solution)/shard_map/ppermute | solution.py:501
  50.5 7.8 %collective-permute-start.42 = (f32[5,32,128]{2,1,0:T(8,128)S(1)}, f32[5,32,128]{2,1,0:T(8,128)S(1)}, u32[]{:S(2)}, u32[]{:S(2)}) collective-permute-start(f32[5,32,128]{2,1,0:T(8,128)S(1)} %get-tuple-element.622), channel_id=1, source_target_pairs={{2,1},{1,0},{6,5},{5,4},{10,9},{9,8},{14,13},{13,12},{18,17},{17,1... | collective-permute-start | bytes 245768 | tf_op jit(solution)/shard_map/ppermute | solution.py:500
  51.8 11.3 %collective-permute-start.41 = (f32[5,32,128]{2,1,0:T(8,128)S(1)}, f32[5,32,128]{2,1,0:T(8,128)S(1)}, u32[]{:S(2)}, u32[]{:S(2)}) collective-permute-start(f32[5,32,128]{2,1,0:T(8,128)S(1)} %get-tuple-element.622), channel_id=1, source_target_pairs={{2,0},{6,4},{10,8},{14,12},{18,16},{22,20},{26,24},{30,28},{34,32}... | collective-permute-start | bytes 245768 | tf_op jit(solution)/shard_map/ppermute | solution.py:502

commit v5 on v4

--- a/solution.py
+++ b/solution.py
@@ -44,10 +44,8 @@
 
 
 def pack_kernel(
-    planes, columns, state, inverse, towards_low, interface, towards_high, lowest, highest, blocks, arrived,
+    planes, columns, state, towards_low, interface, towards_high, lowest,
 ):
-    copy = pltpu.make_async_copy(inverse, blocks, arrived)
-    copy.start()
     row = lax.axis_index("row")
     face = jnp.where(row == 0, planes - 1, 0)
     for v in range(V):
@@ -55,10 +53,14 @@
         interface[v] = plane
         towards_low[v, planes:] = plane
         lowest[v] = state[0, v, 0]
-        highest[v] = state[0, v, planes - 1]
         for x in range(planes):
             towards_low[v, x : x + 1] = state[0, v, x, 0:1]
             towards_high[v, x : x + 1] = state[0, v, x, columns - 1 : columns]
+
+
+def load_kernel(inverse, lowest, blocks, arrived):
+    copy = pltpu.make_async_copy(inverse, blocks, arrived)
+    copy.start()
     copy.wait()
 
 
@@ -244,6 +246,8 @@
             up[v, at] = previous[v] + last
         for k in range(V * V):
             up[V + k, at] = prefix_in[k, at]
+        for v in range(V):
+            up[V + V * V + v, at] = wide[v, planes - 1, middle]
         for x in range(planes - 2, -1, -1):
             carried = matvec(lambda i, j: inverse[0, i, j, x, at], matvec(ja, previous))
             previous = [forward[v, x] - carried[v] for v in range(V)]
@@ -297,7 +301,7 @@
 
 
 def last_kernel(
-    planes, axial, ghost, below, came_side, to_third, to_zero, to_lower, second, top,
+    planes, axial, ghost, up_other, came_side, to_third, to_zero, to_lower, second, top,
     right_other, partial, inverse, state, residual, new_state, forward, inflow, beyond, under,
 ):
     row = lax.axis_index("row")
@@ -305,67 +309,65 @@
     ja = halved(axial)
     has_top = jnp.where((row == 0) & (slab == 3), 1.0, 0.0)
 
+    at = pl.ds(pl.multiple_of(pl.program_id(0) * 8, 8), 8)
+
+    def fetch(ref, base=0):
+        return [ref[base + v, at] for v in range(V)]
+
     @pl.when(slab == 0)
     def _():
-        inflow[...] = ghost[...]
-        under[...] = ghost[...]
+        put(inflow, 0, fetch(ghost))
+        put(under, 0, fetch(ghost))
+        moved = matvec(lambda i, j: right_other[V * i + j, at], fetch(to_zero))
+        put(beyond, 0, [to_lower[v, at] + moved[v] for v in range(V)])
 
     @pl.when(slab != 0)
     def _():
-        under[...] = below[...]
+        put(under, 0, fetch(up_other, V + V * V))
 
     @pl.when(slab == 1)
     def _():
-        inflow[...] = came_side[...]
-        beyond[...] = to_lower[...]
+        put(inflow, 0, fetch(came_side))
+        put(beyond, 0, fetch(to_lower))
 
     @pl.when(slab == 2)
     def _():
-        inflow[...] = second[...]
-        beyond[...] = top[...]
+        put(inflow, 0, fetch(second))
+        put(beyond, 0, fetch(top))
 
     @pl.when(slab == 3)
     def _():
-        inflow[...] = to_third[...]
-        beyond[...] = jnp.zeros_like(beyond)
-
-    def one_strip(step, carry):
-        at = pl.ds(pl.multiple_of(step * 8, 8), 8)
-
-        @pl.when(slab == 0)
-        def _():
-            came = [to_zero[v, at] for v in range(V)]
-            moved = matvec(lambda i, j: right_other[V * i + j, at], came)
-            for v in range(V):
-                beyond[v, at] = to_lower[v, at] + moved[v]
-
-        previous = [inflow[v, at] for v in range(V)]
-        for x in range(planes):
-            values = [partial[v, x, at] for v in range(V)]
-            if x == planes - 1:
-                top_part = matvec(ja, [ghost[v, at] * has_top for v in range(V)])
-                values = [values[v] - top_part[v] for v in range(V)]
-            if x == 0:
-                bottom = matvec(ja, [under[v, at] for v in range(V)])
-                for v in range(V):
-                    residual[0, v, x, at] = values[v] + bottom[v]
-            else:
-                for v in range(V):
-                    residual[0, v, x, at] = values[v]
-            carried = matvec(ja, previous)
-            values = [values[v] + carried[v] for v in range(V)]
-            previous = matvec(lambda i, j: inverse[0, i, j, x, at], values)
-            for v in range(V):
-                forward[v, x] = previous[v]
-        following = [beyond[v, at] for v in range(V)]
-        for x in range(planes - 1, -1, -1):
-            carried = matvec(lambda i, j: inverse[0, i, j, x, at], matvec(ja, following))
-            following = [forward[v, x] - carried[v] for v in range(V)]
-            for v in range(V):
-                new_state[0, v, x, at] = state[0, v, x, at] + following[v]
-        return carry
-
-    lax.fori_loop(0, state.shape[3] // 8, one_strip, 0)
+        put(inflow, 0, fetch(to_third))
+        put(beyond, 0, [jnp.zeros((8, 128), F32)] * V)
+
+    previous = planes_of(inflow, 0)
+    for x in range(planes):
+        values = [partial[v, x, at] for v in range(V)]
+        if x == planes - 1:
+            top_part = matvec(ja, [ghost[v, at] * has_top for v in range(V)])
+            values = [values[v] - top_part[v] for v in range(V)]
+        if x == 0:
+            bottom = matvec(ja, planes_of(under, 0))
+            for v in range(V):
+                residual[0, v, x] = values[v] + bottom[v]
+        else:
+            for v in range(V):
+                residual[0, v, x] = values[v]
+        carried = matvec(ja, previous)
+        values = [values[v] + carried[v] for v in range(V)]
+        previous = matvec(lambda i, j: inverse[0, i, j, x, at], values)
+        for v in range(V):
+            forward[v, x] = previous[v]
+    following = planes_of(beyond, 0)
+    for x in range(planes - 1, -1, -1):
+        carried = matvec(lambda i, j: inverse[0, i, j, x, at], matvec(ja, following))
+        following = [forward[v, x] - carried[v] for v in range(V)]
+        for v in range(V):
+            new_state[0, v, x] = state[0, v, x, at] + following[v]
+
+
+def near(*shape):
+    return pltpu.VMEM(shape, F32)
 
 
 def sds(*shape):
@@ -389,6 +391,7 @@
     sectors = lax.axis_size("sector")
     slabs = lax.axis_size("slab")
     plane = (V, columns, radial)
+    cells = pl.BlockSpec((1, V, planes, 8, radial), lambda i: (0, 0, 0, i, 0))
     size = slabs * sectors
 
     def device(row, sector, slab):
@@ -410,29 +413,33 @@
     assert total & (total - 1) == 0 and columns & (columns - 1) == 0
     axial = jnp.transpose(jac_axial, (1, 0, 2))
     cross = jnp.transpose(jac_cross[0], (1, 0, 2))
-    towards_low, interface, towards_high, lowest, highest, blocks = pl.pallas_call(
+    towards_low, interface, towards_high, lowest = pl.pallas_call(
         lambda *refs: pack_kernel(planes, columns, *refs),
-        in_specs=[WHOLE, pl.BlockSpec(memory_space=pltpu.HBM)],
-        out_specs=[WHOLE] * 6,
-        out_shape=(
-            sds(V, planes + columns, radial), sds(*plane), sds(V, planes, radial), sds(*plane),
-            sds(*plane), pltpu.VMEM(diag_inverse.shape, F32),
-        ),
-        scratch_shapes=[pltpu.SemaphoreType.DMA],
+        out_shape=(near(V, planes + columns, radial), near(*plane), near(V, planes, radial), near(*plane)),
         compiler_params=params(),
         name="pack",
-    )(state, pltpu.with_memory_space_constraint(diag_inverse, pltpu.HBM))
+    )(state)
     above = lax.ppermute(lowest, "slab", [(k, k - 1) for k in range(1, slabs)])
     from_low = lax.ppermute(towards_high, "sector", [(j, (j + 1) % sectors) for j in range(sectors)])
     from_second = lax.ppermute(interface, AXES, two_down)
     from_high = lax.ppermute(towards_low, "sector", [(j, (j - 1) % sectors) for j in range(sectors)])
 
-    square = sds(V * V, columns, radial)
+    square = near(V * V, columns, radial)
+    blocks = pl.pallas_call(
+        load_kernel,
+        in_specs=[pl.BlockSpec(memory_space=pltpu.HBM), pl.BlockSpec(memory_space=pl.ANY)],
+        out_specs=WHOLE,
+        out_shape=near(*diag_inverse.shape),
+        scratch_shapes=[pltpu.SemaphoreType.DMA],
+        compiler_params=params(),
+        cost_estimate=cost(20_000_000),
+        name="load",
+    )(pltpu.with_memory_space_constraint(diag_inverse, pltpu.HBM), lowest)
     message, pair = pl.pallas_call(
         lambda *refs: window_kernel(planes, columns, sectors, *refs),
         in_specs=[SCALARS] + [WHOLE] * 3,
         out_specs=[WHOLE, SCALARS],
-        out_shape=(sds(*plane), jax.ShapeDtypeStruct((1,), jnp.int32)),
+        out_shape=(near(*plane), jax.ShapeDtypeStruct((1,), jnp.int32)),
         scratch_shapes=[
             pltpu.VMEM((V, 3 * columns, radial), F32),
             pltpu.VMEM((V, columns + 8, radial), F32),
@@ -441,9 +448,8 @@
         name="window",
     )(owner, interface, from_high, from_second)
 
-    def exchange(even, message, from_low, above, from_high, blocks, highest):
+    def exchange(even, message, from_low, above, from_high, blocks):
         ghost = lax.ppermute(message, AXES, import_pairs(even))
-        below = lax.ppermute(highest, "slab", [(k, k + 1) for k in range(slabs - 1)])
         prefix, right, left = pl.pallas_call(
             lambda *refs: matrix_kernel(planes, *refs),
             in_specs=[WHOLE, WHOLE],
@@ -462,7 +468,7 @@
             lambda *refs: residual_kernel(planes, columns, *refs),
             in_specs=[WHOLE] * 9,
             out_shape=(
-                sds(V, planes, columns, radial), sds(V + V * V, columns, radial), sds(*plane),
+                near(V, planes, columns, radial), near(2 * V + V * V, columns, radial), near(*plane),
             ),
             scratch_shapes=[
                 pltpu.VMEM((V, planes, columns + 16, radial), F32),
@@ -472,18 +478,18 @@
             cost_estimate=cost(40_000_000),
             name="residual",
         )(axial, cross, state, source, blocks, from_high, from_low, above, prefix)
-        return ghost, below, partial, up, down, right, left
-
-    ghost, below, partial, up, down, right, left = lax.switch(
+        return ghost, partial, up, down, right, left
+
+    ghost, partial, up, down, right, left = lax.switch(
         pair[0],
         [lambda *args, e=e: exchange(2 * e, *args) for e in range(sectors // 2)],
-        message, from_low, above, from_high, blocks, highest,
+        message, from_low, above, from_high, blocks,
     )
-    up_other = lax.ppermute(up, "slab", [(1, 2)])
+    up_other = lax.ppermute(up, "slab", [(k, k + 1) for k in range(slabs - 1)])
     left_other = lax.ppermute(left, "slab", [(3, 2)])
     entry, side_message = pl.pallas_call(
         first_kernel,
-        out_shape=(sds(*plane), sds(*plane)),
+        out_shape=(near(*plane), near(*plane)),
         compiler_params=params(),
         name="first",
     )(ghost, up, down, right)
@@ -493,7 +499,7 @@
     right_other = lax.ppermute(right, "slab", [(1, 0)])
     lower, onward, second, top = pl.pallas_call(
         middle_kernel,
-        out_shape=(sds(*plane),) * 4,
+        out_shape=(near(*plane),) * 4,
         compiler_params=params(),
         name="middle",
     )(came, came_side, up_other, left_other, up, down, right, left)
@@ -503,13 +509,15 @@
 
     residual, new_state = pl.pallas_call(
         lambda *refs: last_kernel(planes, *refs),
+        grid=(columns // 8,),
         in_specs=[WHOLE] * 13,
+        out_specs=(cells, cells),
         out_shape=(sds(*state.shape), sds(*state.shape)),
-        scratch_shapes=[pltpu.VMEM((V, planes, 8, radial), F32)] + [pltpu.VMEM(plane, F32)] * 3,
+        scratch_shapes=[pltpu.VMEM((V, planes, 8, radial), F32)] + [pltpu.VMEM((V, 8, radial), F32)] * 3,
         compiler_params=params(),
         name="last",
     )(
-        axial, ghost, below, came_side, to_third, to_zero, to_lower, second, top,
+        axial, ghost, up_other, came_side, to_third, to_zero, to_lower, second, top,
         right_other, partial, blocks, state,
     )
     return residual, new_state

time: 66.9 us -> 69.6 us (1.040)
  the two profiles are of different devices: /device:TPU:0 before, /device:TPU:1 now
where the time goes in v5:
time: 69.6 us; the launch traced here: 68.9 us
  starting transfers between devices  29.4 us (42%)
  waiting for transfers between devices  22.6 us (32%)
  Pallas kernels  15.2 us (22%)
  between operations  1.47 us (2%)
    ppermute x1, waiting for transfers between devices, per_device(): came = lax.ppermute(entry, 'slab', [(0, 2)])  9.36 us
    ppermute x1, starting transfers between devices, per_device(): lax.ppermute(towards_low, 'sector', [(j, (j - 1) % sectors) for j in rang...  8.93 us
    ppermute x1, waiting for transfers between devices, per_device(): right_other = lax.ppermute(right, 'slab', [(1, 0)])  7.54 us
    ppermute x1, starting transfers between devices, exchange(): ghost = lax.ppermute(message, AXES, import_pairs(even))  6.94 us
    pallas_call x1, Pallas kernels, per_device(): pl.pallas_call(lambda *refs: last_kernel(planes, *refs), grid=(columns //...  3.51 us
    pallas_call x1, Pallas kernels, exchange(): pl.pallas_call(lambda *refs: matrix_kernel(planes, *refs), in_specs=[WHOL...  3.37 us
    ppermute x1, waiting for transfers between devices, exchange(): ghost = lax.ppermute(message, AXES, import_pairs(even))  2.63 us
    ppermute x1, starting transfers between devices, per_device(): from_second = lax.ppermute(interface, AXES, two_down)  2.25 us
  transfers between devices with their start and end apart: 13, of which 7 were waited for; matrix products, arithmetic and copies ran while one was open for 0% of the time, Pallas kernels for 15%

profile of v5, /device:TPU:1, one launch (start us, length us, event | category | flops | bytes accessed | tf_op | source)
XLA Modules:
  0.0 68.9 jit_solution(7606879772526909956)
XLA Ops:
  0.6 1.1 %pack.1 = (f32[5,40,128]{2,1,0:T(8,128)S(1)}, f32[5,32,128]{2,1,0:T(8,128)S(1)}, f32[5,8,128]{2,1,0:T(8,128)S(1)}, f32[5,32,128]{2,1,0:T(8,128)S(1)}) custom-call(f32[1,5,8,32,128]{4,3,2,1,0:T(8,128)} %refs_12_.1), custom_call_target="tpu_custom_call" | custom-call | tf_op jit(solution)/shard_map/pack/pallas_call | solution.py:416
  1.8 8.9 %collective-permute-start.16 = (f32[5,40,128]{2,1,0:T(8,128)S(1)}, f32[5,40,128]{2,1,0:T(8,128)S(1)}, u32[]{:S(2)}, u32[]{:S(2)}) collective-permute-start(f32[5,40,128]{2,1,0:T(8,128)S(1)} %get-tuple-element.552), channel_id=1, source_target_pairs={{0,124},{4,0},{8,4},{12,8},{16,12},{20,16},{24,20},{28,24},{32,28}... | collective-permute-start | bytes 307208 | tf_op jit(solution)/shard_map/ppermute | solution.py:425
  10.7 2.2 %collective-permute-start.17 = (f32[5,32,128]{2,1,0:T(8,128)S(1)}, f32[5,32,128]{2,1,0:T(8,128)S(1)}, u32[]{:S(2)}, u32[]{:S(2)}) collective-permute-start(f32[5,32,128]{2,1,0:T(8,128)S(1)} %get-tuple-element.551.refs_1_), channel_id=1, source_target_pairs={{3,123},{128,248},{7,127},{132,252},{11,3},{136,128},{15,7},{140,1... | collective-permute-start | bytes 245768 | tf_op jit(solution)/shard_map/ppermute | solution.py:424
  13.0 1.3 %collective-permute-start.19 = (f32[5,32,128]{2,1,0:T(8,128)S(1)}, f32[5,32,128]{2,1,0:T(8,128)S(1)}, u32[]{:S(2)}, u32[]{:S(2)}) collective-permute-start(f32[5,32,128]{2,1,0:T(8,128)S(1)} %get-tuple-element.555.lowest), channel_id=1, source_target_pairs={{1,0},{2,1},{3,2},{5,4},{6,5},{7,6},{9,8},{10,9},{11,10},{13,12},{... | collective-permute-start | bytes 245768 | tf_op jit(solution)/shard_map/ppermute | solution.py:422
  14.3 0.0 copy-start
  14.3 0.0 copy-start.1
  14.3 0.0 copy-start.3
  14.3 0.0 copy-start.4
  14.3 0.0 copy-start.5
  14.3 0.8 %collective-permute-start.18 = (f32[5,8,128]{2,1,0:T(8,128)S(1)}, f32[5,8,128]{2,1,0:T(8,128)S(1)}, u32[]{:S(2)}, u32[]{:S(2)}) collective-permute-start(f32[5,8,128]{2,1,0:T(8,128)S(1)} %get-tuple-element.556), channel_id=1, source_target_pairs={{0,4},{4,8},{8,12},{12,16},{16,20},{20,24},{24,28},{28,32},{32,36}... | collective-permute-start | bytes 61448 | tf_op jit(solution)/shard_map/ppermute | solution.py:423
  15.1 1.9 %load.1.refs_11_ = f32[1,5,5,8,32,128]{5,4,3,2,1,0:T(8,128)S(1)} custom-call(f32[1,5,5,8,32,128]{5,4,3,2,1,0:T(8,128)} %inverse.1, f32[5,32,128]{2,1,0:T(8,128)S(1)} %get-tuple-element.555.lowest), custom_call_target="tpu_custom_call" | custom-call | flops 20000000 | bytes 2500000 | tf_op jit(solution)/shard_map/load/pallas_call | solution.py:428
  17.0 0.4 collective-permute-done.17.refs_3_
  17.4 0.0 collective-permute-done.16.refs_2_
  17.4 0.0 copy-done
  17.4 1.3 %window.1 = (f32[5,32,128]{2,1,0:T(8,128)S(1)}, s32[1]{0:T(128)}) custom-call(s32[1024]{0:T(1024)S(1)} %copy-done, f32[5,32,128]{2,1,0:T(8,128)S(1)} %get-tuple-element.551.refs_1_, f32[5,40,128]{2,1,0:T(8,128)S(1)} %collective-permute-done.16.refs_2_, f32[5,32,128]{2,1,0:T(8,128)S(1)} %collective-permute-done.17.refs_3_), custom_call_target="tpu_custom_call" | custom-call | tf_op jit(solution)/shard_map/window/pallas_call | solution.py:438
  19.3 1.2 %collective-permute-done.18 = f32[5,8,128]{2,1,0:T(8,128)S(1)} collective-permute-done((f32[5,8,128]{2,1,0:T(8,128)S(1)}, f32[5,8,128]{2,1,0:T(8,128)S(1)}, u32[]{:S(2)}, u32[]{:S(2)}) %collective-permute-start.18) | collective-permute-done | bytes 20512 | tf_op jit(solution)/shard_map/ppermute | solution.py:423
  20.5 0.0 collective-permute-done.19
  20.5 0.0 copy-done.1
  20.5 0.0 copy-done.3
  20.5 0.0 copy-done.4
  20.5 0.0 copy-done.5
  20.5 15.1 %conditional.1 = (f32[5,32,128]{2,1,0:T(8,128)}, f32[5,8,32,128]{3,2,1,0:T(8,128)S(1)}, f32[35,32,128]{2,1,0:T(8,128)S(1)}, f32[5,32,128]{2,1,0:T(8,128)S(1)}, f...) conditional(s32[]{:T(128)} %bitcast.1, (f32[5,32,128]{2,1,0:T(8,128)S(1)}, ...), branch_computations={%region_0.0_spmd, %region_1.0_spmd, %region_2.0_spmd, %region_3.0_... | conditional | flops 100000000 | bytes 12827768 | solution.py:483
  20.6 6.9 %collective-permute-start.6 = (f32[5,32,128]{2,1,0:T(8,128)S(1)}, f32[5,32,128]{2,1,0:T(8,128)}, u32[]{:S(2)}, u32[]{:S(2)}) collective-permute-start(f32[5,32,128]{2,1,0:T(8,128)S(1)} %get-tuple-element.378), channel_id=1, source_target_pairs={{128,83},{3,184},{132,87},{7,188},{136,91},{11,192},{140,95},{15,1... | collective-permute-start | bytes 245768 | tf_op jit(solution)/shard_map/cond/branch_6_fun/ppermute | solution.py:452
  27.5 3.4 %matrices.22 = (f32[25,32,128]{2,1,0:T(8,128)S(1)}, f32[25,32,128]{2,1,0:T(8,128)S(1)}, f32[25,32,128]{2,1,0:T(8,128)}) custom-call(f32[5,1,5]{2,1,0:T(1,128)S(1)} %get-tuple-element.379.refs_0_, f32[1,5,5,8,32,128]{5,4,3,2,1,0:T(8,128)S(1)} %get-tuple-element.383.refs_1_.refs_4_), custom_call_target="tpu_custom_call" | custom-call | flops 60000000 | bytes 7500000 | tf_op jit(solution)/shard_map/cond/branch_6_fun/matrices/pallas_call | solution.py:453
  30.9 2.1 %residual.22 = (f32[5,8,32,128]{3,2,1,0:T(8,128)S(1)}, f32[35,32,128]{2,1,0:T(8,128)S(1)}, f32[5,32,128]{2,1,0:T(8,128)S(1)}) custom-call(f32[5,1,5]{2,1,0:T(1,128)S(1)} %get-tuple-element.379.refs_0_, f32[5,2,5]{2,1,0:T(2,128)S(1)} %get-tuple-element.380.refs_1_, f32[1,5,8,32,128]{4,3,2,1,0:T(8,128)S(1)} %get-tuple-element.381.refs_2_, ...), custom_call_target="tpu_custom_call" | custom-call | flops 40000000 | bytes 5000000 | tf_op jit(solution)/shard_map/cond/branch_6_fun/residual/pallas_call | solution.py:467
  33.0 2.6 %collective-permute-done.6 = f32[5,32,128]{2,1,0:T(8,128)} collective-permute-done((f32[5,32,128]{2,1,0:T(8,128)S(1)}, f32[5,32,128]{2,1,0:T(8,128)}, u32[]{:S(2)}, u32[]{:S(2)}) %collective-permute-start.6) | collective-permute-done | bytes 81952 | tf_op jit(solution)/shard_map/cond/branch_6_fun/ppermute | solution.py:452
  35.6 0.0 copy-start.2
  35.6 1.4 %collective-permute-start.20 = (f32[35,32,128]{2,1,0:T(8,128)S(1)}, f32[35,32,128]{2,1,0:T(8,128)S(1)}, u32[]{:S(2)}, u32[]{:S(2)}) collective-permute-start(f32[35,32,128]{2,1,0:T(8,128)S(1)} %get-tuple-element.558.up), channel_id=1, source_target_pairs={{0,1},{1,2},{2,3},{4,5},{5,6},{6,7},{8,9},{9,10},{10,11},{12,13},{... | collective-permute-start | bytes 1720328 | tf_op jit(solution)/shard_map/ppermute | solution.py:488
  37.0 0.9 %first.1 = (f32[5,32,128]{2,1,0:T(8,128)S(1)}, f32[5,32,128]{2,1,0:T(8,128)S(1)}) custom-call(f32[5,32,128]{2,1,0:T(8,128)} %get-tuple-element.557.ghost.refs_1_, f32[35,32,128]{2,1,0:T(8,128)S(1)} %get-tuple-element.558.up, f32[5,32,128]{2,1,0:T(8,128)S(1)} %get-tuple-element.560.down, f32[25,32,128]{2,1,0:T(8,128)S(1)} %get-tuple-element.566.right), custom_call_target="tpu_custom_call" | custom-call | tf_op jit(solution)/shard_map/first/pallas_call | solution.py:490
  38.0 1.3 %collective-permute-start.21 = (f32[5,32,128]{2,1,0:T(8,128)S(1)}, f32[5,32,128]{2,1,0:T(8,128)S(1)}, u32[]{:S(2)}, u32[]{:S(2)}) collective-permute-start(f32[5,32,128]{2,1,0:T(8,128)S(1)} %get-tuple-element.561), channel_id=1, source_target_pairs={{0,2},{4,6},{8,10},{12,14},{16,18},{20,22},{24,26},{28,30},{32,34}... | collective-permute-start | bytes 245768 | tf_op jit(solution)/shard_map/ppermute | solution.py:497
  39.3 0.7 collective-permute-start.23
  40.0 1.3 %collective-permute-start.22 = (f32[5,32,128]{2,1,0:T(8,128)S(1)}, f32[5,32,128]{2,1,0:T(8,128)S(1)}, u32[]{:S(2)}, u32[]{:S(2)}) collective-permute-start(f32[5,32,128]{2,1,0:T(8,128)S(1)} %get-tuple-element.562), channel_id=1, source_target_pairs={{0,1},{3,2},{4,5},{7,6},{8,9},{11,10},{12,13},{15,14},{16,17},{19,... | collective-permute-start | bytes 245768 | tf_op jit(solution)/shard_map/ppermute | solution.py:496
  41.3 9.4 %collective-permute-done.21.came = f32[5,32,128]{2,1,0:T(8,128)S(1)} collective-permute-done((f32[5,32,128]{2,1,0:T(8,128)S(1)}, f32[5,32,128]{2,1,0:T(8,128)S(1)}, u32[]{:S(2)}, u32[]{:S(2)}) %collective-permute-start.21) | collective-permute-done | bytes 81952 | tf_op jit(solution)/shard_map/ppermute | solution.py:497
  50.6 0.9 %collective-permute-done.22.came_side.refs_3_ = f32[5,32,128]{2,1,0:T(8,128)S(1)} collective-permute-done((f32[5,32,128]{2,1,0:T(8,128)S(1)}, f32[5,32,128]{2,1,0:T(8,128)S(1)}, u32[]{:S(2)}, u32[]{:S(2)}) %collective-permute-start.22) | collective-permute-done | bytes 81952 | tf_op jit(solution)/shard_map/ppermute | solution.py:496
  51.5 1.3 %collective-permute-start.27 = (f32[25,32,128]{2,1,0:T(8,128)S(1)}, f32[25,32,128]{2,1,0:T(8,128)S(1)}, u32[]{:S(2)}, u32[]{:S(2)}) collective-permute-start(f32[25,32,128]{2,1,0:T(8,128)S(1)} %get-tuple-element.566.right), channel_id=1, source_target_pairs={{1,0},{5,4},{9,8},{13,12},{17,16},{21,20},{25,24},{29,28},{33,32},... | collective-permute-start | bytes 1228808 | tf_op jit(solution)/shard_map/ppermute | solution.py:499
  52.8 0.0 collective-permute-done.23.left_other
  52.8 0.0 collective-permute-done.20.up_other.refs_2_
  52.8 1.0 %middle.1 = (f32[5,32,128]{2,1,0:T(8,128)S(1)}, f32[5,32,128]{2,1,0:T(8,128)S(1)}, f32[5,32,128]{2,1,0:T(8,128)S(1)}, f32[5,32,128]{2,1,0:T(8,128)S(1)}) custom-call(f32[5,32,128]{2,1,0:T(8,128)S(1)} %collective-permute-done.21.came, f32[5,32,128]{2,1,0:T(8,128)S(1)} %collective-permute-done.22.came_side.refs_3_, ...), custom_call_target="tpu_custom_call" | custom-call | tf_op jit(solution)/shard_map/middle/pallas_call | solution.py:500
  53.8 0.7 collective-permute-start.24
  54.5 1.3 %collective-permute-start.26 = (f32[5,32,128]{2,1,0:T(8,128)S(1)}, f32[5,32,128]{2,1,0:T(8,128)S(1)}, u32[]{:S(2)}, u32[]{:S(2)}) collective-permute-start(f32[5,32,128]{2,1,0:T(8,128)S(1)} %get-tuple-element.568), channel_id=1, source_target_pairs={{2,1},{1,0},{6,5},{5,4},{10,9},{9,8},{14,13},{13,12},{18,17},{17,1... | collective-permute-start | bytes 245768 | tf_op jit(solution)/shard_map/ppermute | solution.py:506
  55.8 1.3 %collective-permute-start.25 = (f32[5,32,128]{2,1,0:T(8,128)S(1)}, f32[5,32,128]{2,1,0:T(8,128)S(1)}, u32[]{:S(2)}, u32[]{:S(2)}) collective-permute-start(f32[5,32,128]{2,1,0:T(8,128)S(1)} %get-tuple-element.568), channel_id=1, source_target_pairs={{2,0},{6,4},{10,8},{14,12},{18,16},{22,20},{26,24},{30,28},{34,32}... | collective-permute-start | bytes 245768 | tf_op jit(solution)/shard_map/ppermute | solution.py:508
  57.1 7.5 %collective-permute-done.27.refs_9_ = f32[25,32,128]{2,1,0:T(8,128)S(1)} collective-permute-done((f32[25,32,128]{2,1,0:T(8,128)S(1)}, f32[25,32,128]{2,1,0:T(8,128)S(1)}, u32[]{:S(2)}, u32[]{:S(2)}) %collective-permute-start.27) | collective-permute-done | bytes 409632 | tf_op jit(solution)/shard_map/ppermute | solution.py:499
  64.6 0.0 collective-permute-done.24.refs_4_
  64.6 0.7 %collective-permute-done.26.refs_6_ = f32[5,32,128]{2,1,0:T(8,128)S(1)} collective-permute-done((f32[5,32,128]{2,1,0:T(8,128)S(1)}, f32[5,32,128]{2,1,0:T(8,128)S(1)}, u32[]{:S(2)}, u32[]{:S(2)}) %collective-permute-start.26) | collective-permute-done | bytes 81952 | tf_op jit(solution)/shard_map/ppermute | solution.py:506
  65.3 0.0 collective-permute-done.25.refs_5_
  65.3 0.0 copy-done.2
  65.3 3.5 %last.1 = (f32[1,5,8,32,128]{4,3,2,1,0:T(8,128)}, f32[1,5,8,32,128]{4,3,2,1,0:T(8,128)}) custom-call(f32[5,1,5]{2,1,0:T(1,128)S(1)} %bitcast.21, f32[5,32,128]{2,1,0:T(8,128)} %get-tuple-element.557.ghost.refs_1_, f32[35,32,128]{2,1,0:T(8,128)S(1)} %collective-permute-done.20.up_other.refs_2_, f32[5,32,128]{2,1,0:T(8,128)S(1)} %collective-permute-done.22.came_side.refs_3_, ...), custom_call_target="tpu_custom_call" | custom-call | tf_op jit(solution)/shard_map/last/pallas_call | solution.py:510
Async XLA Ops:
  1.8 15.6 %collective-permute-start.16 = (f32[5,40,128]{2,1,0:T(8,128)S(1)}, f32[5,40,128]{2,1,0:T(8,128)S(1)}, u32[]{:S(2)}, u32[]{:S(2)}) collective-permute-start(f32[5,40,128]{2,1,0:T(8,128)S(1)} %get-tuple-element.552), channel_id=1, source_target_pairs={{0,124},{4,0},{8,4},{12,8},{16,12},{20,16},{24,20},{28,24},{32,28}... | collective-permute-start | bytes 307208 | tf_op jit(solution)/shard_map/ppermute | solution.py:425
  10.7 6.7 %collective-permute-start.17 = (f32[5,32,128]{2,1,0:T(8,128)S(1)}, f32[5,32,128]{2,1,0:T(8,128)S(1)}, u32[]{:S(2)}, u32[]{:S(2)}) collective-permute-start(f32[5,32,128]{2,1,0:T(8,128)S(1)} %get-tuple-element.551.refs_1_), channel_id=1, source_target_pairs={{3,123},{128,248},{7,127},{132,252},{11,3},{136,128},{15,7},{140,1... | collective-permute-start | bytes 245768 | tf_op jit(solution)/shard_map/ppermute | solution.py:424
  13.0 7.5 %collective-permute-start.19 = (f32[5,32,128]{2,1,0:T(8,128)S(1)}, f32[5,32,128]{2,1,0:T(8,128)S(1)}, u32[]{:S(2)}, u32[]{:S(2)}) collective-permute-start(f32[5,32,128]{2,1,0:T(8,128)S(1)} %get-tuple-element.555.lowest), channel_id=1, source_target_pairs={{1,0},{2,1},{3,2},{5,4},{6,5},{7,6},{9,8},{10,9},{11,10},{13,12},{... | collective-permute-start | bytes 245768 | tf_op jit(solution)/shard_map/ppermute | solution.py:422
  14.3 3.1 %copy-start = (s32[1024]{0:T(1024)S(1)}, s32[1024]{0:T(1024)}, u32[]{:S(2)}) copy-start(s32[1024]{0:T(1024)} %refs_0_.3) | copy-start | bytes 12292
  14.3 6.2 %copy-start.1 = (f32[1,5,8,32,128]{4,3,2,1,0:T(8,128)S(1)}, f32[1,5,8,32,128]{4,3,2,1,0:T(8,128)}, u32[]{:S(2)}) copy-start(f32[1,5,8,32,128]{4,3,2,1,0:T(8,128)} %refs_12_.1) | copy-start | bytes 1966084
  14.3 6.2 %copy-start.3 = (f32[1,5,8,32,128]{4,3,2,1,0:T(8,128)S(1)}, f32[1,5,8,32,128]{4,3,2,1,0:T(8,128)}, u32[]{:S(2)}) copy-start(f32[1,5,8,32,128]{4,3,2,1,0:T(8,128)} %param.23) | copy-start | bytes 1966084
  14.3 6.2 %copy-start.4 = (f32[1,5,5]{2,0,1:T(1,128)S(1)}, f32[1,5,5]{2,0,1:T(1,128)}, u32[]{:S(2)}) copy-start(f32[1,5,5]{2,0,1:T(1,128)} %param.25) | copy-start | bytes 304
  14.3 6.2 %copy-start.5 = (f32[1,2,5,5]{3,1,2,0:T(2,128)S(1)}, f32[1,2,5,5]{3,1,2,0:T(2,128)}, u32[]{:S(2)}) copy-start(f32[1,2,5,5]{3,1,2,0:T(2,128)} %param.26) | copy-start | bytes 604
  14.3 6.2 %collective-permute-start.18 = (f32[5,8,128]{2,1,0:T(8,128)S(1)}, f32[5,8,128]{2,1,0:T(8,128)S(1)}, u32[]{:S(2)}, u32[]{:S(2)}) collective-permute-start(f32[5,8,128]{2,1,0:T(8,128)S(1)} %get-tuple-element.556), channel_id=1, source_target_pairs={{0,4},{4,8},{8,12},{12,16},{16,20},{20,24},{24,28},{28,32},{32,36}... | collective-permute-start | bytes 61448 | tf_op jit(solution)/shard_map/ppermute | solution.py:423
  20.6 15.0 %collective-permute-start.6 = (f32[5,32,128]{2,1,0:T(8,128)S(1)}, f32[5,32,128]{2,1,0:T(8,128)}, u32[]{:S(2)}, u32[]{:S(2)}) collective-permute-start(f32[5,32,128]{2,1,0:T(8,128)S(1)} %get-tuple-element.378), channel_id=1, source_target_pairs={{128,83},{3,184},{132,87},{7,188},{136,91},{11,192},{140,95},{15,1... | collective-permute-start | bytes 245768 | tf_op jit(solution)/shard_map/cond/branch_6_fun/ppermute | solution.py:452
  35.6 29.8 %copy-start.2 = (f32[1,5,8,32,128]{4,3,2,1,0:T(8,128)S(1)}, f32[1,5,8,32,128]{4,3,2,1,0:T(8,128)}, u32[]{:S(2)}) copy-start(f32[1,5,8,32,128]{4,3,2,1,0:T(8,128)} %refs_12_.1) | copy-start | bytes 1966084
  35.6 17.2 %collective-permute-start.20 = (f32[35,32,128]{2,1,0:T(8,128)S(1)}, f32[35,32,128]{2,1,0:T(8,128)S(1)}, u32[]{:S(2)}, u32[]{:S(2)}) collective-permute-start(f32[35,32,128]{2,1,0:T(8,128)S(1)} %get-tuple-element.558.up), channel_id=1, source_target_pairs={{0,1},{1,2},{2,3},{4,5},{5,6},{6,7},{8,9},{9,10},{10,11},{12,13},{... | collective-permute-start | bytes 1720328 | tf_op jit(solution)/shard_map/ppermute | solution.py:488
  38.0 12.7 %collective-permute-start.21 = (f32[5,32,128]{2,1,0:T(8,128)S(1)}, f32[5,32,128]{2,1,0:T(8,128)S(1)}, u32[]{:S(2)}, u32[]{:S(2)}) collective-permute-start(f32[5,32,128]{2,1,0:T(8,128)S(1)} %get-tuple-element.561), channel_id=1, source_target_pairs={{0,2},{4,6},{8,10},{12,14},{16,18},{20,22},{24,26},{28,30},{32,34}... | collective-permute-start | bytes 245768 | tf_op jit(solution)/shard_map/ppermute | solution.py:497
  39.3 13.5 %collective-permute-start.23 = (f32[25,32,128]{2,1,0:T(8,128)}, f32[25,32,128]{2,1,0:T(8,128)S(1)}, u32[]{:S(2)}, u32[]{:S(2)}) collective-permute-start(f32[25,32,128]{2,1,0:T(8,128)} %get-tuple-element.565.left), channel_id=1, source_target_pairs={{3,2},{7,6},{11,10},{15,14},{19,18},{23,22},{27,26},{31,30},{35,34... | collective-permute-start | bytes 1228808 | tf_op jit(solution)/shard_map/ppermute | solution.py:489
  40.0 11.5 %collective-permute-start.22 = (f32[5,32,128]{2,1,0:T(8,128)S(1)}, f32[5,32,128]{2,1,0:T(8,128)S(1)}, u32[]{:S(2)}, u32[]{:S(2)}) collective-permute-start(f32[5,32,128]{2,1,0:T(8,128)S(1)} %get-tuple-element.562), channel_id=1, source_target_pairs={{0,1},{3,2},{4,5},{7,6},{8,9},{11,10},{12,13},{15,14},{16,17},{19,... | collective-permute-start | bytes 245768 | tf_op jit(solution)/shard_map/ppermute | solution.py:496
  51.5 13.1 %collective-permute-start.27 = (f32[25,32,128]{2,1,0:T(8,128)S(1)}, f32[25,32,128]{2,1,0:T(8,128)S(1)}, u32[]{:S(2)}, u32[]{:S(2)}) collective-permute-start(f32[25,32,128]{2,1,0:T(8,128)S(1)} %get-tuple-element.566.right), channel_id=1, source_target_pairs={{1,0},{5,4},{9,8},{13,12},{17,16},{21,20},{25,24},{29,28},{33,32},... | collective-permute-start | bytes 1228808 | tf_op jit(solution)/shard_map/ppermute | solution.py:499
  53.8 10.8 %collective-permute-start.24 = (f32[5,32,128]{2,1,0:T(8,128)S(1)}, f32[5,32,128]{2,1,0:T(8,128)S(1)}, u32[]{:S(2)}, u32[]{:S(2)}) collective-permute-start(f32[5,32,128]{2,1,0:T(8,128)S(1)} %get-tuple-element.567), channel_id=1, source_target_pairs={{2,3},{6,7},{10,11},{14,15},{18,19},{22,23},{26,27},{30,31},{34,35... | collective-permute-start | bytes 245768 | tf_op jit(solution)/shard_map/ppermute | solution.py:507
  54.5 10.8 %collective-permute-start.26 = (f32[5,32,128]{2,1,0:T(8,128)S(1)}, f32[5,32,128]{2,1,0:T(8,128)S(1)}, u32[]{:S(2)}, u32[]{:S(2)}) collective-permute-start(f32[5,32,128]{2,1,0:T(8,128)S(1)} %get-tuple-element.568), channel_id=1, source_target_pairs={{2,1},{1,0},{6,5},{5,4},{10,9},{9,8},{14,13},{13,12},{18,17},{17,1... | collective-permute-start | bytes 245768 | tf_op jit(solution)/shard_map/ppermute | solution.py:506
  55.8 9.6 %collective-permute-start.25 = (f32[5,32,128]{2,1,0:T(8,128)S(1)}, f32[5,32,128]{2,1,0:T(8,128)S(1)}, u32[]{:S(2)}, u32[]{:S(2)}) collective-permute-start(f32[5,32,128]{2,1,0:T(8,128)S(1)} %get-tuple-element.568), channel_id=1, source_target_pairs={{2,0},{6,4},{10,8},{14,12},{18,16},{22,20},{26,24},{30,28},{34,32}... | collective-permute-start | bytes 245768 | tf_op jit(solution)/shard_map/ppermute | solution.py:508
